TPU v7x, 32 devices: a whole 2x2x4 slice. The times are simulated.
32 devices in a mesh: seq: 8 (over z, y), mlp: 4 (over x, core).
Axes of the slice: x: 2, y: 2, z: 4, core: 2. Of those that a mesh axis runs over, the one named last changes fastest.
Arguments:
- block_input: bfloat16 [8, 512, 2048], P('mlp', 'seq'), may hold values from -6 to 6
- w_branch: bfloat16 [2048, 2560], P(('seq', 'mlp')), may hold values from -0.125 to 0.125
- w_recur_in: bfloat16 [2048, 2560], P(('seq', 'mlp')), may hold values from -0.125 to 0.125
- w_recur_out: bfloat16 [2560, 2048], P(('seq', 'mlp')), may hold values from -0.25 to 0.25
- w_rgate: bfloat16 [2560, 256], P(('seq', 'mlp')), may hold values from -0.375 to 0.375
- w_igate: bfloat16 [2560, 256], P(('seq', 'mlp')), may hold values from -0.375 to 0.375
- conv_weight: bfloat16 [4, 2560], P(None, ('seq', 'mlp')), may hold values from -3 to 3
- conv_bias: bfloat16 [2560], P(('seq', 'mlp')), may hold values from -3 to 3
- rgate_bias: bfloat16 [2560], P(('seq', 'mlp')), may hold values from -3 to 3
- igate_bias: bfloat16 [2560], P(('seq', 'mlp')), may hold values from -3 to 3
- rate_param: bfloat16 [2560], P(('seq', 'mlp')), may hold values from -15 to -3
- norm_gain: bfloat16 [2048], P(('seq', 'mlp')), may hold values from 0.25 to 1.75
- mlp_gain: bfloat16 [2048], P(('seq', 'mlp')), may hold values from 0.25 to 1.75
- w_gate: bfloat16 [2048, 6144], P('seq', 'mlp'), may hold values from -0.125 to 0.125
- w_up: bfloat16 [2048, 6144], P('seq', 'mlp'), may hold values from -0.125 to 0.125
- w_down: bfloat16 [6144, 2048], P('mlp', 'seq'), may hold values from -0.15625 to 0.15625
- cotangent: bfloat16 [8, 512, 2048], P('mlp', 'seq'), may hold values from -6 to 6
Outputs:
- block_output: bfloat16 [8, 512, 2048], P('mlp', 'seq')
- input_grad: bfloat16 [8, 512, 2048], P('mlp', 'seq')
- grad_branch: float32 [2048, 2560], P(('seq', 'mlp'))
- grad_recur_in: float32 [2048, 2560], P(('seq', 'mlp'))
- grad_recur_out: float32 [2560, 2048], P(('seq', 'mlp'))
- grad_rgate: float32 [2560, 256], P(('seq', 'mlp'))
- grad_igate: float32 [2560, 256], P(('seq', 'mlp'))
- grad_conv_weight: float32 [4, 2560], P(None, ('seq', 'mlp'))
- grad_conv_bias: float32 [2560], P(('seq', 'mlp'))
- grad_rgate_bias: float32 [2560], P(('seq', 'mlp'))
- grad_igate_bias: float32 [2560], P(('seq', 'mlp'))
- grad_rate: float32 [2560], P(('seq', 'mlp'))
- grad_norm_gain: float32 [2048], P(('seq', 'mlp'))
- grad_mlp_gain: float32 [2048], P(('seq', 'mlp'))
- grad_gate: float32 [2048, 6144], P('seq', 'mlp')
- grad_up: float32 [2048, 6144], P('seq', 'mlp')
- grad_down: float32 [6144, 2048], P('mlp', 'seq')
All inputs are finite; a program needn't handle non-finite values.
Results may differ from a plain program's by a relative error of at most 0.013.
Values may be sent and summed in bfloat16 or wider, within the bound.
No kernel may reach another device: no remote copies, remote signals or barrier semaphores. Data moves between devices by JAX's collectives and lax.ppermute only.
A program may use at most 256 MiB of HBM per device.

v0:
```python
from functools import partial

import jax
import jax.numpy as jnp
from jax import lax
from jax.sharding import PartitionSpec as P

HEADS = 10
CONV = 4
MICRO = 2
SEQ_DEV = 1


def from_behind(value, axis, steps):
    count = lax.axis_size(axis)
    initial, last = (max(0, -steps), min(count, count - steps))
    return lax.ppermute(value, axis, [(source, source + steps) for source in range(initial, last)])


def prefix(shard, axis, combine, identity, reverse):
    devices, here = (lax.axis_size(axis), lax.axis_index(axis))
    everything = jax.tree.map(lambda part: lax.all_gather(part, axis), shard)
    start = jax.tree.map(
        lambda part, zero: jnp.broadcast_to(jnp.asarray(zero, part.dtype), part.shape),
        shard,
        identity,
    )

    def hop(k, before):
        at = devices - 1 - k if reverse else k
        reached = at > here if reverse else at < here
        new = combine(before, jax.tree.map(lambda part: part[at], everything))
        return jax.tree.map(lambda a, b: jnp.where(reached, a, b), new, before)

    return lax.fori_loop(0, devices, hop, start)


def combine_pairs(earlier, later):
    return (earlier[0] * later[0], later[0] * earlier[1] + later[1])


def rms_scale(values, gain):
    return values * lax.rsqrt(jnp.mean(values * values, axis=-1, keepdims=True) + 1e-06) * gain


def recur_terms(r_pre, i_pre, conv_out, rate):
    decay_log = -8.0 * jax.nn.softplus(rate) * jax.nn.sigmoid(r_pre)
    return (
        jnp.exp(decay_log),
        jax.nn.sigmoid(i_pre) * conv_out * jnp.sqrt(-jnp.expm1(2.0 * decay_log)),
    )


def mlp_act(gate_pre, up_pre):
    return jax.nn.gelu(gate_pre, approximate=True) * up_pre


def split_heads(values):
    return values.reshape(values.shape[0], values.shape[1], HEADS, values.shape[2] // HEADS)


def head_blocks(weight):
    return weight.reshape(HEADS, weight.shape[1], weight.shape[1])


def gate_mix(values, weight):
    mixed_heads = jnp.einsum(
        "sthj,hjk->sthk",
        split_heads(values),
        head_blocks(weight),
        preferred_element_type=jnp.float32,
    )
    return mixed_heads.reshape(values.shape)


def gate_back(grads, weight):
    mixed_heads = jnp.einsum(
        "sthk,hjk->sthj",
        split_heads(grads),
        head_blocks(weight),
        preferred_element_type=jnp.float32,
    )
    return mixed_heads.reshape(grads.shape)


def gate_weight_grad(values, grads):
    blocks = jnp.einsum(
        "sthj,sthk->hjk",
        split_heads(values),
        split_heads(grads),
        preferred_element_type=jnp.float32,
    )
    return blocks.reshape(values.shape[2], blocks.shape[2])


def times_rows(left, weight):
    return lax.dot_general(
        left, weight, (((2,), (1,)), ((), ())), preferred_element_type=jnp.float32
    )


def outer_sum(left, right):
    return jnp.einsum("sta,stb->ab", left, right, preferred_element_type=jnp.float32)


def micro_pass(block_input, cotangent, weights):
    (
        branch_full,
        recur_in_full,
        recur_out_full,
        rgate_full,
        igate_full,
        conv_full,
        cbias_full,
        rbias_full,
        ibias_full,
        rate_full,
        ngain_full,
        mgain_full,
        gate_full,
        up_full,
        down_full,
    ) = weights
    length = block_input.shape[1]
    rows_in = block_input.astype(jnp.float32)
    ngain = ngain_full.astype(jnp.float32)
    mgain = mgain_full.astype(jnp.float32)
    conv_taps = conv_full.astype(jnp.float32)
    rate = rate_full.astype(jnp.float32)
    normed_f, norm_pull = jax.vjp(rms_scale, rows_in, ngain)
    normed = normed_f.astype(jnp.bfloat16)
    branch_pre = jnp.dot(normed, branch_full, preferred_element_type=jnp.float32)
    branch_act, gelu_pull = jax.vjp(partial(jax.nn.gelu, approximate=True), branch_pre)
    recur_pre = jnp.dot(normed, recur_in_full, preferred_element_type=jnp.float32)
    edge_rows = from_behind(recur_pre[:, length - (CONV - 1) :], "seq", 1)
    extended = jnp.concatenate([edge_rows, recur_pre], axis=1)
    conv_out = cbias_full.astype(jnp.float32) + sum(
        (conv_taps[k] * extended[:, CONV - 1 - k : CONV - 1 - k + length] for k in range(CONV))
    )
    conv_low = conv_out.astype(jnp.bfloat16)
    r_pre = gate_mix(conv_low, rgate_full) + rbias_full.astype(jnp.float32)
    i_pre = gate_mix(conv_low, igate_full) + ibias_full.astype(jnp.float32)
    (decay_rate, driven), terms_pull = jax.vjp(recur_terms, r_pre, i_pre, conv_out, rate)
    cum_decay, local_state = lax.associative_scan(combine_pairs, (decay_rate, driven), axis=1)
    ones_state = jnp.ones_like(cum_decay[:, -1])
    zeros_state = jnp.zeros_like(cum_decay[:, -1])
    carry_in = prefix(
        (cum_decay[:, -1], local_state[:, -1]),
        "seq",
        combine_pairs,
        (ones_state, zeros_state),
        False,
    )[1]
    states = local_state + cum_decay * carry_in[:, None]
    mixed_low = (states * branch_act).astype(jnp.bfloat16)
    middle = rows_in + jnp.dot(mixed_low, recur_out_full, preferred_element_type=jnp.float32)
    normed2_f, norm2_pull = jax.vjp(rms_scale, middle, mgain)
    normed2 = normed2_f.astype(jnp.bfloat16)
    tokens_all = lax.all_gather(normed2, "mlp", axis=0, tiled=True)
    gate_pre = jnp.dot(tokens_all, gate_full, preferred_element_type=jnp.float32)
    up_pre = jnp.dot(tokens_all, up_full, preferred_element_type=jnp.float32)
    hidden_f, mlp_pull = jax.vjp(mlp_act, gate_pre, up_pre)
    hidden = hidden_f.astype(jnp.bfloat16)
    partial_out = jnp.dot(hidden, down_full, preferred_element_type=jnp.float32)
    mlp_out = lax.psum_scatter(
        partial_out.astype(jnp.bfloat16), "mlp", scatter_dimension=0, tiled=True
    ).astype(jnp.float32)
    block_output = (middle + mlp_out).astype(jnp.bfloat16)
    grad_all = lax.all_gather(cotangent, "mlp", axis=0, tiled=True)
    grad_hidden = times_rows(grad_all, down_full)
    grad_down = outer_sum(hidden, grad_all)
    grad_gate_pre, grad_up_pre = mlp_pull(grad_hidden)
    ggate_low = grad_gate_pre.astype(jnp.bfloat16)
    gup_low = grad_up_pre.astype(jnp.bfloat16)
    grad_tokens_part = times_rows(ggate_low, gate_full) + times_rows(gup_low, up_full)
    grad_normed2 = lax.psum_scatter(
        grad_tokens_part.astype(jnp.bfloat16), "mlp", scatter_dimension=0, tiled=True
    ).astype(jnp.float32)
    grad_gate = outer_sum(tokens_all, ggate_low)
    grad_up = outer_sum(tokens_all, gup_low)
    grad_middle_norm, grad_mgain = norm2_pull(grad_normed2)
    grad_middle = cotangent.astype(jnp.float32) + grad_middle_norm
    grad_out_low = grad_middle.astype(jnp.bfloat16)
    grad_mixed = times_rows(grad_out_low, recur_out_full)
    grad_recur_out_w = outer_sum(mixed_low, grad_out_low)
    grad_states = grad_mixed * branch_act
    grad_branch_low = gelu_pull(grad_mixed * states)[0].astype(jnp.bfloat16)
    ahead = jnp.concatenate([decay_rate[:, 1:], jnp.ones_like(decay_rate[:, :1])], axis=1)
    cum_ahead, local_grad = lax.associative_scan(
        combine_pairs, (ahead, grad_states), reverse=True, axis=1
    )
    grad_in_carry = prefix(
        (cum_decay[:, -1], decay_rate[:, 0] * local_grad[:, 0]),
        "seq",
        combine_pairs,
        (ones_state, zeros_state),
        True,
    )[1]
    delta = local_grad + cum_ahead * grad_in_carry[:, None]
    prev_states = jnp.concatenate([carry_in[:, None], states[:, :-1]], axis=1)
    grad_r, grad_i, grad_conv_direct, grad_rate = terms_pull((delta * prev_states, delta))
    grad_r_low = grad_r.astype(jnp.bfloat16)
    grad_i_low = grad_i.astype(jnp.bfloat16)
    grad_rgate_w = gate_weight_grad(conv_low, grad_r_low)
    grad_igate_w = gate_weight_grad(conv_low, grad_i_low)
    grad_rbias = jnp.sum(grad_r_low.astype(jnp.float32), axis=(0, 1))
    grad_ibias = jnp.sum(grad_i_low.astype(jnp.float32), axis=(0, 1))
    grad_conv = (
        grad_conv_direct + gate_back(grad_r_low, rgate_full) + gate_back(grad_i_low, igate_full)
    )
    grad_cbias = jnp.sum(grad_conv, axis=(0, 1))
    grad_taps = jnp.stack(
        [
            jnp.sum(grad_conv * extended[:, CONV - 1 - k : CONV - 1 - k + length], axis=(0, 1))
            for k in range(CONV)
        ]
    )
    next_rim = from_behind(grad_conv[:, : CONV - 1], "seq", -1)
    grad_ext = jnp.concatenate([grad_conv, next_rim], axis=1)
    grad_recur_low = sum((conv_taps[k] * grad_ext[:, k : k + length] for k in range(CONV))).astype(
        jnp.bfloat16
    )
    grad_branch_w = outer_sum(normed, grad_branch_low)
    grad_recur_in_w = outer_sum(normed, grad_recur_low)
    grad_normed = times_rows(grad_branch_low, branch_full) + times_rows(
        grad_recur_low, recur_in_full
    )
    grad_rows, grad_ngain = norm_pull(grad_normed)
    input_grad = (grad_middle + grad_rows).astype(jnp.bfloat16)
    recur_grads = (
        grad_branch_w,
        grad_recur_in_w,
        grad_recur_out_w,
        grad_rgate_w,
        grad_igate_w,
        grad_taps,
        grad_cbias,
        grad_rbias,
        grad_ibias,
        grad_rate,
        grad_ngain,
        grad_mgain,
    )
    mlp_grads = (grad_gate, grad_up, grad_down)
    return (block_output, input_grad, recur_grads, mlp_grads)


def on_device(
    block_input,
    w_branch,
    w_recur_in,
    w_recur_out,
    w_rgate,
    w_igate,
    conv_weight,
    conv_bias,
    rgate_bias,
    igate_bias,
    rate_param,
    norm_gain,
    mlp_gain,
    w_gate,
    w_up,
    w_down,
    cotangent,
):
    recur_full = (
        lax.all_gather(w_branch, ("seq", "mlp"), axis=0, tiled=True),
        lax.all_gather(w_recur_in, ("seq", "mlp"), axis=0, tiled=True),
        lax.all_gather(w_recur_out, ("seq", "mlp"), axis=0, tiled=True),
        lax.all_gather(w_rgate, ("seq", "mlp"), axis=0, tiled=True),
        lax.all_gather(w_igate, ("seq", "mlp"), axis=0, tiled=True),
        lax.all_gather(conv_weight, ("seq", "mlp"), axis=1, tiled=True),
        lax.all_gather(conv_bias, ("seq", "mlp"), axis=0, tiled=True),
        lax.all_gather(rgate_bias, ("seq", "mlp"), axis=0, tiled=True),
        lax.all_gather(igate_bias, ("seq", "mlp"), axis=0, tiled=True),
        lax.all_gather(rate_param, ("seq", "mlp"), axis=0, tiled=True),
        lax.all_gather(norm_gain, ("seq", "mlp"), axis=0, tiled=True),
        lax.all_gather(mlp_gain, ("seq", "mlp"), axis=0, tiled=True),
    )
    mlp_full = (
        lax.all_gather(w_gate, "seq", axis=0, tiled=True),
        lax.all_gather(w_up, "seq", axis=0, tiled=True),
        lax.all_gather(w_down, "seq", axis=1, tiled=True),
    )
    weights = tuple(recur_full) + tuple(mlp_full)
    out_blocks = []
    grad_blocks = []
    recur_total = None
    mlp_total = None
    for micro_index in range(MICRO):
        first_seq = micro_index * SEQ_DEV
        out_part, grad_part, recur_local, mlp_local = micro_pass(
            block_input[first_seq : first_seq + SEQ_DEV],
            cotangent[first_seq : first_seq + SEQ_DEV],
            weights,
        )
        out_blocks.append(out_part)
        grad_blocks.append(grad_part)
        if recur_total is None:
            recur_total = tuple(recur_local)
            mlp_total = tuple(mlp_local)
        else:
            recur_total = tuple(jax.tree.map(jnp.add, tuple(recur_total), tuple(recur_local)))
            mlp_total = tuple(jax.tree.map(jnp.add, tuple(mlp_total), tuple(mlp_local)))
    recur_total = (
        lax.psum_scatter(recur_total[0], ("seq", "mlp"), scatter_dimension=0, tiled=True),
        lax.psum_scatter(recur_total[1], ("seq", "mlp"), scatter_dimension=0, tiled=True),
        lax.psum_scatter(recur_total[2], ("seq", "mlp"), scatter_dimension=0, tiled=True),
        lax.psum_scatter(recur_total[3], ("seq", "mlp"), scatter_dimension=0, tiled=True),
        lax.psum_scatter(recur_total[4], ("seq", "mlp"), scatter_dimension=0, tiled=True),
        lax.psum_scatter(recur_total[5], ("seq", "mlp"), scatter_dimension=1, tiled=True),
        lax.psum_scatter(recur_total[6], ("seq", "mlp"), scatter_dimension=0, tiled=True),
        lax.psum_scatter(recur_total[7], ("seq", "mlp"), scatter_dimension=0, tiled=True),
        lax.psum_scatter(recur_total[8], ("seq", "mlp"), scatter_dimension=0, tiled=True),
        lax.psum_scatter(recur_total[9], ("seq", "mlp"), scatter_dimension=0, tiled=True),
        lax.psum_scatter(recur_total[10], ("seq", "mlp"), scatter_dimension=0, tiled=True),
        lax.psum_scatter(recur_total[11], ("seq", "mlp"), scatter_dimension=0, tiled=True),
    )
    mlp_total = (
        lax.psum_scatter(mlp_total[0], "seq", scatter_dimension=0, tiled=True),
        lax.psum_scatter(mlp_total[1], "seq", scatter_dimension=0, tiled=True),
        lax.psum_scatter(mlp_total[2], "seq", scatter_dimension=1, tiled=True),
    )
    block_output = jnp.concatenate(out_blocks, axis=0)
    input_grad = jnp.concatenate(grad_blocks, axis=0)
    return (
        block_output,
        input_grad,
        recur_total[0],
        recur_total[1],
        recur_total[2],
        recur_total[3],
        recur_total[4],
        recur_total[5],
        recur_total[6],
        recur_total[7],
        recur_total[8],
        recur_total[9],
        recur_total[10],
        recur_total[11],
        mlp_total[0],
        mlp_total[1],
        mlp_total[2],
    )


def solution(mesh):
    in_specs = (
        P("mlp", "seq", None),
        P(("seq", "mlp"), None),
        P(("seq", "mlp"), None),
        P(("seq", "mlp"), None),
        P(("seq", "mlp"), None),
        P(("seq", "mlp"), None),
        P(None, ("seq", "mlp")),
        P(("seq", "mlp")),
        P(("seq", "mlp")),
        P(("seq", "mlp")),
        P(("seq", "mlp")),
        P(("seq", "mlp")),
        P(("seq", "mlp")),
        P("seq", "mlp"),
        P("seq", "mlp"),
        P("mlp", "seq"),
        P("mlp", "seq", None),
    )
    out_specs = (
        P("mlp", "seq", None),
        P("mlp", "seq", None),
        P(("seq", "mlp"), None),
        P(("seq", "mlp"), None),
        P(("seq", "mlp"), None),
        P(("seq", "mlp"), None),
        P(("seq", "mlp"), None),
        P(None, ("seq", "mlp")),
        P(("seq", "mlp")),
        P(("seq", "mlp")),
        P(("seq", "mlp")),
        P(("seq", "mlp")),
        P(("seq", "mlp")),
        P(("seq", "mlp")),
        P("seq", "mlp"),
        P("seq", "mlp"),
        P("mlp", "seq"),
    )
    return jax.shard_map(
        on_device, mesh=mesh, in_specs=in_specs, out_specs=out_specs, check_vma=False
    )
```

profile of v0, /device:TPU:10, one launch (start us, length us, event | category | flops | bytes accessed | tf_op | source)
XLA Modules:
  0.0 3237.9 jit_solution(9853041949278427960)
XLA Ops:
  15.7 42.9 %all-reduce.113 = (bf16[2560]{0:T(1024)(128)(2,1)S(1)}, bf16[2048]{0:T(1024)(128)(2,1)S(1)}, bf16[2560]{0:T(1024)(128)(2,1)S(1)}, bf16[2560]{0:T(1024)(128)(2,1)...) all-reduce(bf16[2560]{0:T(1024)(128)(2,1)S(1)} %dynamic-update-slic, ...), channel_id=1, replica_groups=mesh['seq'=8,'mlp'=4] {'seq','mlp'}, use_global_device_ids=true, to_apply=%add.103 | all-reduce | flops 14336 | bytes 57344
  59.0 30.6 all-gather
  90.0 8.0 all-gather.14.cloned.1.call-done
  112.7 73.2 %all-gather.20.cloned.1.call-done = bf16[2048,2560]{1,0:T(8,128)(2,1)} async-done(((bf16[64,2560]{1,0:T(8,128)(2,1)}), bf16[2048,2560]{1,0:T(8,128)(2,1)}) %all-gather.20.cloned.1.call-update) | async-done | bytes 10485776 | tf_op jit(solution)/shard_map/all_gather | solution.py:268
  194.8 46.3 %all-gather.16.cloned.1.call-done = bf16[2560,256]{1,0:T(8,128)(2,1)} async-done(((bf16[80,256]{1,0:T(8,128)(2,1)}), bf16[2560,256]{1,0:T(8,128)(2,1)}) %all-gather.16.cloned.1.call-update) | async-done | bytes 1310736 | tf_op jit(solution)/shard_map/all_gather | solution.py:272
  243.6 53.4 %all-gather.18.cloned.1.call-done = bf16[2560,256]{1,0:T(8,128)(2,1)} async-done(((bf16[80,256]{1,0:T(8,128)(2,1)}), bf16[2560,256]{1,0:T(8,128)(2,1)}) %all-gather.18.cloned.1.call-update) | async-done | bytes 1310736 | tf_op jit(solution)/shard_map/all_gather | solution.py:271
  429.8 32.7 %all_gather.88 = f32[8,1,2560]{2,1,0:T(1,128)S(1)} all-gather(f32[1,1,2560]{2,1,0:T(1,128)S(1)} %slice_add_fusion.9), channel_id=1, replica_groups=mesh['seq'=8,'mlp'=4] {'seq'}, dimensions={0}, use_global_device_ids=true | all-gather | bytes 92160 | tf_op jit(solution)/shard_map/all_gather | solution.py:22
  463.4 29.6 all_gather.89
  511.9 91.9 %all-gather.28.cloned.1.call-done = bf16[2048,1536]{1,0:T(8,128)(2,1)} async-done(((bf16[256,1536]{1,0:T(8,128)(2,1)}), bf16[2048,1536]{1,0:T(8,128)(2,1)}) %all-gather.28.cloned.1.call-update) | async-done | bytes 6291472 | tf_op jit(solution)/shard_map/all_gather | solution.py:283
  603.9 17.3 all-gather.24.cloned.1.call-done
  627.2 94.5 %all-gather.26.cloned.1.call-done = bf16[2048,1536]{1,0:T(8,128)(2,1)} async-done(((bf16[256,1536]{1,0:T(8,128)(2,1)}), bf16[2048,1536]{1,0:T(8,128)(2,1)}) %all-gather.26.cloned.1.call-update) | async-done | bytes 6291472 | tf_op jit(solution)/shard_map/all_gather | solution.py:282
  721.7 7.9 fusion.50
  850.5 31.0 all_gather.97
  888.7 30.6 all_gather.98
  944.6 10.2 all-gather.32.cloned.1.call-done
  998.0 9.5 slice.972
  1007.5 9.5 slice.981
  1023.0 9.5 slice.1039
  1032.5 9.4 slice.1048
  1041.9 9.4 slice.1041
  1056.2 8.4 fusion.85
  1068.6 9.4 slice.978
  1161.1 9.4 slice.1018
  1190.9 8.6 fusion.93
  1203.5 9.4 slice.1045
  1296.4 9.4 slice.1085
  1326.3 9.8 rev.16
  1344.5 9.9 rev.17
  1354.4 29.9 all_gather.101
  1391.1 9.8 rev.18
  1409.5 9.9 rev.19
  1419.4 30.8 all_gather.103
  1530.3 8.8 fusion.166
  1539.1 13.5 convolution_add_fusion.2
  1553.8 8.7 fusion.175
  1562.5 13.7 convolution_add_fusion
  1592.7 8.8 fusion.163
  1601.5 13.5 convolution_add_fusion.1
  1624.8 7.4 fusion.168
  1638.9 41.5 %all-reduce.112 = (f32[2560]{0:T(1024)S(1)}, f32[2560]{0:T(1024)S(1)}, f32[2560]{0:T(1024)S(1)}, f32[2560]{0:T(1024)S(1)}, f32[2048]{0:T(1024)S(1)}, /*index=5*/f32[2048]{0:T(1024)S(1)}) all-reduce(f32[2560]{0:T(1024)S(1)} %add.1257, f32[2560]{0:T(1024)S(1)} %add.1258, ...), channel_id=12, replica_groups=mesh['seq'=8,'mlp'=4] {'seq','mlp'}, use_global_device_ids=true, to_apply=%region_36.38.clone | all-reduce | flops 14336 | bytes 114688
  1686.6 59.7 %reduce-scatter.30.cloned.1.call-done = f32[80,256]{1,0:T(8,128)} async-done(((f32[2560,256]{1,0:T(8,128)}), f32[80,256]{1,0:T(8,128)}) %reduce-scatter.30.cloned.1.call-update) | async-done | bytes 81936 | tf_op jit(solution)/shard_map/reduce_scatter | solution.py:310
  1746.3 138.6 %reduce-scatter.32.cloned.1.call-done = f32[80,256]{1,0:T(8,128)} async-done(((f32[2560,256]{1,0:T(8,128)}), f32[80,256]{1,0:T(8,128)}) %reduce-scatter.32.cloned.1.call-update) | async-done | bytes 81936 | tf_op jit(solution)/shard_map/reduce_scatter | solution.py:311
  1885.0 229.6 %reduce-scatter.34.cloned.1.call-done = f32[256,1536]{1,0:T(8,128)} async-done(((f32[2048,1536]{1,0:T(8,128)}), f32[256,1536]{1,0:T(8,128)}) %reduce-scatter.34.cloned.1.call-update) | async-done | bytes 1572880 | tf_op jit(solution)/shard_map/reduce_scatter | solution.py:321
  2114.6 210.7 %reduce-scatter.36.cloned.1.call-done = f32[256,1536]{1,0:T(8,128)} async-done(((f32[2048,1536]{1,0:T(8,128)}), f32[256,1536]{1,0:T(8,128)}) %reduce-scatter.36.cloned.1.call-update) | async-done | bytes 1572880 | tf_op jit(solution)/shard_map/reduce_scatter | solution.py:322
  2325.3 211.2 %reduce-scatter.38.cloned.1.call-done = f32[1536,256]{1,0:T(8,128)} async-done(((f32[1536,2048]{1,0:T(8,128)}), f32[1536,256]{1,0:T(8,128)}) %reduce-scatter.38.cloned.1.call-update) | async-done | bytes 1572880 | tf_op jit(solution)/shard_map/reduce_scatter | solution.py:323
  2536.5 229.7 %reduce-scatter.24.cloned.1.call-done = f32[64,2560]{1,0:T(8,128)} async-done(((f32[2048,2560]{1,0:T(8,128)}), f32[64,2560]{1,0:T(8,128)}) %reduce-scatter.24.cloned.1.call-update) | async-done | bytes 655376 | tf_op jit(solution)/shard_map/reduce_scatter | solution.py:307
  2766.1 232.5 %reduce-scatter.28.cloned.1.call-done = f32[80,2048]{1,0:T(8,128)} async-done(((f32[2560,2048]{1,0:T(8,128)}), f32[80,2048]{1,0:T(8,128)}) %reduce-scatter.28.cloned.1.call-update) | async-done | bytes 655376 | tf_op jit(solution)/shard_map/reduce_scatter | solution.py:309
  2998.6 232.6 %reduce-scatter.26.cloned.1.call-done = f32[64,2560]{1,0:T(8,128)} async-done(((f32[2048,2560]{1,0:T(8,128)}), f32[64,2560]{1,0:T(8,128)}) %reduce-scatter.26.cloned.1.call-update) | async-done | bytes 655376 | tf_op jit(solution)/shard_map/reduce_scatter | solution.py:308
  (902 shorter events, 776.8 us)
Async XLA Ops:
  7.3 51.7 %copy-start.126 = (bf16[4,80]{1,0:T(4,128)(2,1)S(1)}, bf16[4,80]{1,0:T(4,128)(2,1)}, u32[]{:S(2)}) copy-start(bf16[4,80]{1,0:T(4,128)(2,1)} %param.32) | copy-start | bytes 1924
  7.3 90.8 %all-gather.14.cloned.1.call-start = ((), (), s32[]{:S(2)}) async-start(), calls=%async_computation.13 | async-start | bytes 10813440 | tf_op jit(solution)/shard_map/all_gather | solution.py:269
  8.0 177.9 %all-gather.20.cloned.1.call-start = ((), (), s32[]{:S(2)}) async-start(), calls=%async_computation.16 | async-start | bytes 10813440 | tf_op jit(solution)/shard_map/all_gather | solution.py:268
  8.8 232.3 %all-gather.16.cloned.1.call-start = ((), (), s32[]{:S(2)}) async-start(), calls=%async_computation.14 | async-start | bytes 1351680 | tf_op jit(solution)/shard_map/all_gather | solution.py:272
  9.5 287.5 %all-gather.18.cloned.1.call-start = ((), (), s32[]{:S(2)}) async-start(), calls=%async_computation.15 | async-start | bytes 1351680 | tf_op jit(solution)/shard_map/all_gather | solution.py:271
  10.1 487.0 %all-gather.22.cloned.1.call-start = ((), (), s32[]{:S(2)}) async-start(), calls=%async_computation.17 | async-start | bytes 10813440 | tf_op jit(solution)/shard_map/all_gather | solution.py:270
  10.7 495.2 %all-gather.34.cloned.1.call-start = ((), (), s32[]{:S(2)}) async-start(), calls=%async_computation.25 | async-start | bytes 1310720 | tf_op jit(solution)/shard_map/all_gather | solution.py:169
  12.6 493.2 %all-gather.30.cloned.1.call-start = ((), (), s32[]{:S(2)}) async-start(), calls=%async_computation.21 | async-start | bytes 7077888 | tf_op jit(solution)/shard_map/all_gather | solution.py:284
  13.4 590.5 %all-gather.28.cloned.1.call-start = ((), (), s32[]{:S(2)}) async-start(), calls=%async_computation.20 | async-start | bytes 7077888 | tf_op jit(solution)/shard_map/all_gather | solution.py:283
  14.1 607.1 %all-gather.24.cloned.1.call-start = ((), (), s32[]{:S(2)}) async-start(), calls=%async_computation.18 | async-start | bytes 1310720 | tf_op jit(solution)/shard_map/all_gather | solution.py:159
  58.7 678.1 %copy-start.35 = (f32[2048]{0:T(1024)}, f32[2048]{0:T(1024)S(1)}, u32[]{:S(2)}) copy-start(f32[2048]{0:T(1024)S(1)} %convert_element_type.163) | copy-start | bytes 24580
  58.9 127.0 %copy-start.93 = (f32[64]{0:T(128)}, f32[64]{0:T(128)S(1)}, u32[]{:S(2)}) copy-start(f32[64]{0:T(128)S(1)} %fusion.229) | copy-start | bytes 772
  59.0 245.0 %copy-start.82 = (f32[2560]{0:T(1024)}, f32[2560]{0:T(1024)S(1)}, u32[]{:S(2)}) copy-start(f32[2560]{0:T(1024)S(1)} %fusion.228) | copy-start | bytes 30724
  89.9 102.9 %copy-start.89 = (f32[2560]{0:T(1024)}, f32[2560]{0:T(1024)S(1)}, u32[]{:S(2)}) copy-start(f32[2560]{0:T(1024)S(1)} %get-tuple-element.571) | copy-start | bytes 30724
  89.9 102.9 %copy-start.90 = (f32[2560]{0:T(1024)}, f32[2560]{0:T(1024)S(1)}, u32[]{:S(2)}) copy-start(f32[2560]{0:T(1024)S(1)} %get-tuple-element.572) | copy-start | bytes 30724
  89.9 102.9 %copy-start.91 = (f32[2560]{0:T(1024)}, f32[2560]{0:T(1024)S(1)}, u32[]{:S(2)}) copy-start(f32[2560]{0:T(1024)S(1)} %get-tuple-element.573) | copy-start | bytes 30724
  89.9 102.9 %copy-start.92 = (f32[2560]{0:T(1024)}, f32[2560]{0:T(1024)S(1)}, u32[]{:S(2)}) copy-start(f32[2560]{0:T(1024)S(1)} %get-tuple-element.574) | copy-start | bytes 30724
  89.9 646.9 %copy-start.95 = (f32[64]{0:T(128)}, f32[64]{0:T(128)S(1)}, u32[]{:S(2)}) copy-start(f32[64]{0:T(128)S(1)} %fusion.231) | copy-start | bytes 772
  90.0 214.0 %copy-start.78 = (f32[2560]{0:T(1024)}, f32[2560]{0:T(1024)S(1)}, u32[]{:S(2)}) copy-start(f32[2560]{0:T(1024)S(1)} %convert_element_type.166) | copy-start | bytes 30724
  90.0 214.0 %copy-start.84 = (f32[2560]{0:T(1024)}, f32[2560]{0:T(1024)S(1)}, u32[]{:S(2)}) copy-start(f32[2560]{0:T(1024)S(1)} %convert_element_type.168) | copy-start | bytes 30724
  90.0 413.3 %copy-start.80 = (f32[2048]{0:T(1024)}, f32[2048]{0:T(1024)S(1)}, u32[]{:S(2)}) copy-start(f32[2048]{0:T(1024)S(1)} %convert_element_type.170) | copy-start | bytes 24580
  104.1 88.6 %copy-start.6 = (f32[64,2560]{1,0:T(8,128)}, f32[64,2560]{1,0:T(8,128)S(1)}, u32[]{:S(2)}) copy-start(f32[64,2560]{1,0:T(8,128)S(1)} %fusion.251) | copy-start | bytes 1966084
  104.2 88.5 %collective-permute-start = (f32[1,3,2560]{2,1,0:T(4,128)S(1)}, f32[1,3,2560]{2,1,0:T(4,128)S(1)}, u32[]{:S(2)}, u32[]{:S(2)}) collective-permute-start(f32[1,3,2560]{2,1,0:T(4,128)S(1)} %slice.1104), channel_id=1, source_target_pairs={{0,4},{4,8},{8,12},{12,16},{16,20},{20,24},{24,28},{1,5},{5,9},{9,... | collective-permute-start | bytes 92168 | tf_op jit(solution)/shard_map/ppermute | solution.py:17
  109.0 83.8 %copy-start.4 = (f32[64,2560]{1,0:T(8,128)}, f32[64,2560]{1,0:T(8,128)S(1)}, u32[]{:S(2)}) copy-start(f32[64,2560]{1,0:T(8,128)S(1)} %fusion.245) | copy-start | bytes 1966084
  109.0 83.7 %collective-permute-start.1 = (f32[1,3,2560]{2,1,0:T(4,128)S(1)}, f32[1,3,2560]{2,1,0:T(4,128)S(1)}, u32[]{:S(2)}, u32[]{:S(2)}) collective-permute-start(f32[1,3,2560]{2,1,0:T(4,128)S(1)} %slice.1151), channel_id=1, source_target_pairs={{0,4},{4,8},{8,12},{12,16},{16,20},{20,24},{24,28},{1,5},{5,9},{9,... | collective-permute-start | bytes 92168 | tf_op jit(solution)/shard_map/ppermute | solution.py:17
  194.7 102.2 %copy-start.28 = (bf16[64,10,256]{2,1,0:T(8,128)(2,1)}, bf16[64,10,256]{2,1,0:T(8,128)(2,1)S(1)}, u32[]{:S(2)}) copy-start(bf16[64,10,256]{2,1,0:T(8,128)(2,1)S(1)} %reshape.1178) | copy-start | bytes 983044
  504.9 216.8 %all-gather.26.cloned.1.call-start = ((), (), s32[]{:S(2)}) async-start(), calls=%async_computation.19 | async-start | bytes 7077888 | tf_op jit(solution)/shard_map/all_gather | solution.py:282
  505.5 429.9 %reduce-scatter.20.cloned.1.call-start = ((), (), s32[]{:S(2)}) async-start(), calls=%async_computation.26 | async-start | bytes 1310720 | tf_op jit(solution)/shard_map/reduce_scatter | solution.py:176
  735.8 202.8 %all-gather.36.cloned.1.call-start = ((), (), s32[]{:S(2)}) async-start(), calls=%async_computation.27 | async-start | bytes 1310720 | tf_op jit(solution)/shard_map/all_gather | solution.py:169
  736.4 218.5 %all-gather.32.cloned.1.call-start = ((), (), s32[]{:S(2)}) async-start(), calls=%async_computation.23 | async-start | bytes 1310720 | tf_op jit(solution)/shard_map/all_gather | solution.py:159
  846.0 73.2 %copy-start.70 = (f32[1,2560]{1,0:T(1,128)S(1)}, f32[1,2560]{1,0:T(1,128)}, u32[]{:S(2)}) copy-start(f32[1,2560]{1,0:T(1,128)} %custom-call.1) | copy-start | bytes 30724
  938.3 113.1 %reduce-scatter.22.cloned.1.call-start = ((), (), s32[]{:S(2)}) async-start(), calls=%async_computation.28 | async-start | bytes 1310720 | tf_op jit(solution)/shard_map/reduce_scatter | solution.py:176
  971.5 81.8 %reduce-scatter.16.cloned.1.call-start = ((), (), s32[]{:S(2)}) async-start(), calls=%async_computation.22 | async-start | bytes 1310720 | tf_op jit(solution)/shard_map/reduce_scatter | solution.py:165
  977.4 76.0 %reduce-scatter.18.cloned.1.call-start = ((), (), s32[]{:S(2)}) async-start(), calls=%async_computation.24 | async-start | bytes 1310720 | tf_op jit(solution)/shard_map/reduce_scatter | solution.py:165
  983.6 701.5 %reduce-scatter.40.cloned.1.call-start = ((), (), s32[]{:S(2)}) async-start(), calls=%async_computation.37 | async-start | bytes 1351680
  994.5 56.8 %copy-start.128 = (f32[64]{0:T(128)S(1)}, f32[64]{0:T(128)}, u32[]{:S(2)}) copy-start(f32[64]{0:T(128)} %copy-done.127) | copy-start | bytes 772
  1344.5 60.9 %copy-start.59 = (f32[1,32,2560]{2,1,0:T(8,128)S(1)}, f32[1,32,2560]{2,1,0:T(8,128)}, u32[]{:S(2)}) copy-start(f32[1,32,2560]{2,1,0:T(8,128)} %add.1239) | copy-start | bytes 983044
  1405.4 51.5 %copy-start.79 = (f32[2560]{0:T(1024)S(1)}, f32[2560]{0:T(1024)}, u32[]{:S(2)}) copy-start(f32[2560]{0:T(1024)} %copy-done.78) | copy-start | bytes 30724
  1491.2 255.2 %reduce-scatter.30.cloned.1.call-start = ((), (), s32[]{:S(2)}) async-start(), calls=%async_computation.32 | async-start | bytes 2703360 | tf_op jit(solution)/shard_map/reduce_scatter | solution.py:310
  1494.5 390.5 %reduce-scatter.32.cloned.1.call-start = ((), (), s32[]{:S(2)}) async-start(), calls=%async_computation.33 | async-start | bytes 2703360 | tf_op jit(solution)/shard_map/reduce_scatter | solution.py:311
  1498.4 616.2 %reduce-scatter.34.cloned.1.call-start = ((), (), s32[]{:S(2)}) async-start(), calls=%async_computation.34 | async-start | bytes 14155776 | tf_op jit(solution)/shard_map/reduce_scatter | solution.py:321
  1509.1 816.2 %reduce-scatter.36.cloned.1.call-start = ((), (), s32[]{:S(2)}) async-start(), calls=%async_computation.35 | async-start | bytes 14155776 | tf_op jit(solution)/shard_map/reduce_scatter | solution.py:322
  1518.7 1017.8 %reduce-scatter.38.cloned.1.call-start = ((), (), s32[]{:S(2)}) async-start(), calls=%async_computation.36 | async-start | bytes 14155776 | tf_op jit(solution)/shard_map/reduce_scatter | solution.py:323
  1529.3 1236.8 %reduce-scatter.24.cloned.1.call-start = ((), (), s32[]{:S(2)}) async-start(), calls=%async_computation.29 | async-start | bytes 21626880 | tf_op jit(solution)/shard_map/reduce_scatter | solution.py:307
  1552.7 1445.9 %reduce-scatter.28.cloned.1.call-start = ((), (), s32[]{:S(2)}) async-start(), calls=%async_computation.31 | async-start | bytes 21626880 | tf_op jit(solution)/shard_map/reduce_scatter | solution.py:309
  1576.2 1655.0 %reduce-scatter.26.cloned.1.call-start = ((), (), s32[]{:S(2)}) async-start(), calls=%async_computation.30 | async-start | bytes 21626880 | tf_op jit(solution)/shard_map/reduce_scatter | solution.py:308
  1577.3 9.3 collective-permute-start.2
  1584.0 5.9 collective-permute-start.3
  (130 other events, 1291.6 us)
Sparse Core Ops, SparseCore 0:
  10.9 87.0 all-gather.13
  100.9 85.0 all-gather.19
  188.8 52.2 all-gather.15
  243.8 53.1 all-gather.17
  299.7 85.5 all-gather.21
  386.7 14.6 all-gather.33
  403.4 100.6 all-gather.29
  506.3 97.5 all-gather.27
  606.0 15.1 all-gather.23
  623.2 98.4 all-gather.25
  735.9 23.1 reduce-scatter.19
  760.5 16.7 all-gather.35
  938.4 16.3 all-gather.31
  971.6 24.8 reduce-scatter.21
  999.4 24.8 reduce-scatter.15
  1027.3 24.8 reduce-scatter.17
  1491.3 116.6 reduce-scatter.39
  1610.7 135.6 reduce-scatter.29
  1749.2 135.7 reduce-scatter.31
  1889.0 225.5 reduce-scatter.33
  2118.8 206.5 reduce-scatter.35
  2329.5 206.9 reduce-scatter.37
  2539.4 226.7 reduce-scatter.23
  2768.9 229.6 reduce-scatter.27
  3001.5 229.6 reduce-scatter.25
where the time goes:
time: 3270 us; the launch traced here: 3240 us
  waiting for transfers between devices  1950 us (60%)
  local copies, waits for them, and re-layouts  488 us (15%)
  blocking collectives  300 us (9%)
  matrix products  252 us (8%)
  other arithmetic  214 us (7%)
    reduce_scatter x1, waiting for transfers between devices, on_device(): lax.psum_scatter(recur_total[1], ('seq', 'mlp'), scatter_dimension=0, til...  233 us
    reduce_scatter x1, waiting for transfers between devices, on_device(): lax.psum_scatter(recur_total[2], ('seq', 'mlp'), scatter_dimension=0, til...  232 us
    reduce_scatter x1, waiting for transfers between devices, on_device(): lax.psum_scatter(recur_total[0], ('seq', 'mlp'), scatter_dimension=0, til...  230 us
    reduce_scatter x1, waiting for transfers between devices, on_device(): lax.psum_scatter(mlp_total[0], 'seq', scatter_dimension=0, tiled=True)  230 us
    reduce_scatter x1, waiting for transfers between devices, on_device(): lax.psum_scatter(mlp_total[2], 'seq', scatter_dimension=1, tiled=True)  211 us
    reduce_scatter x1, waiting for transfers between devices, on_device(): lax.psum_scatter(mlp_total[1], 'seq', scatter_dimension=0, tiled=True)  211 us
    slice x82, local copies, waits for them, and re-layouts, micro_pass(): lax.associative_scan(combine_pairs, (ahead, grad_states), reverse=True, a...  197 us
    all_gather x6, blocking collectives, prefix(): everything = jax.tree.map(lambda part: lax.all_gather(part, axis), shard)  184 us
  transfers between devices with their start and end apart: 29, of which 17 were waited for; matrix products, arithmetic and copies ran while one was open for 17% of the time, Pallas kernels for 0%

commit v1 on v0

v1 whole, which is shorter than its diff:
```python
from functools import partial

import jax
import jax.numpy as jnp
from jax import lax
from jax.experimental import pallas as pl
from jax.experimental.pallas import tpu as pltpu
from jax.sharding import Mesh, PartitionSpec as P

HEADS = 10
CONV = 4
RING = (0, 1, 3, 2)
F32 = jnp.float32
BF16 = jnp.bfloat16
PAIR = ((0, 1), (1, 0))


def swap(value, axis):
    return lax.ppermute(value, axis, PAIR)


def low(value):
    return value.astype(BF16)


def ordered(first, mine, theirs, axis):
    return jnp.where(
        first, jnp.concatenate([mine, theirs], axis), jnp.concatenate([theirs, mine], axis)
    )


def pick(array, index, axis):
    return lax.dynamic_index_in_dim(array, index, axis, keepdims=False)


def z_ring():
    return lax.axis_size("z") == len(RING)


def z_at(j):
    if not z_ring():
        return jnp.int32(j)
    here = pick(jnp.array(RING, jnp.int32), lax.axis_index("z"), 0)
    return pick(jnp.array(RING, jnp.int32), (here - j) % len(RING), 0)


def z_place(z):
    if not z_ring():
        return jnp.int32(z)
    table = jnp.array(RING, jnp.int32)
    return (pick(table, lax.axis_index("z"), 0) - RING[z]) % len(RING)


def z_next(value):
    count = len(RING)
    return lax.ppermute(value, "z", [(RING[p], RING[(p + 1) % count]) for p in range(count)])


def z_gather(shard):
    if not z_ring():
        everything = lax.all_gather(shard, "z")
        return [everything[j] for j in range(lax.axis_size("z"))]
    shards = [shard]
    for _ in range(len(RING) - 1):
        shards.append(z_next(shards[-1]))
    return shards


def z_scatter(part):
    count = lax.axis_size("z")
    if not z_ring():
        stacked = jnp.stack([low(part(j)) for j in range(count)])
        return lax.psum_scatter(stacked, "z", scatter_dimension=0).astype(F32)
    total = None
    for j in list(range(1, count)) + [0]:
        term = part(j)
        if total is not None:
            term = term + total.astype(F32)
        total = z_next(low(term)) if j else term
    return total


def z_shift(value, steps):
    count = lax.axis_size("z")
    return lax.ppermute(
        value, "z", [(s, s + steps) for s in range(count) if 0 <= s + steps < count]
    )


def z_carry(decay, state, step):
    count = lax.axis_size("z")
    pair = jnp.stack([decay, state])
    if z_ring():
        near = [z_shift(pair, step * k) for k in range(1, count)]
        carry = near[-1][1]
        for got in near[-2::-1]:
            carry = got[1] + got[0] * carry
        return carry
    everything, here = lax.all_gather(pair, "z"), lax.axis_index("z")

    def hop(k, before):
        at = k if step == 1 else count - 1 - k
        reached = at < here if step == 1 else at > here
        return jnp.where(reached, everything[at, 1] + everything[at, 0] * before, before)

    return lax.fori_loop(0, count, hop, jnp.zeros_like(state))


def group_gather(own):
    half = own.shape[0] // 2
    over_x, over_y = swap(own, "x"), swap(own, "y")
    corner = jnp.concatenate([swap(over_x[:half], "y"), swap(over_y[half:], "x")])
    near = jnp.concatenate([over_x, over_y, corner])
    return jnp.concatenate([own, near, swap(own, "c"), swap(near, "c")])


def group_scatter(partial_sum):
    rows = partial_sum.shape[0] // 8
    mine = partial_sum[: 4 * rows] + swap(low(partial_sum[4 * rows :]), "c").astype(F32)
    own, to_x, to_y, corner = (mine[k * rows : (k + 1) * rows] for k in range(4))
    half = rows // 2
    via_x = swap(low(corner[:half]), "x").astype(F32)
    via_y = swap(low(corner[half:]), "y").astype(F32)
    to_y = jnp.concatenate([to_y[:half] + via_x, to_y[half:]])
    to_x = jnp.concatenate([to_x[:half], to_x[half:] + via_y])
    return own + swap(low(to_x), "x").astype(F32) + swap(low(to_y), "y").astype(F32)


def fine_gather(shard, first, second):
    shards = z_gather(shard)
    near = [swap(s, first) for s in shards]
    far = [swap(s, second) for s in shards]
    both = [swap(s, second) for s in near]
    over_y, over_x = (near, far) if first == "y" else (far, near)
    return jnp.concatenate(shards + over_y + over_x + both)


def fine_scatter(full, first, second):
    count = lax.axis_size("z")
    blocks = full.reshape((2, 2, count, -1) + full.shape[1:])

    def part(j):
        def block(on_first, on_second):
            over_x, over_y = (on_second, on_first) if second == "x" else (on_first, on_second)
            return blocks[over_x, over_y, j]

        sent = swap(low(block(1, 1)), second).astype(F32)
        near = swap(low(block(1, 0) + sent), first).astype(F32)
        return block(0, 0) + swap(low(block(0, 1)), second).astype(F32) + near

    return z_scatter(part)


def fine_chips():
    y, x = lax.axis_index("y"), lax.axis_index("x")
    count = lax.axis_size("z")
    return [
        (z_at(j) * 2 + (y ^ over_y)) * 2 + (x ^ over_x)
        for over_x in (0, 1)
        for over_y in (0, 1)
        for j in range(count)
    ]


def fine_places():
    y, x = lax.axis_index("y"), lax.axis_index("x")
    count = lax.axis_size("z")
    return [
        ((x ^ at_x) * 2 + (y ^ at_y)) * count + z_place(z)
        for z in range(count)
        for at_y in (0, 1)
        for at_x in (0, 1)
    ]


def columns(values, places):
    width = values.shape[-1] // len(places)
    return jnp.concatenate(
        [lax.dynamic_slice_in_dim(values, at * width, width, values.ndim - 1) for at in places],
        axis=-1,
    )


def whole_gather(shard, first, second):
    shards = jnp.stack(z_gather(shard))
    count = lax.axis_size("z")
    if z_ring():
        shards = jnp.stack([pick(shards, z_place(z), 0) for z in range(count)])
    at = {"y": lax.axis_index("y"), "x": lax.axis_index("x")}
    near = swap(shards, first)
    held = jnp.stack([shards, near], 1)
    far = swap(held, second)
    both = jnp.where(at[first] == 0, held, held[:, ::-1])
    far = jnp.where(at[first] == 0, far, far[:, ::-1])
    full = jnp.where(at[second] == 0, jnp.stack([both, far], 2), jnp.stack([far, both], 2))
    if first == "x":
        full = jnp.swapaxes(full, 1, 2)
    return full.reshape((-1,) + shard.shape[1:])


def whole_scatter(full, first, second):
    count = lax.axis_size("z")
    blocks = full.reshape((count, 2, 2, -1) + full.shape[1:])
    places = {"y": 1, "x": 2}
    for axis in (second, first):
        at, dim = lax.axis_index(axis), places.pop(axis)
        dim = min(dim, blocks.ndim - full.ndim - 1)
        sent = swap(low(pick(blocks, 1 - at, dim)), axis)
        blocks = pick(blocks, at, dim) + sent.astype(F32)
    return z_scatter(lambda j: pick(blocks, z_at(j), 0))


def to_halves(count):
    return [(count // 2 * c + q, 2 * q + c) for q in range(count // 2) for c in range(2)]


EVERY = ("z", "y", "x", "c")


def expm1_neg(value):
    series = 1.0
    for k in range(10, 1, -1):
        series = 1.0 + value / k * series
    return jnp.where(value > -1.0, -value * series, 1.0 - jnp.exp(value))


def forward_kernel(
    rec_ref, halo_ref, vec_ref, wr_ref, wi_ref, conv_ref, sr_ref, si_ref, a_ref, s_ref, p_ref, ext
):
    head, heads = pl.program_id(0), pl.num_programs(0)
    seqs, length, width = rec_ref.shape
    lanes = pl.ds(pl.multiple_of(head * width, width), width)
    vec = vec_ref[...]
    for s in range(seqs):
        ext[s, 0:8, :] = halo_ref[s]
        ext[s, 8 : 8 + length, :] = rec_ref[s]
        conv = vec[4:5] + sum(
            vec[k : k + 1] * ext[s, 8 - k : 8 - k + length, :] for k in range(CONV)
        )
        conv_low = low(conv)
        sig_r = jax.nn.sigmoid(
            jnp.dot(conv_low, wr_ref[...], preferred_element_type=F32) + vec[5:6]
        )
        sig_i = jax.nn.sigmoid(
            jnp.dot(conv_low, wi_ref[...], preferred_element_type=F32) + vec[6:7]
        )
        decay_log = vec[7:8] * sig_r
        conv_ref[s] = conv
        sr_ref[s] = sig_r
        si_ref[s] = sig_i
        a_ref[s, :, lanes] = jnp.exp(decay_log)
        s_ref[s, :, lanes] = sig_i * conv * jnp.sqrt(expm1_neg(2.0 * decay_log))

    @pl.when(head == heads - 1)
    def _():
        def step(t, carry):
            new = []
            for s in range(seqs):
                prod, state = carry[s]
                row = pl.ds(t, 1)
                decay = a_ref[s, row, :]
                prod = decay * prod
                state = decay * state + s_ref[s, row, :]
                p_ref[s, row, :] = prod
                s_ref[s, row, :] = state
                new.append((prod, state))
            return tuple(new)

        full = a_ref.shape[2]
        start = (jnp.ones((1, full), F32), jnp.zeros((1, full), F32))
        lax.fori_loop(0, length, step, (start,) * seqs)


def reverse_kernel(a_ref, g_ref, l_ref, q_ref, e_ref):
    seqs, length, full = a_ref.shape

    def step(k, carry):
        t = length - 1 - k
        new = []
        for s in range(seqs):
            prod, sent = carry[s]
            row = pl.ds(t, 1)
            q_ref[s, row, :] = prod
            delta = g_ref[s, row, :] + sent
            l_ref[s, row, :] = delta
            decay = a_ref[s, row, :]
            new.append((prod * decay, decay * delta))
        return tuple(new)

    start = (jnp.ones((1, full), F32), jnp.zeros((1, full), F32))
    last = lax.fori_loop(0, length, step, (start,) * seqs)
    for s in range(seqs):
        e_ref[pl.ds(s, 1), :] = last[s][1]


def backward_kernel(
    l_ref, q_ref, e_ref, s_ref, p_ref, carry_ref, conv_ref, sr_ref, si_ref, rec_ref, halo_ref,
    vec_ref, wr_ref, wi_ref, gconv_ref, gwr_ref, gwi_ref, small_ref, ext, before,
):
    seqs, length, width = rec_ref.shape
    vec = vec_ref[...]
    rows = [jnp.zeros((1, width), F32)] * 8
    contract_rows = (((0,), (0,)), ((), ()))
    contract_last = (((1,), (1,)), ((), ()))
    for s in range(seqs):
        ext[s, 0:8, :] = halo_ref[s]
        ext[s, 8 : 8 + length, :] = rec_ref[s]
        carry = carry_ref[s : s + 1, :]
        before[s, 0:8, :] = jnp.broadcast_to(carry, (8, width))
        before[s, 8 : 8 + length, :] = s_ref[s] + p_ref[s] * carry
        prev = before[s, 7 : 7 + length, :]
        delta = l_ref[s] + q_ref[s] * e_ref[s : s + 1, :]
        conv, sig_r, sig_i = conv_ref[s], sr_ref[s], si_ref[s]
        decay_log = vec[7:8] * sig_r
        decay = jnp.exp(decay_log)
        scale = jnp.sqrt(expm1_neg(2.0 * decay_log))
        through = delta * sig_i
        grad_log = delta * prev * decay - through * conv * decay * decay / scale
        slope_r = grad_log * sig_r
        rows[7] = rows[7] + jnp.sum(slope_r, axis=0, keepdims=True)
        grad_r = low(slope_r * vec[7:8] * (1.0 - sig_r))
        grad_i = low(through * conv * scale * (1.0 - sig_i))
        conv_low = low(conv)
        gwr = lax.dot_general(conv_low, grad_r, contract_rows, preferred_element_type=F32)
        gwi = lax.dot_general(conv_low, grad_i, contract_rows, preferred_element_type=F32)
        if s == 0:
            gwr_ref[...], gwi_ref[...] = gwr, gwi
        else:
            gwr_ref[...] += gwr
            gwi_ref[...] += gwi
        rows[5] = rows[5] + jnp.sum(grad_r.astype(F32), axis=0, keepdims=True)
        rows[6] = rows[6] + jnp.sum(grad_i.astype(F32), axis=0, keepdims=True)
        grad_conv = (
            through * scale
            + lax.dot_general(grad_r, wr_ref[...], contract_last, preferred_element_type=F32)
            + lax.dot_general(grad_i, wi_ref[...], contract_last, preferred_element_type=F32)
        )
        gconv_ref[s] = grad_conv
        rows[4] = rows[4] + jnp.sum(grad_conv, axis=0, keepdims=True)
        for k in range(CONV):
            tap = grad_conv * ext[s, 8 - k : 8 - k + length, :]
            rows[k] = rows[k] + jnp.sum(tap, axis=0, keepdims=True)
    for k in range(8):
        small_ref[k : k + 1, :] = rows[k]


def cost(flops, values):
    return pl.CostEstimate(flops=flops, bytes_accessed=values, transcendentals=0)


def run_forward(rec, halo, vec, gates):
    seqs, length, full = rec.shape
    heads = HEADS // 2
    width = full // heads
    block = pl.BlockSpec((seqs, length, width), lambda h: (0, 0, h))
    whole = pl.BlockSpec((seqs, length, full), lambda h: (0, 0, 0))
    array = jax.ShapeDtypeStruct(rec.shape, F32)
    return pl.pallas_call(
        forward_kernel,
        grid=(heads,),
        in_specs=[
            block,
            pl.BlockSpec((seqs, 8, width), lambda h: (0, 0, h)),
            pl.BlockSpec((8, width), lambda h: (0, h)),
            pl.BlockSpec((width, width), lambda h: (h, 0)),
            pl.BlockSpec((width, width), lambda h: (h, 1)),
        ],
        out_specs=[block, block, block, whole, whole, whole],
        out_shape=[array] * 6,
        scratch_shapes=[pltpu.VMEM((seqs, length + 8, width), F32)],
        cost_estimate=cost(seqs * length * full * width * 4, rec.size * 28),
        name="recur_forward",
    )(rec, halo, vec, gates, gates)


def run_reverse(decay, grad_states):
    seqs, length, full = decay.shape
    array = jax.ShapeDtypeStruct(decay.shape, F32)
    return pl.pallas_call(
        reverse_kernel,
        out_shape=[array, array, jax.ShapeDtypeStruct((seqs, full), F32)],
        cost_estimate=cost(decay.size * 4, decay.size * 16),
        name="recur_reverse",
    )(decay, grad_states)


def run_backward(local, ahead, entering, state, prod, carry, conv, sig_r, sig_i, rec, halo, vec, gates):
    seqs, length, full = rec.shape
    heads = HEADS // 2
    width = full // heads
    block = pl.BlockSpec((seqs, length, width), lambda h: (0, 0, h))
    row = pl.BlockSpec((seqs, width), lambda h: (0, h))
    weight = pl.BlockSpec((width, width), lambda h: (h, 0))
    return pl.pallas_call(
        backward_kernel,
        grid=(heads,),
        in_specs=[
            block,
            block,
            row,
            block,
            block,
            row,
            block,
            block,
            block,
            block,
            pl.BlockSpec((seqs, 8, width), lambda h: (0, 0, h)),
            pl.BlockSpec((8, width), lambda h: (0, h)),
            weight,
            pl.BlockSpec((width, width), lambda h: (h, 1)),
        ],
        out_specs=[block, weight, weight, pl.BlockSpec((8, width), lambda h: (0, h))],
        out_shape=[
            jax.ShapeDtypeStruct(rec.shape, F32),
            jax.ShapeDtypeStruct((full, width), F32),
            jax.ShapeDtypeStruct((full, width), F32),
            jax.ShapeDtypeStruct((8, full), F32),
        ],
        scratch_shapes=[pltpu.VMEM((seqs, length + 8, width), F32)] * 2,
        cost_estimate=cost(seqs * length * full * width * 8, rec.size * 40),
        name="recur_backward",
    )(local, ahead, entering, state, prod, carry, conv, sig_r, sig_i, rec, halo, vec, gates, gates)


def rms_scale(values, gain):
    return values * lax.rsqrt(jnp.mean(values * values, axis=-1, keepdims=True) + 1e-06) * gain


def mlp_act(gate_pre, up_pre):
    return jax.nn.gelu(gate_pre, approximate=True) * up_pre


def mm(left, right):
    return jnp.dot(left, right, preferred_element_type=F32)


def mm_rows(left, weight):
    return lax.dot_general(left, weight, (((1,), (1,)), ((), ())), preferred_element_type=F32)


def outer_sum(left, right):
    return lax.dot_general(left, right, (((0,), (0,)), ((), ())), preferred_element_type=F32)


def on_device(
    block_input,
    w_branch,
    w_recur_in,
    w_recur_out,
    w_rgate,
    w_igate,
    conv_weight,
    conv_bias,
    rgate_bias,
    igate_bias,
    rate_param,
    norm_gain,
    mlp_gain,
    w_gate,
    w_up,
    w_down,
    cotangent,
):
    z, y, c = (lax.axis_index(axis) for axis in ("z", "y", "c"))
    z_count = lax.axis_size("z")
    devices = z_count * 8
    first_y, first_c = y == 0, c == 0
    half_tokens, width = block_input.shape[1:]
    length = 2 * half_tokens
    channels = w_branch.shape[1] // 2
    z_places = [z_at(j) for j in range(z_count)]
    z_back = [z_place(j) for j in range(z_count)]

    def own_sequence(block):
        return ordered(first_y, pick(block, y, 0), swap(pick(block, 1 - y, 0), "y"), 0)

    def own_tokens(rows):
        halves = rows.reshape(2, half_tokens, width)
        mine, theirs = pick(halves, y, 0), swap(pick(halves, 1 - y, 0), "y")
        return jnp.where(first_y, jnp.stack([mine, theirs]), jnp.stack([theirs, mine]))

    def core_columns(weight):
        parts = weight.reshape(weight.shape[0], 2, channels)
        return ordered(first_c, pick(parts, c, 1), swap(pick(parts, 1 - c, 1), "c"), 0)

    gains = jnp.stack([norm_gain, mlp_gain]).reshape(1, -1)
    gains = lax.all_to_all(jnp.tile(gains, (devices, 1)), EVERY, 0, 0, tiled=True)
    gains = jnp.swapaxes(gains.reshape(devices, 2, -1), 0, 1).reshape(2, width).astype(F32)
    ngain, mgain = gains[0], gains[1]

    vectors = jnp.concatenate(
        [conv_weight, conv_bias[None], rgate_bias[None], igate_bias[None], rate_param[None]]
    )
    vectors = jnp.pad(vectors.T, ((0, 0), (0, 120)))
    gate_shard = jnp.concatenate([w_rgate, w_igate, vectors], axis=1)
    gate_shard = lax.ppermute(gate_shard, EVERY, to_halves(devices))
    gates = whole_gather(gate_shard, "y", "x")
    branch_full = fine_gather(core_columns(w_branch), "y", "x")
    recur_in_full = fine_gather(core_columns(w_recur_in), "x", "y")
    out_shard = lax.ppermute(w_recur_out, EVERY, to_halves(devices))
    out_full = jnp.concatenate(
        [
            whole_gather(out_shard[:, : width // 2], "y", "x"),
            whole_gather(out_shard[:, width // 2 :], "x", "y"),
        ],
        axis=1,
    )

    units = w_gate.shape[1] // 2
    gate_up = jnp.stack([w_gate, w_up], 1).reshape(w_gate.shape[0], 2, 2, units)
    mine = pick(gate_up, y, 2).reshape(-1, 2 * units)
    theirs = swap(pick(gate_up, 1 - y, 2).reshape(-1, 2 * units), "y")
    gate_up_full = jnp.concatenate(z_gather(ordered(first_y, mine, theirs, 0)))
    down = w_down.reshape(2, units, -1)
    down_shard = ordered(first_y, pick(down, y, 0), swap(pick(down, 1 - y, 0), "y"), 1)
    down_full = jnp.concatenate(z_gather(down_shard), axis=1)

    vec = gates[:, 512:520].T.astype(F32)
    rate = vec[7]
    eight = -8.0 * jax.nn.softplus(rate)
    vec = jnp.concatenate([vec[:7], eight[None]])

    rows_in = own_sequence(block_input).astype(F32)
    normed_f, norm_pull = jax.vjp(rms_scale, rows_in, ngain)
    chips, places = fine_chips(), fine_places()
    normed = columns(low(normed_f), chips)
    normed = jnp.concatenate([normed, swap(normed, "c")])
    branch_pre = mm(normed, branch_full)
    recur_pre = mm(normed, recur_in_full).reshape(2, length, channels)
    branch_act, gelu_pull = jax.vjp(partial(jax.nn.gelu, approximate=True), branch_pre)
    halo = z_shift(recur_pre[:, length - 8 :], 1)
    conv, sig_r, sig_i, decay, state, prod = run_forward(recur_pre, halo, vec, gates)
    carry = z_carry(prod[:, -1], state[:, -1], 1)
    states = (state + prod * carry[:, None]).reshape(2 * length, channels)
    mixed_low = low(states * branch_act)
    recur_out = mm(mixed_low, out_full)
    middle = rows_in + recur_out[:length] + swap(recur_out[length:], "c")

    normed2_f, norm2_pull = jax.vjp(rms_scale, middle, mgain)
    tokens_all = group_gather(columns(low(normed2_f), z_places))
    pre = mm(tokens_all, gate_up_full)
    hidden_f, mlp_pull = jax.vjp(mlp_act, pre[:, :units], pre[:, units:])
    hidden = low(hidden_f)
    mlp_out = columns(group_scatter(mm(hidden, down_full)), z_back)
    block_output = own_tokens(low(middle + mlp_out))

    own_grad = own_sequence(cotangent)
    grad_all = group_gather(columns(own_grad, z_places))
    grad_hidden = mm_rows(grad_all, down_full)
    grad_pre = jnp.concatenate([low(g) for g in mlp_pull(grad_hidden)], axis=1)
    grad_normed2 = columns(group_scatter(mm_rows(grad_pre, gate_up_full)), z_back)
    block = width // z_count
    grad_gate_up = z_scatter(
        lambda j: outer_sum(tokens_all[:, j * block : (j + 1) * block], grad_pre)
    )
    grad_down = z_scatter(lambda j: outer_sum(hidden, grad_all[:, j * block : (j + 1) * block]))
    grad_gate_up = grad_gate_up.reshape(2, block // 2, 2 * units)
    kept, other = pick(grad_gate_up, y, 0), swap(low(pick(grad_gate_up, 1 - y, 0)), "y")
    kept = kept.reshape(-1, 2, 1, units)
    other = other.astype(F32).reshape(-1, 2, 1, units)
    both = ordered(first_y, kept, other, 2).reshape(-1, 2, 2 * units)
    grad_gate, grad_up = both[:, 0], both[:, 1]
    grad_down = grad_down.reshape(units, 2, -1)
    kept, other = pick(grad_down, y, 1), swap(low(pick(grad_down, 1 - y, 1)), "y")
    grad_down = ordered(first_y, kept, other.astype(F32), 0)

    grad_middle_norm, grad_mgain = norm2_pull(grad_normed2)
    grad_middle = own_grad.astype(F32) + grad_middle_norm
    grad_out_low = low(grad_middle)
    grad_out_low = jnp.concatenate([grad_out_low, swap(grad_out_low, "c")])
    grad_mixed = mm_rows(grad_out_low, out_full)
    grad_states = (grad_mixed * branch_act).reshape(2, length, channels)
    grad_branch_low = low(gelu_pull(grad_mixed * states)[0])
    local, ahead, sent = run_reverse(decay, grad_states)
    entering = z_carry(prod[:, -1], sent, -1)
    grad_conv, grad_rgate, grad_igate, small = run_backward(
        local, ahead, entering, state, prod, carry, conv, sig_r, sig_i, recur_pre, halo, vec, gates
    )
    rim = z_shift(grad_conv[:, :8], -1)
    grad_ext = jnp.concatenate([grad_conv, rim], axis=1)
    grad_recur_low = low(sum(vec[k] * grad_ext[:, k : k + length] for k in range(CONV)))
    grad_recur_low = grad_recur_low.reshape(2 * length, channels)
    grad_normed = mm_rows(grad_branch_low, branch_full) + mm_rows(grad_recur_low, recur_in_full)
    grad_normed = grad_normed[:length] + swap(grad_normed[length:], "c")
    grad_rows, grad_ngain = norm_pull(columns(grad_normed, places))
    input_grad = own_tokens(low(grad_middle + grad_rows))

    def own_rows(chunk):
        parts = chunk.reshape(2, -1, channels)
        return ordered(first_c, pick(parts, c, 0), swap(pick(parts, 1 - c, 0), "c"), 1)

    from_halves = [(target, source) for source, target in to_halves(devices)]
    grad_out_w = outer_sum(mixed_low, grad_out_low)
    grad_out_w = jnp.concatenate(
        [
            whole_scatter(grad_out_w[:, : width // 2], "y", "x"),
            whole_scatter(grad_out_w[:, width // 2 :], "x", "y"),
        ],
        axis=1,
    )
    grad_recur_out = lax.ppermute(low(grad_out_w), EVERY, from_halves).astype(F32)
    small = jnp.concatenate([small[:7], (small[7] * -8.0 * jax.nn.sigmoid(rate))[None]])
    small = jnp.pad(small.T, ((0, 0), (0, 120)))
    gate_grads = jnp.concatenate([grad_rgate, grad_igate, small], axis=1)
    gate_grads = lax.ppermute(whole_scatter(gate_grads, "y", "x"), EVERY, from_halves)
    small = gate_grads[:, 512:520].T
    grad_branch = own_rows(fine_scatter(outer_sum(normed, grad_branch_low), "y", "x"))
    grad_recur_in = own_rows(fine_scatter(outer_sum(normed, grad_recur_low), "x", "y"))
    gain_grads = jnp.stack([grad_ngain, grad_mgain]).reshape(2, devices, -1)
    gain_grads = jnp.swapaxes(gain_grads, 0, 1).reshape(devices, -1)
    gain_grads = lax.all_to_all(gain_grads, EVERY, 0, 0, tiled=True)
    gain_grads = jnp.sum(gain_grads, axis=0).reshape(2, -1)
    return (
        block_output,
        input_grad,
        grad_branch,
        grad_recur_in,
        grad_recur_out,
        gate_grads[:, :256],
        gate_grads[:, 256:512],
        small[:4],
        small[4],
        small[5],
        small[6],
        small[7],
        gain_grads[0],
        gain_grads[1],
        grad_gate,
        grad_up,
        grad_down,
    )


def solution(mesh):
    seq, mlp = mesh.shape["seq"], mesh.shape["mlp"]
    fine = Mesh(mesh.devices.reshape(seq // 2, 2, mlp // 2, 2), EVERY)
    over_seq, over_mlp = ("z", "y"), ("x", "c")
    rows, channel, vector = P(EVERY, None), P(None, EVERY), P(EVERY)
    tokens = P(over_mlp, over_seq, None)
    in_specs = (
        (tokens,) + (rows,) * 5 + (channel,) + (vector,) * 6
        + (P(over_seq, over_mlp), P(over_seq, over_mlp), P(over_mlp, over_seq), tokens)
    )
    out_specs = (
        (tokens, tokens) + (rows,) * 5 + (channel,) + (vector,) * 6
        + (P(over_seq, over_mlp), P(over_seq, over_mlp), P(over_mlp, over_seq))
    )
    return jax.shard_map(
        on_device, mesh=fine, in_specs=in_specs, out_specs=out_specs, check_vma=False
    )
```

time: 3270 us -> 1060 us (0.32)
  waiting for transfers between devices: 1950 us -> 499 us
  local copies, waits for them, and re-layouts: 488 us -> 119 us
  blocking collectives: 300 us -> 0 us
  starting transfers between devices: 17.3 us -> 198 us
  matrix products: 252 us -> 92.1 us
  other arithmetic: 214 us -> 94 us
    reduce_scatter x12 -> x0, waiting for transfers between devices: 1540 us -> none  [the longest x1 233 us: on_device(): lax.psum_scatter(recur_total[1], ('seq', 'mlp'), scatter_dimension=0, til...]
    ppermute x4 -> x152, waiting for transfers between devices: 3.3 us -> 474 us  [the longest x98 232 us: swap(): return lax.ppermute(value, axis, PAIR)]
    all_gather x12 -> x0, waiting for transfers between devices: 395 us -> none  [the longest x1 94.5 us: on_device(): lax.all_gather(w_gate, 'seq', axis=0, tiled=True)]
    slice x162 -> x18, local copies, waits for them, and re-layouts: 303 us -> 12.5 us  [the longest x1 5.06 us: on_device(): grad_out_w[:, :width // 2]]
    all_gather x7 -> x0, blocking collectives: 215 us -> none  [the longest x6 184 us: prefix(): everything = jax.tree.map(lambda part: lax.all_gather(part, axis), shard)]
    ppermute x4 -> x152, starting transfers between devices: 14.9 us -> 186 us  [the longest x42 79 us: z_next(): lax.ppermute(value, 'z', [(RING[p], RING[(p + 1) % count]) for p in range...]
    dot_general x48 -> x21, matrix products: 252 us -> 92.1 us  [the longest x11 34.7 us: outer_sum(): lax.dot_general(left, right, (((0,), (0,)), ((), ())), preferred_element_...]
    pad x80 -> x0, local copies, waits for them, and re-layouts: 109 us -> none  [the longest x40 58.9 us: micro_pass(): lax.associative_scan(combine_pairs, (decay_rate, driven), axis=1)]
  transfers between devices with their start and end apart: 29 -> 154, of which waited for: 17 -> 72; matrix products, arithmetic and copies ran while one was open for 17% -> 27% of each run, Pallas kernels for 0% -> 2%
where the time goes in v1:
time: 1060 us; the launch traced here: 1050 us
  waiting for transfers between devices  499 us (47%)
  starting transfers between devices  198 us (19%)
  local copies, waits for them, and re-layouts  119 us (11%)
  other arithmetic  94 us (9%)
  matrix products  92.1 us (9%)
  Pallas kernels  23.8 us (2%)
  between operations  20.5 us (2%)
    ppermute x98, waiting for transfers between devices, swap(): return lax.ppermute(value, axis, PAIR)  232 us
    ppermute x42, waiting for transfers between devices, z_next(): lax.ppermute(value, 'z', [(RING[p], RING[(p + 1) % count]) for p in range...  224 us
    ppermute x42, starting transfers between devices, z_next(): lax.ppermute(value, 'z', [(RING[p], RING[(p + 1) % count]) for p in range...  79 us
    ppermute x98, starting transfers between devices, swap(): return lax.ppermute(value, axis, PAIR)  71.5 us
    unnamed x286, local copies, waits for them, and re-layouts  56.2 us
    dot_general x11, matrix products, outer_sum(): lax.dot_general(left, right, (((0,), (0,)), ((), ())), preferred_element_...  34.7 us
    dot_general x5, matrix products, mm_rows(): lax.dot_general(left, weight, (((1,), (1,)), ((), ())), preferred_element...  29.1 us
    dot_general x5, matrix products, mm(): return jnp.dot(left, right, preferred_element_type=F32)  28.3 us
  transfers between devices with their start and end apart: 154, of which 72 were waited for; matrix products, arithmetic and copies ran while one was open for 27% of the time, Pallas kernels for 2%

profile of v1, /device:TPU:10, one launch (start us, length us, event | category | flops | bytes accessed | tf_op | source)
XLA Modules:
  0.0 1046.8 jit_solution(12821203697181268446)
XLA Ops:
  2.1 6.0 all-to-all-start
  60.5 5.9 collective-permute-done.21
  101.3 6.0 collective-permute-done.30
  111.7 6.3 collective-permute-done.4
  129.6 6.1 collective-permute-done.33
  145.5 7.8 collective-permute-done.6
  157.7 6.9 collective-permute-done.8
  169.5 6.6 collective-permute-done.35
  181.7 6.7 collective-permute-done.38
  189.9 5.5 collective-permute-done.39
  199.0 10.5 %collective-permute-done.41 = bf16[128,1280]{1,0:T(8,128)(2,1)S(1)} collective-permute-done((bf16[128,1280]{1,0:T(8,128)(2,1)S(1)}, bf16[128,1280]{1,0:T(8,128)(2,1)S(1)}, u32[]{:S(2)}, u32[]{:S(2)}) %collective-permute-start.41) | collective-permute-done | bytes 327712 | tf_op jit(solution)/shard_map/ppermute | solution.py:19
  211.0 5.5 collective-permute-done.42
  219.3 15.5 %collective-permute-done.12 = bf16[128,1280]{1,0:T(8,128)(2,1)S(1)} collective-permute-done((bf16[128,1280]{1,0:T(8,128)(2,1)S(1)}, bf16[128,1280]{1,0:T(8,128)(2,1)S(1)}, u32[]{:S(2)}, u32[]{:S(2)}) %collective-permute-start.12) | collective-permute-done | bytes 327712 | tf_op jit(solution)/shard_map/ppermute | solution.py:19
  241.6 10.8 %collective-permute-done.15 = bf16[128,1280]{1,0:T(8,128)(2,1)S(1)} collective-permute-done((bf16[128,1280]{1,0:T(8,128)(2,1)S(1)}, bf16[128,1280]{1,0:T(8,128)(2,1)S(1)}, u32[]{:S(2)}, u32[]{:S(2)}) %collective-permute-start.15) | collective-permute-done | bytes 327712 | tf_op jit(solution)/shard_map/ppermute | solution.py:19
  264.6 12.5 %collective-permute-done.24 = bf16[4,2,80,640]{3,2,0,1:T(8,128)(2,1)S(1)} collective-permute-done((bf16[4,2,80,640]{3,2,0,1:T(8,128)(2,1)S(1)}, bf16[4,2,80,640]{3,2,0,1:T(8,128)(2,1)S(1)}, u32[]{:S(2)}, u32[]{:S(2)}) %collective-permute-start.24) | collective-permute-done | bytes 819232 | tf_op jit(solution)/shard_map/ppermute | solution.py:19
  295.4 9.5 recur_forward.1
  309.2 6.9 collective-permute-start.26
  322.6 6.0 fusion.29
  328.6 13.2 %collective-permute-done.54 = bf16[4,2,80,1024]{3,2,0,1:T(8,128)(2,1)S(1)} collective-permute-done((bf16[4,2,80,1024]{3,2,0,1:T(8,128)(2,1)S(1)}, bf16[4,2,80,1024]{3,2,0,1:T(8,128)(2,1)S(1)}, u32[]{:S(2)}, u32[]{:S(2)}) %collective-permute-start.54) | collective-permute-done | bytes 1310752 | tf_op jit(solution)/shard_map/ppermute | solution.py:19
  380.7 25.2 %collective-permute-done.63 = bf16[512,1536]{0,1:T(8,128)(2,1)} collective-permute-done((bf16[512,1536]{0,1:T(8,128)(2,1)S(1)}, bf16[512,1536]{0,1:T(8,128)(2,1)}, u32[]{:S(2)}, u32[]{:S(2)}) %collective-permute-start.63) | collective-permute-done | bytes 1572896 | tf_op jit(solution)/shard_map/ppermute | solution.py:56
  415.7 7.1 collective-permute-done.67
  436.8 34.7 %collective-permute-done.68 = bf16[768,512]{1,0:T(8,128)(2,1)} collective-permute-done((bf16[768,512]{1,0:T(8,128)(2,1)}, bf16[768,512]{1,0:T(8,128)(2,1)}, u32[]{:S(2)}, u32[]{:S(2)}) %collective-permute-start.68) | collective-permute-done | bytes 786464 | tf_op jit(solution)/shard_map/ppermute | solution.py:56
  485.3 38.8 %collective-permute-done.65 = bf16[512,1536]{0,1:T(8,128)(2,1)S(1)} collective-permute-done((bf16[512,1536]{0,1:T(8,128)(2,1)}, bf16[512,1536]{0,1:T(8,128)(2,1)S(1)}, u32[]{:S(2)}, u32[]{:S(2)}) %collective-permute-start.65) | collective-permute-done | bytes 1572896 | tf_op jit(solution)/shard_map/ppermute | solution.py:56
  524.1 11.4 %fusion.33 = f32[1024,1536]{1,0:T(8,128)} fusion(bf16[1024,2048]{1,0:T(8,128)(2,1)} %constant_dynamic-update-slice_fusion.48, bf16[512,1536]{0,1:T(8,128)(2,1)S(1)} %collective-permute-done.65, bf16[512,1536]{0,1:T(8,128)(2,1)} %collective-permute-done.64, bf16[512,1536]{0,1:T(8,128)(2,1)} %collective-permute-done.63, bf16[512,1536]{0,1:T(8,128)(2,1)S(1)} %copy-done.47), kind=kOutput, calls=%fused_computation.107 | convolution fusion | flops 6467616768 | bytes 16777216 | tf_op jit(solution)/shard_map/dot_general | solution.py:435
  535.5 10.5 %fusion.8 = (bf16[1024,768]{1,0:T(8,128)(2,1)S(1)}, bf16[1024,768]{1,0:T(8,128)(2,1)S(1)}, bf16[1024,768]{1,0:T(8,128)(2,1)S(1)}) fusion(f32[1024,1536]{1,0:T(8,128)} %fusion.33, bf16[1024,2048]{1,0:T(8,128)(2,1)} %constant_dynamic-update-slice_fusion.55, bf16[768,512]{1,0:T(8,128)(2,1)S(1)} %collective-permute-done.69, ...), kind=kOutput, calls=%fused_computation.21 | convolution fusion | flops 3254255616 | bytes 18350080 | tf_op jit(solution)/shard_map/dot_general | solution.py:439
  555.9 9.5 fusion.32
  565.8 5.5 collective-permute-done.148
  575.4 5.0 fusion.109
  580.9 24.1 %collective-permute-done.144 = bf16[512,1536]{1,0:T(8,128)(2,1)S(1)} collective-permute-done((bf16[512,1536]{1,0:T(8,128)(2,1)S(1)}, bf16[512,1536]{1,0:T(8,128)(2,1)S(1)}, u32[]{:S(2)}, u32[]{:S(2)}) %collective-permute-start.144) | collective-permute-done | bytes 1572896 | tf_op jit(solution)/shard_map/ppermute | solution.py:56
  611.1 10.8 %collective-permute-done.149 = bf16[768,512]{0,1:T(8,128)(2,1)S(1)} collective-permute-done((bf16[768,512]{0,1:T(8,128)(2,1)S(1)}, bf16[768,512]{0,1:T(8,128)(2,1)S(1)}, u32[]{:S(2)}, u32[]{:S(2)}) %collective-permute-start.149) | collective-permute-done | bytes 786464 | tf_op jit(solution)/shard_map/ppermute | solution.py:56
  644.0 25.2 %collective-permute-done.150 = bf16[768,512]{0,1:T(8,128)(2,1)S(1)} collective-permute-done((bf16[768,512]{0,1:T(8,128)(2,1)}, bf16[768,512]{0,1:T(8,128)(2,1)S(1)}, u32[]{:S(2)}, u32[]{:S(2)}) %collective-permute-start.150) | collective-permute-done | bytes 786464 | tf_op jit(solution)/shard_map/ppermute | solution.py:56
  678.8 7.2 collective-permute-done.151
  699.6 5.1 fusion.9
  710.8 5.0 recur_reverse.1
  735.6 5.1 fusion.157
  749.4 9.3 recur_backward.1
  790.9 6.2 collective-permute-done.118
  797.9 6.2 collective-permute-done.115
  811.1 7.4 collective-permute-done.106
  822.6 6.1 collective-permute-done.122
  854.5 6.5 all-to-all-start.1
  863.5 24.9 %all-to-all-done.1 = f32[32,1,128]{2,1,0:T(1,128)S(1)} async-done(((f32[32,1,128]{2,1,0:T(1,128)}), f32[32,1,128]{2,1,0:T(1,128)S(1)}, u32[]{:S(2)}, u32[]{:S(2)}) %all-to-all-start.1) | async-done | bytes 16416 | tf_op jit(solution)/shard_map/all_to_all | solution.py:612
  906.7 14.3 %collective-permute-done.132 = bf16[4,2,80,1024]{3,2,0,1:T(8,128)(2,1)} collective-permute-done((bf16[4,2,80,1024]{3,2,0,1:T(8,128)(2,1)}, bf16[4,2,80,1024]{3,2,0,1:T(8,128)(2,1)}, u32[]{:S(2)}, u32[]{:S(2)}) %collective-permute-start.132) | collective-permute-done | bytes 1310752 | tf_op jit(solution)/shard_map/ppermute | solution.py:19
  927.2 6.9 collective-permute-done.100
  943.4 5.8 collective-permute-done.141
  978.2 7.3 collective-permute-done.143
  987.5 10.8 %collective-permute-done.128 = bf16[4,80,1024]{2,1,0:T(8,128)(2,1)} collective-permute-done((bf16[4,80,1024]{2,1,0:T(8,128)(2,1)}, bf16[4,80,1024]{2,1,0:T(8,128)(2,1)}, u32[]{:S(2)}, u32[]{:S(2)}) %collective-permute-start.128) | collective-permute-done | bytes 655392 | tf_op jit(solution)/shard_map/ppermute | solution.py:19
  1037.8 6.9 collective-permute-done.137
  (758 shorter events, 523.3 us)
Async XLA Ops:
  2.1 37.7 %all-to-all-start = ((bf16[32,1,128]{2,1,0:T(2,128)(2,1)}), bf16[32,1,128]{2,1,0:T(2,128)(2,1)S(1)}, u32[]{:S(2)}, u32[]{:S(2)}) async-start(bf16[32,1,128]{2,1,0:T(2,128)(2,1)} %tile.9), calls=%async_computation | async-start | bytes 32768 | tf_op jit(solution)/shard_map/all_to_all | solution.py:488
  10.4 32.0 %collective-permute-start.19 = (bf16[80,640]{1,0:T(8,128)(2,1)}, bf16[80,640]{1,0:T(8,128)(2,1)}, u32[]{:S(2)}, u32[]{:S(2)}) collective-permute-start(bf16[80,640]{1,0:T(8,128)(2,1)} %fusion.126), channel_id=1, source_target_pairs={{0,0},{16,1},{1,2},{17,3},{2,4},{18,5},{3,6},{19,7},{4,8},{20,9},{... | collective-permute-start | bytes 307208 | tf_op jit(solution)/shard_map/ppermute | solution.py:497
  20.1 48.9 %collective-permute-start.44 = (bf16[80,2048]{1,0:T(8,128)(2,1)}, bf16[80,2048]{1,0:T(8,128)(2,1)}, u32[]{:S(2)}, u32[]{:S(2)}) collective-permute-start(bf16[80,2048]{1,0:T(8,128)(2,1)} %param.116), channel_id=1, source_target_pairs={{0,0},{16,1},{1,2},{17,3},{2,4},{18,5},{3,6},{19,7},{4,8},{20,9},{... | collective-permute-start | bytes 983048 | tf_op jit(solution)/shard_map/ppermute | solution.py:501
  42.5 324.2 %collective-permute-start.62 = (bf16[256,1536]{0,1:T(8,128)(2,1)}, bf16[256,1536]{0,1:T(8,128)(2,1)}, u32[]{:S(2)}, u32[]{:S(2)}) collective-permute-start(bf16[256,1536]{0,1:T(8,128)(2,1)} %bitcast.456), channel_id=1, source_target_pairs={{0,4},{4,0},{1,5},{5,1},{2,6},{6,2},{3,7},{7,3},{8,12},{12,8},{9,1... | collective-permute-start | bytes 2359304 | tf_op jit(solution)/shard_map/ppermute | solution.py:19
  44.8 36.3 %collective-permute-start.29 = (bf16[128,1280]{1,0:T(8,128)(2,1)S(1)}, bf16[128,1280]{1,0:T(8,128)(2,1)S(1)}, u32[]{:S(2)}, u32[]{:S(2)}) collective-permute-start(bf16[128,1280]{1,0:T(8,128)(2,1)S(1)} %get-tuple-element.168), channel_id=1, source_target_pairs={{0,8},{8,24},{24,16},{16,0},{1,9},{9,25},{25,17},{17,1},{2,10},{10... | collective-permute-start | bytes 983048 | tf_op jit(solution)/shard_map/ppermute | solution.py:56
  76.2 101.6 %collective-permute-start.36 = (bf16[128,1280]{1,0:T(8,128)(2,1)S(1)}, bf16[128,1280]{1,0:T(8,128)(2,1)S(1)}, u32[]{:S(2)}, u32[]{:S(2)}) collective-permute-start(bf16[128,1280]{1,0:T(8,128)(2,1)S(1)} %get-tuple-element.168), channel_id=1, source_target_pairs={{0,2},{2,0},{1,3},{3,1},{4,6},{6,4},{5,7},{7,5},{8,10},{10,8},{9,1... | collective-permute-start | bytes 983048 | tf_op jit(solution)/shard_map/ppermute | solution.py:19
  91.7 35.1 %collective-permute-start.32 = (bf16[128,1280]{1,0:T(8,128)(2,1)S(1)}, bf16[128,1280]{1,0:T(8,128)(2,1)S(1)}, u32[]{:S(2)}, u32[]{:S(2)}) collective-permute-start(bf16[128,1280]{1,0:T(8,128)(2,1)S(1)} %get-tuple-element.168), channel_id=1, source_target_pairs={{0,4},{4,0},{1,5},{5,1},{2,6},{6,2},{3,7},{7,3},{8,12},{12,8},{9,1... | collective-permute-start | bytes 983048 | tf_op jit(solution)/shard_map/ppermute | solution.py:19
  99.7 69.2 %collective-permute-start.10 = (bf16[128,1280]{1,0:T(8,128)(2,1)S(1)}, bf16[128,1280]{1,0:T(8,128)(2,1)S(1)}, u32[]{:S(2)}, u32[]{:S(2)}) collective-permute-start(bf16[128,1280]{1,0:T(8,128)(2,1)S(1)} %get-tuple-element.170), channel_id=1, source_target_pairs={{0,2},{2,0},{1,3},{3,1},{4,6},{6,4},{5,7},{7,5},{8,10},{10,8},{9,1... | collective-permute-start | bytes 983048 | tf_op jit(solution)/shard_map/ppermute | solution.py:19
  164.6 32.3 %collective-permute-start.40 = (bf16[128,1280]{1,0:T(8,128)(2,1)S(1)}, bf16[128,1280]{1,0:T(8,128)(2,1)S(1)}, u32[]{:S(2)}, u32[]{:S(2)}) collective-permute-start(bf16[128,1280]{1,0:T(8,128)(2,1)S(1)} %collective-permute-done.32), channel_id=1, source_target_pairs={{0,2},{2,0},{1,3},{3,1},{4,6},{6,4},{5,7},{7,5},{8,10},{10,8},{9,1... | collective-permute-start | bytes 983048 | tf_op jit(solution)/shard_map/ppermute | solution.py:19
  176.1 63.4 %collective-permute-start.14 = (bf16[128,1280]{1,0:T(8,128)(2,1)S(1)}, bf16[128,1280]{1,0:T(8,128)(2,1)S(1)}, u32[]{:S(2)}, u32[]{:S(2)}) collective-permute-start(bf16[128,1280]{1,0:T(8,128)(2,1)S(1)} %collective-permute-done.10), channel_id=1, source_target_pairs={{0,4},{4,0},{1,5},{5,1},{2,6},{6,2},{3,7},{7,3},{8,12},{12,8},{9,1... | collective-permute-start | bytes 983048 | tf_op jit(solution)/shard_map/ppermute | solution.py:19
  209.5 46.5 %collective-permute-start.53 = (bf16[4,80,1024]{2,1,0:T(8,128)(2,1)S(1)}, bf16[4,80,1024]{2,1,0:T(8,128)(2,1)S(1)}, u32[]{:S(2)}, u32[]{:S(2)}) collective-permute-start(bf16[4,80,1024]{2,1,0:T(8,128)(2,1)S(1)} %get-tuple-element.246), channel_id=1, source_target_pairs={{0,2},{2,0},{1,3},{3,1},{4,6},{6,4},{5,7},{7,5},{8,10},{10,8},{9,1... | collective-permute-start | bytes 1966088 | tf_op jit(solution)/shard_map/ppermute | solution.py:19
  252.4 31.6 %collective-permute-start.1 = (bf16[128,2048]{1,0:T(8,128)(2,1)}, bf16[128,2048]{1,0:T(8,128)(2,1)}, u32[]{:S(2)}, u32[]{:S(2)}) collective-permute-start(bf16[128,2048]{1,0:T(8,128)(2,1)} %constant_dynamic-update-slice_fusion), channel_id=1, source_target_pairs={{0,1},{1,0},{2,3},{3,2},{4,5},{5,4},{6,7},{7,6},{8,9},{9,8},{10,11... | collective-permute-start | bytes 1572872 | tf_op jit(solution)/shard_map/ppermute | solution.py:19
  256.0 60.1 %collective-permute-start.43 = (bf16[128,1280]{1,0:T(8,128)(2,1)}, bf16[128,1280]{1,0:T(8,128)(2,1)}, u32[]{:S(2)}, u32[]{:S(2)}) collective-permute-start(bf16[128,1280]{1,0:T(8,128)(2,1)} %collective-permute-done.35), channel_id=1, source_target_pairs={{0,2},{2,0},{1,3},{3,1},{4,6},{6,4},{5,7},{7,5},{8,10},{10,8},{9,1... | collective-permute-start | bytes 983048 | tf_op jit(solution)/shard_map/ppermute | solution.py:19
  277.1 65.9 %collective-permute-start.49 = (bf16[4,2,80,1024]{3,2,1,0:T(8,128)(2,1)}, bf16[4,2,80,1024]{3,2,1,0:T(8,128)(2,1)}, u32[]{:S(2)}, u32[]{:S(2)}) collective-permute-start(bf16[4,2,80,1024]{3,2,1,0:T(8,128)(2,1)} %pad_maximum_fusion.8), channel_id=1, source_target_pairs={{0,2},{2,0},{1,3},{3,1},{4,6},{6,4},{5,7},{7,5},{8,10},{10,8},{9,1... | collective-permute-start | bytes 3932168 | tf_op jit(solution)/shard_map/ppermute | solution.py:19
  368.5 37.4 %collective-permute-start.63 = (bf16[512,1536]{0,1:T(8,128)(2,1)S(1)}, bf16[512,1536]{0,1:T(8,128)(2,1)}, u32[]{:S(2)}, u32[]{:S(2)}) collective-permute-start(bf16[512,1536]{0,1:T(8,128)(2,1)S(1)} %maximum_select_fusion.4), channel_id=1, source_target_pairs={{0,8},{8,24},{24,16},{16,0},{1,9},{9,25},{25,17},{17,1},{2,10},{10... | collective-permute-start | bytes 4718600 | tf_op jit(solution)/shard_map/ppermute | solution.py:56
  372.1 37.1 %collective-permute-start.57 = (bf16[128,2048]{1,0:T(8,128)(2,1)}, bf16[128,2048]{1,0:T(8,128)(2,1)S(1)}, u32[]{:S(2)}, u32[]{:S(2)}) collective-permute-start(bf16[128,2048]{1,0:T(8,128)(2,1)} %get-tuple-element.263), channel_id=1, source_target_pairs={{0,4},{4,0},{1,5},{5,1},{2,6},{6,2},{3,7},{7,3},{8,12},{12,8},{9,1... | collective-permute-start | bytes 1572872 | tf_op jit(solution)/shard_map/ppermute | solution.py:19
  376.1 46.6 %collective-permute-start.67 = (bf16[768,512]{1,0:T(8,128)(2,1)}, bf16[768,512]{1,0:T(8,128)(2,1)}, u32[]{:S(2)}, u32[]{:S(2)}) collective-permute-start(bf16[768,512]{1,0:T(8,128)(2,1)} %maximum_select_fusion.6), channel_id=1, source_target_pairs={{0,8},{8,24},{24,16},{16,0},{1,9},{9,25},{25,17},{17,1},{2,10},{10... | collective-permute-start | bytes 2359304 | tf_op jit(solution)/shard_map/ppermute | solution.py:56
  380.7 93.2 %collective-permute-start.82 = (bf16[384,2048]{1,0:T(8,128)(2,1)}, bf16[384,2048]{1,0:T(8,128)(2,1)}, u32[]{:S(2)}, u32[]{:S(2)}) collective-permute-start(bf16[384,2048]{1,0:T(8,128)(2,1)} %pad_maximum_fusion.7), channel_id=1, source_target_pairs={{0,1},{1,0},{2,3},{3,2},{4,5},{5,4},{6,7},{7,6},{8,9},{9,8},{10,11... | collective-permute-start | bytes 4718600 | tf_op jit(solution)/shard_map/ppermute | solution.py:19
  405.9 66.8 %collective-permute-start.64 = (bf16[512,1536]{0,1:T(8,128)(2,1)}, bf16[512,1536]{0,1:T(8,128)(2,1)}, u32[]{:S(2)}, u32[]{:S(2)}) collective-permute-start(bf16[512,1536]{0,1:T(8,128)(2,1)} %collective-permute-done.63), channel_id=1, source_target_pairs={{0,8},{8,24},{24,16},{16,0},{1,9},{9,25},{25,17},{17,1},{2,10},{10... | collective-permute-start | bytes 4718600 | tf_op jit(solution)/shard_map/ppermute | solution.py:56
  422.8 48.8 %collective-permute-start.68 = (bf16[768,512]{1,0:T(8,128)(2,1)}, bf16[768,512]{1,0:T(8,128)(2,1)}, u32[]{:S(2)}, u32[]{:S(2)}) collective-permute-start(bf16[768,512]{1,0:T(8,128)(2,1)} %collective-permute-done.67), channel_id=1, source_target_pairs={{0,8},{8,24},{24,16},{16,0},{1,9},{9,25},{25,17},{17,1},{2,10},{10... | collective-permute-start | bytes 2359304 | tf_op jit(solution)/shard_map/ppermute | solution.py:56
  435.7 46.9 %collective-permute-start.61 = (bf16[384,2048]{1,0:T(8,128)(2,1)}, bf16[384,2048]{1,0:T(8,128)(2,1)}, u32[]{:S(2)}, u32[]{:S(2)}) collective-permute-start(bf16[384,2048]{1,0:T(8,128)(2,1)} %pad_maximum_fusion.6), channel_id=1, source_target_pairs={{0,1},{1,0},{2,3},{3,2},{4,5},{5,4},{6,7},{7,6},{8,9},{9,8},{10,11... | collective-permute-start | bytes 4718600 | tf_op jit(solution)/shard_map/ppermute | solution.py:19
  471.5 64.0 %collective-permute-start.69 = (bf16[768,512]{1,0:T(8,128)(2,1)}, bf16[768,512]{1,0:T(8,128)(2,1)S(1)}, u32[]{:S(2)}, u32[]{:S(2)}) collective-permute-start(bf16[768,512]{1,0:T(8,128)(2,1)} %collective-permute-done.68), channel_id=1, source_target_pairs={{0,8},{8,24},{24,16},{16,0},{1,9},{9,25},{25,17},{17,1},{2,10},{10... | collective-permute-start | bytes 2359304 | tf_op jit(solution)/shard_map/ppermute | solution.py:56
  472.7 51.4 %collective-permute-start.65 = (bf16[512,1536]{0,1:T(8,128)(2,1)}, bf16[512,1536]{0,1:T(8,128)(2,1)S(1)}, u32[]{:S(2)}, u32[]{:S(2)}) collective-permute-start(bf16[512,1536]{0,1:T(8,128)(2,1)} %collective-permute-done.64), channel_id=1, source_target_pairs={{0,8},{8,24},{24,16},{16,0},{1,9},{9,25},{25,17},{17,1},{2,10},{10... | collective-permute-start | bytes 4718600 | tf_op jit(solution)/shard_map/ppermute | solution.py:56
  554.6 50.4 %collective-permute-start.144 = (bf16[512,1536]{1,0:T(8,128)(2,1)S(1)}, bf16[512,1536]{1,0:T(8,128)(2,1)S(1)}, u32[]{:S(2)}, u32[]{:S(2)}) collective-permute-start(bf16[512,1536]{1,0:T(8,128)(2,1)S(1)} %convolution_convert_fusion), channel_id=1, source_target_pairs={{0,8},{8,24},{24,16},{16,0},{1,9},{9,25},{25,17},{17,1},{2,10},{10... | collective-permute-start | bytes 4718600 | tf_op jit(solution)/shard_map/ppermute | solution.py:56
  565.7 61.3 %collective-permute-start.83 = (bf16[512,2048]{1,0:T(8,128)(2,1)S(1)}, bf16[512,2048]{1,0:T(8,128)(2,1)S(1)}, u32[]{:S(2)}, u32[]{:S(2)}) collective-permute-start(bf16[512,2048]{1,0:T(8,128)(2,1)S(1)} %slice.859), channel_id=1, source_target_pairs={{0,1},{1,0},{2,3},{3,2},{4,5},{5,4},{6,7},{7,6},{8,9},{9,8},{10,11... | collective-permute-start | bytes 6291464 | tf_op jit(solution)/shard_map/ppermute | solution.py:19
  573.6 48.3 %collective-permute-start.149 = (bf16[768,512]{0,1:T(8,128)(2,1)S(1)}, bf16[768,512]{0,1:T(8,128)(2,1)S(1)}, u32[]{:S(2)}, u32[]{:S(2)}) collective-permute-start(bf16[768,512]{0,1:T(8,128)(2,1)S(1)} %add_convert_fusion.1), channel_id=1, source_target_pairs={{0,8},{8,24},{24,16},{16,0},{1,9},{9,25},{25,17},{17,1},{2,10},{10... | collective-permute-start | bytes 2359304 | tf_op jit(solution)/shard_map/ppermute | solution.py:56
  580.8 49.2 %collective-permute-start.70 = (bf16[512,2048]{1,0:T(8,128)(2,1)S(1)}, bf16[512,2048]{1,0:T(8,128)(2,1)}, u32[]{:S(2)}, u32[]{:S(2)}) collective-permute-start(bf16[512,2048]{1,0:T(8,128)(2,1)S(1)} %slice.860), channel_id=1, source_target_pairs={{0,1},{1,0},{2,3},{3,2},{4,5},{5,4},{6,7},{7,6},{8,9},{9,8},{10,11... | collective-permute-start | bytes 6291464 | tf_op jit(solution)/shard_map/ppermute | solution.py:19
  609.3 89.7 %collective-permute-start.145 = (bf16[512,1536]{1,0:T(8,128)(2,1)}, bf16[512,1536]{1,0:T(8,128)(2,1)}, u32[]{:S(2)}, u32[]{:S(2)}) collective-permute-start(bf16[512,1536]{1,0:T(8,128)(2,1)} %fusion.10), channel_id=1, source_target_pairs={{0,8},{8,24},{24,16},{16,0},{1,9},{9,25},{25,17},{17,1},{2,10},{10... | collective-permute-start | bytes 4718600 | tf_op jit(solution)/shard_map/ppermute | solution.py:56
  625.1 44.1 %collective-permute-start.150 = (bf16[768,512]{0,1:T(8,128)(2,1)}, bf16[768,512]{0,1:T(8,128)(2,1)S(1)}, u32[]{:S(2)}, u32[]{:S(2)}) collective-permute-start(bf16[768,512]{0,1:T(8,128)(2,1)} %add_convert_fusion), channel_id=1, source_target_pairs={{0,8},{8,24},{24,16},{16,0},{1,9},{9,25},{25,17},{17,1},{2,10},{10... | collective-permute-start | bytes 2359304 | tf_op jit(solution)/shard_map/ppermute | solution.py:56
  638.5 49.8 %collective-permute-start.87 = (bf16[128,2048]{1,0:T(8,128)(2,1)}, bf16[128,2048]{1,0:T(8,128)(2,1)}, u32[]{:S(2)}, u32[]{:S(2)}) collective-permute-start(bf16[128,2048]{1,0:T(8,128)(2,1)} %pad_maximum_fusion.29), channel_id=1, source_target_pairs={{0,4},{4,0},{1,5},{5,1},{2,6},{6,2},{3,7},{7,3},{8,12},{12,8},{9,1... | collective-permute-start | bytes 1572872 | tf_op jit(solution)/shard_map/ppermute | solution.py:19
  642.0 46.3 %collective-permute-start.85 = (bf16[128,2048]{1,0:T(8,128)(2,1)}, bf16[128,2048]{1,0:T(8,128)(2,1)}, u32[]{:S(2)}, u32[]{:S(2)}) collective-permute-start(bf16[128,2048]{1,0:T(8,128)(2,1)} %pad_maximum_fusion.28), channel_id=1, source_target_pairs={{0,2},{2,0},{1,3},{3,1},{4,6},{6,4},{5,7},{7,5},{8,10},{10,8},{9,1... | collective-permute-start | bytes 1572872 | tf_op jit(solution)/shard_map/ppermute | solution.py:19
  704.7 186.8 %collective-permute-start.146 = (bf16[512,1536]{1,0:T(8,128)(2,1)}, bf16[512,1536]{1,0:T(8,128)(2,1)}, u32[]{:S(2)}, u32[]{:S(2)}) collective-permute-start(bf16[512,1536]{1,0:T(8,128)(2,1)} %fusion.9), channel_id=1, source_target_pairs={{0,8},{8,24},{24,16},{16,0},{1,9},{9,25},{25,17},{17,1},{2,10},{10... | collective-permute-start | bytes 4718600 | tf_op jit(solution)/shard_map/ppermute | solution.py:56
  717.2 31.5 %collective-permute-start.90 = (f32[2,2,1280]{2,1,0:T(2,128)S(1)}, f32[2,2,1280]{2,1,0:T(2,128)S(1)}, u32[]{:S(2)}, u32[]{:S(2)}) collective-permute-start(f32[2,2,1280]{2,1,0:T(2,128)S(1)} %pad_maximum_fusion.34), channel_id=1, source_target_pairs={{16,0},{24,8},{17,1},{25,9},{18,2},{26,10},{19,3},{27,11},{20,4},{... | collective-permute-start | bytes 61448 | tf_op jit(solution)/shard_map/ppermute | solution.py:85
  734.1 45.4 %collective-permute-start.105 = (bf16[128,1280]{1,0:T(8,128)(2,1)}, bf16[128,1280]{1,0:T(8,128)(2,1)}, u32[]{:S(2)}, u32[]{:S(2)}) collective-permute-start(bf16[128,1280]{1,0:T(8,128)(2,1)} %get-tuple-element.193), channel_id=1, source_target_pairs={{0,2},{2,0},{1,3},{3,1},{4,6},{6,4},{5,7},{7,5},{8,10},{10,8},{9,1... | collective-permute-start | bytes 983048 | tf_op jit(solution)/shard_map/ppermute | solution.py:19
  746.7 33.4 %collective-permute-start.102 = (bf16[128,1280]{1,0:T(8,128)(2,1)}, bf16[128,1280]{1,0:T(8,128)(2,1)}, u32[]{:S(2)}, u32[]{:S(2)}) collective-permute-start(bf16[128,1280]{1,0:T(8,128)(2,1)} %get-tuple-element.195), channel_id=1, source_target_pairs={{0,2},{2,0},{1,3},{3,1},{4,6},{6,4},{5,7},{7,5},{8,10},{10,8},{9,1... | collective-permute-start | bytes 983048 | tf_op jit(solution)/shard_map/ppermute | solution.py:19
  748.7 32.7 %collective-permute-start.99 = (bf16[128,1280]{1,0:T(8,128)(2,1)}, bf16[128,1280]{1,0:T(8,128)(2,1)}, u32[]{:S(2)}, u32[]{:S(2)}) collective-permute-start(bf16[128,1280]{1,0:T(8,128)(2,1)} %get-tuple-element.197), channel_id=1, source_target_pairs={{0,2},{2,0},{1,3},{3,1},{4,6},{6,4},{5,7},{7,5},{8,10},{10,8},{9,1... | collective-permute-start | bytes 983048 | tf_op jit(solution)/shard_map/ppermute | solution.py:19
  797.1 37.0 %collective-permute-start.101 = (bf16[128,1280]{1,0:T(8,128)(2,1)S(1)}, bf16[128,1280]{1,0:T(8,128)(2,1)S(1)}, u32[]{:S(2)}, u32[]{:S(2)}) collective-permute-start(bf16[128,1280]{1,0:T(8,128)(2,1)S(1)} %get-tuple-element.196), channel_id=1, source_target_pairs={{0,2},{2,0},{1,3},{3,1},{4,6},{6,4},{5,7},{7,5},{8,10},{10,8},{9,1... | collective-permute-start | bytes 983048 | tf_op jit(solution)/shard_map/ppermute | solution.py:19
  844.8 116.5 %collective-permute-start.95 = (bf16[128,1280]{1,0:T(8,128)(2,1)}, bf16[128,1280]{1,0:T(8,128)(2,1)}, u32[]{:S(2)}, u32[]{:S(2)}) collective-permute-start(bf16[128,1280]{1,0:T(8,128)(2,1)} %get-tuple-element.192), channel_id=1, source_target_pairs={{0,2},{2,0},{1,3},{3,1},{4,6},{6,4},{5,7},{7,5},{8,10},{10,8},{9,1... | collective-permute-start | bytes 983048 | tf_op jit(solution)/shard_map/ppermute | solution.py:19
  849.4 76.8 %collective-permute-start.98 = (bf16[128,1280]{1,0:T(8,128)(2,1)}, bf16[128,1280]{1,0:T(8,128)(2,1)}, u32[]{:S(2)}, u32[]{:S(2)}) collective-permute-start(bf16[128,1280]{1,0:T(8,128)(2,1)} %get-tuple-element.198), channel_id=1, source_target_pairs={{0,2},{2,0},{1,3},{3,1},{4,6},{6,4},{5,7},{7,5},{8,10},{10,8},{9,1... | collective-permute-start | bytes 983048 | tf_op jit(solution)/shard_map/ppermute | solution.py:19
  850.2 52.6 %collective-permute-start.127 = (bf16[4,2,80,1024]{3,2,0,1:T(8,128)(2,1)}, bf16[4,2,80,1024]{3,2,0,1:T(8,128)(2,1)}, u32[]{:S(2)}, u32[]{:S(2)}) collective-permute-start(bf16[4,2,80,1024]{3,2,0,1:T(8,128)(2,1)} %fusion.23), channel_id=1, source_target_pairs={{0,2},{2,0},{1,3},{3,1},{4,6},{6,4},{5,7},{7,5},{8,10},{10,8},{9,1... | collective-permute-start | bytes 3932168 | tf_op jit(solution)/shard_map/ppermute | solution.py:19
  852.4 36.6 %collective-permute-start.139 = (bf16[4,80,640]{2,1,0:T(8,128)(2,1)}, bf16[4,80,640]{2,1,0:T(8,128)(2,1)}, u32[]{:S(2)}, u32[]{:S(2)}) collective-permute-start(bf16[4,80,640]{2,1,0:T(8,128)(2,1)} %fusion.114), channel_id=1, source_target_pairs={{0,4},{4,0},{1,5},{5,1},{2,6},{6,2},{3,7},{7,3},{8,12},{12,8},{9,1... | collective-permute-start | bytes 1228808 | tf_op jit(solution)/shard_map/ppermute | solution.py:19
  854.5 33.8 %all-to-all-start.1 = ((f32[32,1,128]{2,1,0:T(1,128)}), f32[32,1,128]{2,1,0:T(1,128)S(1)}, u32[]{:S(2)}, u32[]{:S(2)}) async-start(f32[32,1,128]{2,1,0:T(1,128)} %bitcast.153), calls=%async_computation.1 | async-start | bytes 32768 | tf_op jit(solution)/shard_map/all_to_all | solution.py:612
  889.0 32.0 %collective-permute-start.132 = (bf16[4,2,80,1024]{3,2,0,1:T(8,128)(2,1)}, bf16[4,2,80,1024]{3,2,0,1:T(8,128)(2,1)}, u32[]{:S(2)}, u32[]{:S(2)}) collective-permute-start(bf16[4,2,80,1024]{3,2,0,1:T(8,128)(2,1)} %fusion.24), channel_id=1, source_target_pairs={{0,4},{4,0},{1,5},{5,1},{2,6},{6,2},{3,7},{7,3},{8,12},{12,8},{9,1... | collective-permute-start | bytes 3932168 | tf_op jit(solution)/shard_map/ppermute | solution.py:19
  891.5 59.2 %collective-permute-start.114 = (bf16[128,1280]{1,0:T(8,128)(2,1)}, bf16[128,1280]{1,0:T(8,128)(2,1)}, u32[]{:S(2)}, u32[]{:S(2)}) collective-permute-start(bf16[128,1280]{1,0:T(8,128)(2,1)} %get-tuple-element.190), channel_id=1, source_target_pairs={{0,4},{4,0},{1,5},{5,1},{2,6},{6,2},{3,7},{7,3},{8,12},{12,8},{9,1... | collective-permute-start | bytes 983048 | tf_op jit(solution)/shard_map/ppermute | solution.py:19
  902.7 31.3 %collective-permute-start.100 = (bf16[128,1280]{1,0:T(8,128)(2,1)}, bf16[128,1280]{1,0:T(8,128)(2,1)S(1)}, u32[]{:S(2)}, u32[]{:S(2)}) collective-permute-start(bf16[128,1280]{1,0:T(8,128)(2,1)} %get-tuple-element.180), channel_id=1, source_target_pairs={{0,4},{4,0},{1,5},{5,1},{2,6},{6,2},{3,7},{7,3},{8,12},{12,8},{9,1... | collective-permute-start | bytes 983048 | tf_op jit(solution)/shard_map/ppermute | solution.py:19
  961.3 48.2 %collective-permute-start.147 = (bf16[256,1536]{1,0:T(8,128)(2,1)}, bf16[256,1536]{1,0:T(8,128)(2,1)}, u32[]{:S(2)}, u32[]{:S(2)}) collective-permute-start(bf16[256,1536]{1,0:T(8,128)(2,1)} %fusion.56), channel_id=1, source_target_pairs={{0,4},{4,0},{1,5},{5,1},{2,6},{6,2},{3,7},{7,3},{8,12},{12,8},{9,1... | collective-permute-start | bytes 2359304 | tf_op jit(solution)/shard_map/ppermute | solution.py:19
  966.6 31.7 %collective-permute-start.128 = (bf16[4,80,1024]{2,1,0:T(8,128)(2,1)}, bf16[4,80,1024]{2,1,0:T(8,128)(2,1)}, u32[]{:S(2)}, u32[]{:S(2)}) collective-permute-start(bf16[4,80,1024]{2,1,0:T(8,128)(2,1)} %fusion.60), channel_id=1, source_target_pairs={{0,4},{4,0},{1,5},{5,1},{2,6},{6,2},{3,7},{7,3},{8,12},{12,8},{9,1... | collective-permute-start | bytes 1966088 | tf_op jit(solution)/shard_map/ppermute | solution.py:19
  971.9 31.3 %collective-permute-start.133 = (bf16[4,80,1024]{2,1,0:T(8,128)(2,1)}, bf16[4,80,1024]{2,1,0:T(8,128)(2,1)}, u32[]{:S(2)}, u32[]{:S(2)}) collective-permute-start(bf16[4,80,1024]{2,1,0:T(8,128)(2,1)} %fusion.61), channel_id=1, source_target_pairs={{0,2},{2,0},{1,3},{3,1},{4,6},{6,4},{5,7},{7,5},{8,10},{10,8},{9,1... | collective-permute-start | bytes 1966088 | tf_op jit(solution)/shard_map/ppermute | solution.py:19
  (208 other events, 3316.2 us)

commit v2 on v1

--- a/solution.py
+++ b/solution.py
@@ -9,7 +9,6 @@
 
 HEADS = 10
 CONV = 4
-RING = (0, 1, 3, 2)
 F32 = jnp.float32
 BF16 = jnp.bfloat16
 PAIR = ((0, 1), (1, 0))
@@ -33,50 +32,41 @@
     return lax.dynamic_index_in_dim(array, index, axis, keepdims=False)
 
 
-def z_ring():
-    return lax.axis_size("z") == len(RING)
-
-
-def z_at(j):
-    if not z_ring():
-        return jnp.int32(j)
-    here = pick(jnp.array(RING, jnp.int32), lax.axis_index("z"), 0)
-    return pick(jnp.array(RING, jnp.int32), (here - j) % len(RING), 0)
-
-
-def z_place(z):
-    if not z_ring():
-        return jnp.int32(z)
-    table = jnp.array(RING, jnp.int32)
-    return (pick(table, lax.axis_index("z"), 0) - RING[z]) % len(RING)
-
-
-def z_next(value):
-    count = len(RING)
-    return lax.ppermute(value, "z", [(RING[p], RING[(p + 1) % count]) for p in range(count)])
+def z_direct():
+    return lax.axis_size("z") == 4
+
+
+def z_send(value, j):
+    count = lax.axis_size("z")
+    return lax.ppermute(value, "z", [(s, s ^ j) for s in range(count)])
+
+
+def place(pieces, size):
+    rows = pieces[0][1].shape[0]
+    full = jnp.zeros((size * rows,) + pieces[0][1].shape[1:], pieces[0][1].dtype)
+    for at, piece in pieces:
+        full = lax.dynamic_update_slice_in_dim(full, piece, at * rows, 0)
+    return full
 
 
 def z_gather(shard):
-    if not z_ring():
-        everything = lax.all_gather(shard, "z")
-        return [everything[j] for j in range(lax.axis_size("z"))]
-    shards = [shard]
-    for _ in range(len(RING) - 1):
-        shards.append(z_next(shards[-1]))
-    return shards
+    count = lax.axis_size("z")
+    if not z_direct():
+        return lax.all_gather(shard, "z", axis=0, tiled=True)
+    z = lax.axis_index("z")
+    pieces = [(z, shard)] + [(z ^ j, z_send(shard, j)) for j in range(1, count)]
+    return place(pieces, count)
 
 
 def z_scatter(part):
     count = lax.axis_size("z")
-    if not z_ring():
-        stacked = jnp.stack([low(part(j)) for j in range(count)])
-        return lax.psum_scatter(stacked, "z", scatter_dimension=0).astype(F32)
-    total = None
-    for j in list(range(1, count)) + [0]:
-        term = part(j)
-        if total is not None:
-            term = term + total.astype(F32)
-        total = z_next(low(term)) if j else term
+    if not z_direct():
+        return lax.psum_scatter(low(part), "z", scatter_dimension=0, tiled=True).astype(F32)
+    z, rows = lax.axis_index("z"), part.shape[0] // count
+    total = lax.dynamic_slice_in_dim(part, z * rows, rows, 0)
+    for j in range(1, count):
+        block = lax.dynamic_slice_in_dim(part, (z ^ j) * rows, rows, 0)
+        total = total + z_send(low(block), j).astype(F32)
     return total
 
 
@@ -90,7 +80,7 @@
 def z_carry(decay, state, step):
     count = lax.axis_size("z")
     pair = jnp.stack([decay, state])
-    if z_ring():
+    if z_direct():
         near = [z_shift(pair, step * k) for k in range(1, count)]
         carry = near[-1][1]
         for got in near[-2::-1]:
@@ -126,88 +116,49 @@
     return own + swap(low(to_x), "x").astype(F32) + swap(low(to_y), "y").astype(F32)
 
 
-def fine_gather(shard, first, second):
-    shards = z_gather(shard)
-    near = [swap(s, first) for s in shards]
-    far = [swap(s, second) for s in shards]
-    both = [swap(s, second) for s in near]
+def fine_order(values):
+    count = lax.axis_size("z")
+    blocks = values.reshape(values.shape[0], count, 2, 2, -1)
+    return jnp.transpose(blocks, (0, 3, 2, 1, 4)).reshape(values.shape)
+
+
+def fine_back(values):
+    count = lax.axis_size("z")
+    blocks = values.reshape(values.shape[0], 2, 2, count, -1)
+    return jnp.transpose(blocks, (0, 3, 2, 1, 4)).reshape(values.shape)
+
+
+def fine_gather(own, first, second):
+    x, y = lax.axis_index("x"), lax.axis_index("y")
+    far = swap(own, second)
+    near = swap(own, first)
+    both = swap(near, second)
     over_y, over_x = (near, far) if first == "y" else (far, near)
-    return jnp.concatenate(shards + over_y + over_x + both)
-
-
-def fine_scatter(full, first, second):
-    count = lax.axis_size("z")
-    blocks = full.reshape((2, 2, count, -1) + full.shape[1:])
-
-    def part(j):
-        def block(on_first, on_second):
-            over_x, over_y = (on_second, on_first) if second == "x" else (on_first, on_second)
-            return blocks[over_x, over_y, j]
-
-        sent = swap(low(block(1, 1)), second).astype(F32)
-        near = swap(low(block(1, 0) + sent), first).astype(F32)
-        return block(0, 0) + swap(low(block(0, 1)), second).astype(F32) + near
-
-    return z_scatter(part)
-
-
-def fine_chips():
-    y, x = lax.axis_index("y"), lax.axis_index("x")
-    count = lax.axis_size("z")
-    return [
-        (z_at(j) * 2 + (y ^ over_y)) * 2 + (x ^ over_x)
-        for over_x in (0, 1)
-        for over_y in (0, 1)
-        for j in range(count)
-    ]
-
-
-def fine_places():
-    y, x = lax.axis_index("y"), lax.axis_index("x")
-    count = lax.axis_size("z")
-    return [
-        ((x ^ at_x) * 2 + (y ^ at_y)) * count + z_place(z)
-        for z in range(count)
-        for at_y in (0, 1)
-        for at_x in (0, 1)
-    ]
-
-
-def columns(values, places):
-    width = values.shape[-1] // len(places)
-    return jnp.concatenate(
-        [lax.dynamic_slice_in_dim(values, at * width, width, values.ndim - 1) for at in places],
-        axis=-1,
-    )
-
-
-def whole_gather(shard, first, second):
-    shards = jnp.stack(z_gather(shard))
-    count = lax.axis_size("z")
-    if z_ring():
-        shards = jnp.stack([pick(shards, z_place(z), 0) for z in range(count)])
-    at = {"y": lax.axis_index("y"), "x": lax.axis_index("x")}
-    near = swap(shards, first)
-    held = jnp.stack([shards, near], 1)
-    far = swap(held, second)
-    both = jnp.where(at[first] == 0, held, held[:, ::-1])
-    far = jnp.where(at[first] == 0, far, far[:, ::-1])
-    full = jnp.where(at[second] == 0, jnp.stack([both, far], 2), jnp.stack([far, both], 2))
-    if first == "x":
-        full = jnp.swapaxes(full, 1, 2)
-    return full.reshape((-1,) + shard.shape[1:])
-
-
-def whole_scatter(full, first, second):
-    count = lax.axis_size("z")
-    blocks = full.reshape((count, 2, 2, -1) + full.shape[1:])
-    places = {"y": 1, "x": 2}
-    for axis in (second, first):
-        at, dim = lax.axis_index(axis), places.pop(axis)
-        dim = min(dim, blocks.ndim - full.ndim - 1)
-        sent = swap(low(pick(blocks, 1 - at, dim)), axis)
-        blocks = pick(blocks, at, dim) + sent.astype(F32)
-    return z_scatter(lambda j: pick(blocks, z_at(j), 0))
+    return place(
+        [
+            (2 * x + y, own),
+            (2 * x + (1 - y), over_y),
+            (2 * (1 - x) + y, over_x),
+            (2 * (1 - x) + (1 - y), both),
+        ],
+        4,
+    )
+
+
+def fine_near(part, first, second):
+    x, y = lax.axis_index("x"), lax.axis_index("y")
+
+    def block(on_first, on_second):
+        over_x, over_y = (on_second, on_first) if second == "x" else (on_first, on_second)
+        return part(2 * (x ^ over_x) + (y ^ over_y))
+
+    corner = swap(low(block(1, 1)), second)
+    far = swap(low(block(0, 1)), second)
+    return block, corner, far, lambda got: swap(low(block(1, 0) + got.astype(F32)), first)
+
+
+def fine_total(block, far, near):
+    return block(0, 0) + far.astype(F32) + near.astype(F32)
 
 
 def to_halves(count):
@@ -215,6 +166,7 @@
 
 
 EVERY = ("z", "y", "x", "c")
+CHIPS = ("z", "y", "x")
 
 
 def expm1_neg(value):
@@ -352,6 +304,7 @@
     seqs, length, full = rec.shape
     heads = HEADS // 2
     width = full // heads
+    column = (gates.shape[1] - 640) // width
     block = pl.BlockSpec((seqs, length, width), lambda h: (0, 0, h))
     whole = pl.BlockSpec((seqs, length, full), lambda h: (0, 0, 0))
     array = jax.ShapeDtypeStruct(rec.shape, F32)
@@ -362,8 +315,8 @@
             block,
             pl.BlockSpec((seqs, 8, width), lambda h: (0, 0, h)),
             pl.BlockSpec((8, width), lambda h: (0, h)),
-            pl.BlockSpec((width, width), lambda h: (h, 0)),
-            pl.BlockSpec((width, width), lambda h: (h, 1)),
+            pl.BlockSpec((width, width), lambda h: (h, column)),
+            pl.BlockSpec((width, width), lambda h: (h, column + 1)),
         ],
         out_specs=[block, block, block, whole, whole, whole],
         out_shape=[array] * 6,
@@ -388,6 +341,7 @@
     seqs, length, full = rec.shape
     heads = HEADS // 2
     width = full // heads
+    column = (gates.shape[1] - 640) // width
     block = pl.BlockSpec((seqs, length, width), lambda h: (0, 0, h))
     row = pl.BlockSpec((seqs, width), lambda h: (0, h))
     weight = pl.BlockSpec((width, width), lambda h: (h, 0))
@@ -407,8 +361,8 @@
             block,
             pl.BlockSpec((seqs, 8, width), lambda h: (0, 0, h)),
             pl.BlockSpec((8, width), lambda h: (0, h)),
-            weight,
-            pl.BlockSpec((width, width), lambda h: (h, 1)),
+            pl.BlockSpec((width, width), lambda h: (h, column)),
+            pl.BlockSpec((width, width), lambda h: (h, column + 1)),
         ],
         out_specs=[block, weight, weight, pl.BlockSpec((8, width), lambda h: (0, h))],
         out_shape=[
@@ -469,8 +423,6 @@
     half_tokens, width = block_input.shape[1:]
     length = 2 * half_tokens
     channels = w_branch.shape[1] // 2
-    z_places = [z_at(j) for j in range(z_count)]
-    z_back = [z_place(j) for j in range(z_count)]
 
     def own_sequence(block):
         return ordered(first_y, pick(block, y, 0), swap(pick(block, 1 - y, 0), "y"), 0)
@@ -484,6 +436,13 @@
         parts = weight.reshape(weight.shape[0], 2, channels)
         return ordered(first_c, pick(parts, c, 1), swap(pick(parts, 1 - c, 1), "c"), 0)
 
+    branch_shard, recur_in_shard = core_columns(w_branch), core_columns(w_recur_in)
+    (
+        branch_shard, recur_in_shard, w_recur_out, w_rgate, w_gate, w_up, w_down, norm_gain
+    ) = lax.optimization_barrier(
+        (branch_shard, recur_in_shard, w_recur_out, w_rgate, w_gate, w_up, w_down, norm_gain)
+    )
+
     gains = jnp.stack([norm_gain, mlp_gain]).reshape(1, -1)
     gains = lax.all_to_all(jnp.tile(gains, (devices, 1)), EVERY, 0, 0, tiled=True)
     gains = jnp.swapaxes(gains.reshape(devices, 2, -1), 0, 1).reshape(2, width).astype(F32)
@@ -493,44 +452,38 @@
         [conv_weight, conv_bias[None], rgate_bias[None], igate_bias[None], rate_param[None]]
     )
     vectors = jnp.pad(vectors.T, ((0, 0), (0, 120)))
-    gate_shard = jnp.concatenate([w_rgate, w_igate, vectors], axis=1)
-    gate_shard = lax.ppermute(gate_shard, EVERY, to_halves(devices))
-    gates = whole_gather(gate_shard, "y", "x")
-    branch_full = fine_gather(core_columns(w_branch), "y", "x")
-    recur_in_full = fine_gather(core_columns(w_recur_in), "x", "y")
-    out_shard = lax.ppermute(w_recur_out, EVERY, to_halves(devices))
-    out_full = jnp.concatenate(
-        [
-            whole_gather(out_shard[:, : width // 2], "y", "x"),
-            whole_gather(out_shard[:, width // 2 :], "x", "y"),
-        ],
-        axis=1,
-    )
+    out_gates = jnp.concatenate([w_recur_out, w_rgate, w_igate, vectors], axis=1)
+    out_gates = lax.ppermute(out_gates, EVERY, to_halves(devices))
+    out_gates = lax.all_gather(out_gates, CHIPS, axis=0, tiled=True)
+    out_full = out_gates[:, :width]
+    branch_full = fine_gather(z_gather(branch_shard), "y", "x")
+    recur_in_full = fine_gather(z_gather(recur_in_shard), "x", "y")
 
     units = w_gate.shape[1] // 2
     gate_up = jnp.stack([w_gate, w_up], 1).reshape(w_gate.shape[0], 2, 2, units)
     mine = pick(gate_up, y, 2).reshape(-1, 2 * units)
     theirs = swap(pick(gate_up, 1 - y, 2).reshape(-1, 2 * units), "y")
-    gate_up_full = jnp.concatenate(z_gather(ordered(first_y, mine, theirs, 0)))
+    gate_up_shard = ordered(first_y, mine, theirs, 0)
+    gate_up_full = lax.all_gather(gate_up_shard, "z", axis=0, tiled=True)
     down = w_down.reshape(2, units, -1)
     down_shard = ordered(first_y, pick(down, y, 0), swap(pick(down, 1 - y, 0), "y"), 1)
-    down_full = jnp.concatenate(z_gather(down_shard), axis=1)
-
-    vec = gates[:, 512:520].T.astype(F32)
+    down_full = lax.all_gather(down_shard, "z", axis=0)
+    down_full = jnp.swapaxes(down_full, 0, 1).reshape(units, width)
+
+    vec = out_gates[:, width + 512 : width + 520].T.astype(F32)
     rate = vec[7]
     eight = -8.0 * jax.nn.softplus(rate)
     vec = jnp.concatenate([vec[:7], eight[None]])
 
     rows_in = own_sequence(block_input).astype(F32)
     normed_f, norm_pull = jax.vjp(rms_scale, rows_in, ngain)
-    chips, places = fine_chips(), fine_places()
-    normed = columns(low(normed_f), chips)
+    normed = fine_order(low(normed_f))
     normed = jnp.concatenate([normed, swap(normed, "c")])
     branch_pre = mm(normed, branch_full)
     recur_pre = mm(normed, recur_in_full).reshape(2, length, channels)
     branch_act, gelu_pull = jax.vjp(partial(jax.nn.gelu, approximate=True), branch_pre)
     halo = z_shift(recur_pre[:, length - 8 :], 1)
-    conv, sig_r, sig_i, decay, state, prod = run_forward(recur_pre, halo, vec, gates)
+    conv, sig_r, sig_i, decay, state, prod = run_forward(recur_pre, halo, vec, out_gates)
     carry = z_carry(prod[:, -1], state[:, -1], 1)
     states = (state + prod * carry[:, None]).reshape(2 * length, channels)
     mixed_low = low(states * branch_act)
@@ -538,32 +491,30 @@
     middle = rows_in + recur_out[:length] + swap(recur_out[length:], "c")
 
     normed2_f, norm2_pull = jax.vjp(rms_scale, middle, mgain)
-    tokens_all = group_gather(columns(low(normed2_f), z_places))
+    tokens_all = group_gather(low(normed2_f))
     pre = mm(tokens_all, gate_up_full)
     hidden_f, mlp_pull = jax.vjp(mlp_act, pre[:, :units], pre[:, units:])
     hidden = low(hidden_f)
-    mlp_out = columns(group_scatter(mm(hidden, down_full)), z_back)
+    mlp_out = group_scatter(mm(hidden, down_full))
     block_output = own_tokens(low(middle + mlp_out))
 
     own_grad = own_sequence(cotangent)
-    grad_all = group_gather(columns(own_grad, z_places))
+    grad_all = group_gather(own_grad)
     grad_hidden = mm_rows(grad_all, down_full)
     grad_pre = jnp.concatenate([low(g) for g in mlp_pull(grad_hidden)], axis=1)
-    grad_normed2 = columns(group_scatter(mm_rows(grad_pre, gate_up_full)), z_back)
+    grad_normed2 = group_scatter(mm_rows(grad_pre, gate_up_full))
     block = width // z_count
-    grad_gate_up = z_scatter(
-        lambda j: outer_sum(tokens_all[:, j * block : (j + 1) * block], grad_pre)
-    )
-    grad_down = z_scatter(lambda j: outer_sum(hidden, grad_all[:, j * block : (j + 1) * block]))
+    grad_gate_up = lax.psum_scatter(
+        low(outer_sum(tokens_all, grad_pre)), "z", scatter_dimension=0, tiled=True
+    ).astype(F32)
+    grad_down = lax.psum_scatter(
+        low(outer_sum(grad_all, hidden)), "z", scatter_dimension=0, tiled=True
+    ).astype(F32)
     grad_gate_up = grad_gate_up.reshape(2, block // 2, 2 * units)
-    kept, other = pick(grad_gate_up, y, 0), swap(low(pick(grad_gate_up, 1 - y, 0)), "y")
-    kept = kept.reshape(-1, 2, 1, units)
-    other = other.astype(F32).reshape(-1, 2, 1, units)
-    both = ordered(first_y, kept, other, 2).reshape(-1, 2, 2 * units)
-    grad_gate, grad_up = both[:, 0], both[:, 1]
-    grad_down = grad_down.reshape(units, 2, -1)
-    kept, other = pick(grad_down, y, 1), swap(low(pick(grad_down, 1 - y, 1)), "y")
-    grad_down = ordered(first_y, kept, other.astype(F32), 0)
+    gate_up_kept = pick(grad_gate_up, y, 0).reshape(-1, 2, 1, units)
+    gate_up_other = swap(low(pick(grad_gate_up, 1 - y, 0)), "y")
+    grad_down = grad_down.reshape(2, -1, units)
+    down_kept, down_other = pick(grad_down, y, 0), swap(low(pick(grad_down, 1 - y, 0)), "y")
 
     grad_middle_norm, grad_mgain = norm2_pull(grad_normed2)
     grad_middle = own_grad.astype(F32) + grad_middle_norm
@@ -575,42 +526,65 @@
     local, ahead, sent = run_reverse(decay, grad_states)
     entering = z_carry(prod[:, -1], sent, -1)
     grad_conv, grad_rgate, grad_igate, small = run_backward(
-        local, ahead, entering, state, prod, carry, conv, sig_r, sig_i, recur_pre, halo, vec, gates
-    )
+        local, ahead, entering, state, prod, carry, conv, sig_r, sig_i, recur_pre, halo, vec, out_gates
+    )
+
+    def quarter(grad):
+        def part(at):
+            rows = lax.dynamic_slice_in_dim(normed, at * (width // 4), width // 4, 1)
+            return outer_sum(rows, grad)
+
+        return part
+
+    block, corner, far, onward = fine_near(quarter(grad_branch_low), "y", "x")
+    grad_conv, corner = lax.optimization_barrier((grad_conv, corner))
+    near = onward(corner)
     rim = z_shift(grad_conv[:, :8], -1)
     grad_ext = jnp.concatenate([grad_conv, rim], axis=1)
     grad_recur_low = low(sum(vec[k] * grad_ext[:, k : k + length] for k in range(CONV)))
     grad_recur_low = grad_recur_low.reshape(2 * length, channels)
+    grad_recur_low, far, near = lax.optimization_barrier((grad_recur_low, far, near))
+    branch_near = fine_total(block, far, near)
     grad_normed = mm_rows(grad_branch_low, branch_full) + mm_rows(grad_recur_low, recur_in_full)
     grad_normed = grad_normed[:length] + swap(grad_normed[length:], "c")
-    grad_rows, grad_ngain = norm_pull(columns(grad_normed, places))
-    input_grad = own_tokens(low(grad_middle + grad_rows))
+    grad_rows, grad_ngain = norm_pull(fine_back(grad_normed))
+    input_rows = low(grad_middle + grad_rows)
 
     def own_rows(chunk):
         parts = chunk.reshape(2, -1, channels)
         return ordered(first_c, pick(parts, c, 0), swap(pick(parts, 1 - c, 0), "c"), 1)
 
     from_halves = [(target, source) for source, target in to_halves(devices)]
-    grad_out_w = outer_sum(mixed_low, grad_out_low)
-    grad_out_w = jnp.concatenate(
-        [
-            whole_scatter(grad_out_w[:, : width // 2], "y", "x"),
-            whole_scatter(grad_out_w[:, width // 2 :], "x", "y"),
-        ],
-        axis=1,
-    )
-    grad_recur_out = lax.ppermute(low(grad_out_w), EVERY, from_halves).astype(F32)
     small = jnp.concatenate([small[:7], (small[7] * -8.0 * jax.nn.sigmoid(rate))[None]])
     small = jnp.pad(small.T, ((0, 0), (0, 120)))
-    gate_grads = jnp.concatenate([grad_rgate, grad_igate, small], axis=1)
-    gate_grads = lax.ppermute(whole_scatter(gate_grads, "y", "x"), EVERY, from_halves)
+    out_grads = [low(g) for g in (outer_sum(mixed_low, grad_out_low), grad_rgate, grad_igate, small)]
+    out_grads = jnp.concatenate(out_grads, axis=1)
+    out_grads = lax.psum_scatter(out_grads, CHIPS, scatter_dimension=0, tiled=True)
+    out_grads = lax.ppermute(out_grads, EVERY, from_halves).astype(F32)
+    grad_recur_out, gate_grads = out_grads[:, :width], out_grads[:, width:]
     small = gate_grads[:, 512:520].T
-    grad_branch = own_rows(fine_scatter(outer_sum(normed, grad_branch_low), "y", "x"))
-    grad_recur_in = own_rows(fine_scatter(outer_sum(normed, grad_recur_low), "x", "y"))
-    gain_grads = jnp.stack([grad_ngain, grad_mgain]).reshape(2, devices, -1)
-    gain_grads = jnp.swapaxes(gain_grads, 0, 1).reshape(devices, -1)
-    gain_grads = lax.all_to_all(gain_grads, EVERY, 0, 0, tiled=True)
-    gain_grads = jnp.sum(gain_grads, axis=0).reshape(2, -1)
+    grad_branch = own_rows(z_scatter(branch_near))
+    block, corner, far, onward = fine_near(quarter(grad_recur_low), "x", "y")
+    recur_in_near = fine_total(block, far, onward(corner))
+    (
+        recur_in_near, gate_up_other, down_other, grad_ngain, grad_mgain, input_rows
+    ) = lax.optimization_barrier(
+        (recur_in_near, gate_up_other, down_other, grad_ngain, grad_mgain, input_rows)
+    )
+    grad_recur_in = own_rows(z_scatter(recur_in_near))
+    input_grad = own_tokens(input_rows)
+    gate_up_other = gate_up_other.astype(F32).reshape(-1, 2, 1, units)
+    both = ordered(first_y, gate_up_kept, gate_up_other, 2).reshape(-1, 2, 2 * units)
+    grad_gate, grad_up = both[:, 0], both[:, 1]
+    grad_down = ordered(first_y, down_kept, down_other.astype(F32), 1).T
+    gain_grads = jnp.stack([grad_ngain, grad_mgain])
+    for axis in ("c", "x", "y"):
+        gain_grads = gain_grads + swap(gain_grads, axis)
+    if z_direct():
+        gain_grads = gain_grads + sum(z_send(gain_grads, j) for j in range(1, z_count))
+    else:
+        gain_grads = lax.psum(gain_grads, "z")
+    gain_grads = pick(gain_grads.reshape(2, devices, -1), lax.axis_index(EVERY), 1)
     return (
         block_output,
         input_grad,

time: 1060 us -> 809 us (0.76)
  waiting for transfers between devices: 499 us -> 375 us
  starting transfers between devices: 198 us -> 106 us
  other arithmetic: 94 us -> 65.9 us
    ppermute x46 -> x17, waiting for transfers between devices: 238 us -> 107 us  [the longest x15 85.3 us: z_send(): return lax.ppermute(value, 'z', [(s, s ^ j) for s in range(count)])]
    ppermute x46 -> x17, starting transfers between devices: 92.4 us -> 30.8 us  [the longest x15 20.5 us: z_send(): return lax.ppermute(value, 'z', [(s, s ^ j) for s in range(count)])]
    all_to_all x1, waiting for transfers between devices: 0.01 us -> 28.7 us  [on_device(): lax.all_to_all(jnp.tile(gains, (devices, 1)), EVERY, 0, 0, tiled=True)]
    dynamic_update_slice x0 -> x16, local copies, waits for them, and re-layouts: none -> 25.7 us  [place(): full = lax.dynamic_update_slice_in_dim(full, piece, at * rows, 0)]
    ppermute x98 -> x53, waiting for transfers between devices: 232 us -> 207 us  [swap(): return lax.ppermute(value, axis, PAIR)]
    all_to_all x1 -> x0, waiting for transfers between devices: 24.9 us -> none  [on_device(): gain_grads = lax.all_to_all(gain_grads, EVERY, 0, 0, tiled=True)]
    unnamed x286 -> x177, local copies, waits for them, and re-layouts: 56.2 us -> 32.1 us
    ppermute x98 -> x53, starting transfers between devices: 71.5 us -> 52 us  [swap(): return lax.ppermute(value, axis, PAIR)]
  transfers between devices with their start and end apart: 154 -> 85, of which waited for: 72 -> 38; matrix products, arithmetic and copies ran while one was open for 27% -> 29% of each run, Pallas kernels for 2% -> 3%
where the time goes in v2:
time: 809 us; the launch traced here: 797 us
  waiting for transfers between devices  375 us (46%)
  local copies, waits for them, and re-layouts  119 us (15%)
  starting transfers between devices  106 us (13%)
  matrix products  90.6 us (11%)
  other arithmetic  65.9 us (8%)
  Pallas kernels  24.1 us (3%)
  between operations  16.1 us (2%)
    ppermute x53, waiting for transfers between devices, swap(): return lax.ppermute(value, axis, PAIR)  207 us
    ppermute x15, waiting for transfers between devices, z_send(): return lax.ppermute(value, 'z', [(s, s ^ j) for s in range(count)])  85.3 us
    ppermute x53, starting transfers between devices, swap(): return lax.ppermute(value, axis, PAIR)  52 us
    dot_general x11, matrix products, outer_sum(): lax.dot_general(left, right, (((0,), (0,)), ((), ())), preferred_element_...  36.7 us
    unnamed x177, local copies, waits for them, and re-layouts  32.1 us
    dot_general x5, matrix products, mm_rows(): lax.dot_general(left, weight, (((1,), (1,)), ((), ())), preferred_element...  31.3 us
    all_to_all x1, waiting for transfers between devices, on_device(): lax.all_to_all(jnp.tile(gains, (devices, 1)), EVERY, 0, 0, tiled=True)  28.7 us
    dynamic_update_slice x16, local copies, waits for them, and re-layouts, place(): full = lax.dynamic_update_slice_in_dim(full, piece, at * rows, 0)  25.7 us
  transfers between devices with their start and end apart: 85, of which 38 were waited for; matrix products, arithmetic and copies ran while one was open for 29% of the time, Pallas kernels for 3%

profile of v2, /device:TPU:10, one launch (start us, length us, event | category | flops | bytes accessed | tf_op | source)
XLA Modules:
  0.0 797.2 jit_solution(2819200812041073805)
XLA Ops:
  12.7 4.5 collective-permute-start.11
  17.2 11.6 %collective-permute-done.11 = bf16[80,2688]{1,0:T(8,128)(2,1)} collective-permute-done((bf16[80,2688]{1,0:T(8,128)(2,1)S(1)}, bf16[80,2688]{1,0:T(8,128)(2,1)}, u32[]{:S(2)}, u32[]{:S(2)}) %collective-permute-start.11) | collective-permute-done | bytes 430112 | tf_op jit(solution)/shard_map/ppermute | solution.py:456
  29.7 11.0 %collective-permute-done.29 = bf16[768,256]{1,0:T(8,128)(2,1)S(1)} collective-permute-done((bf16[768,256]{1,0:T(8,128)(2,1)}, bf16[768,256]{1,0:T(8,128)(2,1)S(1)}, u32[]{:S(2)}, u32[]{:S(2)}) %collective-permute-start.29) | collective-permute-done | bytes 393248 | tf_op jit(solution)/shard_map/ppermute | solution.py:18
  50.5 6.9 all-to-all-start
  63.4 28.7 %all-to-all-done = bf16[32,1,128]{2,1,0:T(2,128)(2,1)S(1)} async-done(((bf16[32,1,128]{2,1,0:T(2,128)(2,1)}), bf16[32,1,128]{2,1,0:T(2,128)(2,1)S(1)}, u32[]{:S(2)}, u32[]{:S(2)}) %all-to-all-start) | async-done | bytes 8224 | tf_op jit(solution)/shard_map/all_to_all | solution.py:447
  94.6 5.7 fusion.57
  100.3 3.8 collective-permute-start.16
  113.1 6.2 collective-permute-done.15
  121.9 16.7 %collective-permute-done.16 = bf16[128,1280]{1,0:T(8,128)(2,1)} collective-permute-done((bf16[128,1280]{1,0:T(8,128)(2,1)S(1)}, bf16[128,1280]{1,0:T(8,128)(2,1)}, u32[]{:S(2)}, u32[]{:S(2)}) %collective-permute-start.16) | collective-permute-done | bytes 327712 | tf_op jit(solution)/shard_map/ppermute | solution.py:41
  152.2 8.1 %collective-permute-done.8 = bf16[512,1280]{1,0:T(8,128)(2,1)} collective-permute-done((bf16[512,1280]{1,0:T(8,128)(2,1)S(1)}, bf16[512,1280]{1,0:T(8,128)(2,1)}, u32[]{:S(2)}, u32[]{:S(2)}) %collective-permute-start.8) | collective-permute-done | bytes 1310752 | tf_op jit(solution)/shard_map/ppermute | solution.py:18
  163.7 16.0 %collective-permute-done.7 = bf16[512,1280]{1,0:T(8,128)(2,1)} collective-permute-done((bf16[512,1280]{1,0:T(8,128)(2,1)S(1)}, bf16[512,1280]{1,0:T(8,128)(2,1)}, u32[]{:S(2)}, u32[]{:S(2)}) %collective-permute-start.7) | collective-permute-done | bytes 1310752 | tf_op jit(solution)/shard_map/ppermute | solution.py:18
  185.8 22.0 %collective-permute-done.18 = bf16[512,1280]{1,0:T(8,128)(2,1)} collective-permute-done((bf16[512,1280]{1,0:T(8,128)(2,1)}, bf16[512,1280]{1,0:T(8,128)(2,1)}, u32[]{:S(2)}, u32[]{:S(2)}) %collective-permute-start.18) | collective-permute-done | bytes 1310752 | tf_op jit(solution)/shard_map/ppermute | solution.py:18
  213.9 31.5 %collective-permute-done.9 = bf16[512,1280]{1,0:T(8,128)(2,1)} collective-permute-done((bf16[512,1280]{1,0:T(8,128)(2,1)}, bf16[512,1280]{1,0:T(8,128)(2,1)}, u32[]{:S(2)}, u32[]{:S(2)}) %collective-permute-start.9) | collective-permute-done | bytes 1310752 | tf_op jit(solution)/shard_map/ppermute | solution.py:18
  260.1 9.7 %recur_forward.1 = (f32[2,128,1280]{2,1,0:T(8,128)}, f32[2,128,1280]{2,1,0:T(8,128)}, f32[2,128,1280]{2,1,0:T(8,128)}, f32[2,128,1280]{2,1,0:T(8,128)}, f32[2,12...) custom-call(f32[2,128,1280]{2,1,0:T(8,128)} %bitcast.172, f32[2,8,1280]{2,1,0:T(8,128)} %collective-permute-done.10.halo_ref, ...), custom_call_target="tpu_custom_call" | custom-call | flops 335544320 | bytes 9175040 | tf_op jit(solution)/shard_map/recur_forward/pallas_call | solution.py:311
  283.5 5.9 fusion.30
  297.5 5.5 collective-permute-done.40
  315.5 7.5 collective-permute-done.23
  335.7 5.0 copy.139
  348.9 15.8 %all-gather.6.cloned.1.call-done = bf16[2048,1536]{0,1:T(8,128)(2,1)} async-done(((bf16[512,1536]{0,1:T(8,128)(2,1)}), bf16[2048,1536]{0,1:T(8,128)(2,1)}) %all-gather.6.cloned.1.call-update) | async-done | bytes 6291472 | tf_op jit(solution)/shard_map/all_gather | solution.py:467
  364.7 10.2 %fusion.98 = f32[1024,1536]{1,0:T(8,128)S(1)} fusion(bf16[1024,2048]{1,0:T(8,128)(2,1)} %constant_dynamic-update-slice_fusion, bf16[2048,1536]{0,1:T(8,128)(2,1)} %all-gather.6.cloned.1.call-done), kind=kOutput, calls=%fused_computation.276 | convolution fusion | flops 6442450944 | bytes 16777216 | tf_op jit(solution)/shard_map/dot_general | solution.py:389
  375.0 8.9 %fusion.14 = (bf16[1024,768]{1,0:T(8,128)(2,1)}, bf16[1024,768]{1,0:T(8,128)(2,1)}, bf16[1024,768]{1,0:T(8,128)(2,1)S(1)}) fusion(f32[1024,1536]{1,0:T(8,128)S(1)} %fusion.98, bf16[1024,2048]{1,0:T(8,128)(2,1)} %constant_dynamic-update-slice_fusion.7, bf16[768,2048]{0,1:T(8,128)(2,1)S(1)} %bitcast.177), kind=kOutput, calls=%fused_computation.28 | convolution fusion | flops 3241672704 | bytes 18350080 | tf_op jit(solution)/shard_map/dot_general | solution.py:393
  385.0 7.4 convolution_convert_fusion.2
  392.6 11.2 %convolution_convert_fusion.1 = bf16[2048,1536]{1,0:T(8,128)(2,1)} fusion(bf16[1024,2048]{1,0:T(8,128)(2,1)} %constant_dynamic-update-slice_fusion, bf16[1024,768]{1,0:T(8,128)(2,1)} %get-tuple-element.195, bf16[1024,768]{1,0:T(8,128)(2,1)} %get-tuple-element.194), kind=kOutput, calls=%fused_computation.3 | convolution fusion | flops 6451888128 | bytes 13631488 | tf_op jit(solution)/shard_map/dot_general | solution.py:397
  403.9 10.0 %fusion.17 = f32[1024,2048]{1,0:T(8,128)S(1)} fusion(bf16[2048,1536]{0,1:T(8,128)(2,1)} %all-gather.6.cloned.1.call-done, bf16[1024,768]{1,0:T(8,128)(2,1)} %get-tuple-element.195, bf16[1024,768]{1,0:T(8,128)(2,1)} %get-tuple-element.194), kind=kOutput, calls=%fused_computation.41 | convolution fusion | flops 6448742400 | bytes 17825792 | tf_op jit(solution)/shard_map/dot_general | solution.py:393
  441.1 8.1 %collective-permute-done.47 = bf16[128,2048]{1,0:T(8,128)(2,1)S(1)} collective-permute-done((bf16[128,2048]{1,0:T(8,128)(2,1)S(1)}, bf16[128,2048]{1,0:T(8,128)(2,1)S(1)}, u32[]{:S(2)}, u32[]{:S(2)}) %collective-permute-start.47) | collective-permute-done | bytes 524320 | tf_op jit(solution)/shard_map/ppermute | solution.py:18
  449.7 9.6 %collective-permute-done.34 = bf16[128,2048]{1,0:T(8,128)(2,1)S(1)} collective-permute-done((bf16[128,2048]{1,0:T(8,128)(2,1)S(1)}, bf16[128,2048]{1,0:T(8,128)(2,1)S(1)}, u32[]{:S(2)}, u32[]{:S(2)}) %collective-permute-start.34) | collective-permute-done | bytes 524320 | tf_op jit(solution)/shard_map/ppermute | solution.py:18
  465.3 6.8 fusion.25
  472.0 5.1 recur_reverse.1
  479.8 5.2 collective-permute-start.49
  485.0 4.9 convolution_convert_fusion
  490.5 9.3 %recur_backward.1 = (f32[2,128,1280]{2,1,0:T(8,128)}, f32[1280,256]{1,0:T(8,128)}, f32[1280,256]{1,0:T(8,128)}, f32[8,1280]{1,0:T(8,128)}) custom-call(f32[2,128,1280]{2,1,0:T(8,128)} %get-tuple-element.60.l_ref, f32[2,128,1280]{2,1,0:T(8,128)} %get-tuple-element.61.q_ref, f32[2,1280]{1,0:T(2,128)} %fusion.70.e_ref, ...), custom_call_target="tpu_custom_call" | custom-call | flops 671088640 | bytes 13107200 | tf_op jit(solution)/shard_map/recur_backward/pallas_call | solution.py:348
  505.3 5.8 fusion.1
  517.7 26.9 %collective-permute-done.52 = bf16[512,1280]{1,0:T(8,128)(2,1)S(1)} collective-permute-done((bf16[512,1280]{1,0:T(8,128)(2,1)}, bf16[512,1280]{1,0:T(8,128)(2,1)S(1)}, u32[]{:S(2)}, u32[]{:S(2)}) %collective-permute-start.52) | collective-permute-done | bytes 1310752 | tf_op jit(solution)/shard_map/ppermute | solution.py:18
  549.6 9.4 %collective-permute-done.53 = f32[2,8,1280]{2,1,0:T(8,128)S(1)} collective-permute-done((f32[2,8,1280]{2,1,0:T(8,128)S(1)}, f32[2,8,1280]{2,1,0:T(8,128)S(1)}, u32[]{:S(2)}, u32[]{:S(2)}) %collective-permute-start.53) | collective-permute-done | bytes 81952 | tf_op jit(solution)/shard_map/ppermute | solution.py:75
  559.6 11.8 %collective-permute-done.54 = bf16[512,1280]{1,0:T(8,128)(2,1)S(1)} collective-permute-done((bf16[512,1280]{1,0:T(8,128)(2,1)S(1)}, bf16[512,1280]{1,0:T(8,128)(2,1)S(1)}, u32[]{:S(2)}, u32[]{:S(2)}) %collective-permute-start.54) | collective-permute-done | bytes 1310752 | tf_op jit(solution)/shard_map/ppermute | solution.py:18
  580.3 4.1 convolution_add_fusion.4
  588.6 20.0 %collective-permute-done.65 = bf16[128,1280]{1,0:T(8,128)(2,1)S(1)} collective-permute-done((bf16[128,1280]{1,0:T(8,128)(2,1)S(1)}, bf16[128,1280]{1,0:T(8,128)(2,1)S(1)}, u32[]{:S(2)}, u32[]{:S(2)}) %collective-permute-start.65) | collective-permute-done | bytes 327712 | tf_op jit(solution)/shard_map/ppermute | solution.py:41
  608.6 8.9 %collective-permute-done.64 = bf16[128,1280]{1,0:T(8,128)(2,1)S(1)} collective-permute-done((bf16[128,1280]{1,0:T(8,128)(2,1)S(1)}, bf16[128,1280]{1,0:T(8,128)(2,1)S(1)}, u32[]{:S(2)}, u32[]{:S(2)}) %collective-permute-start.64) | collective-permute-done | bytes 327712 | tf_op jit(solution)/shard_map/ppermute | solution.py:41
  620.0 3.7 collective-permute-start.56
  643.7 3.6 collective-permute-start.58
  654.9 7.7 collective-permute-done.56
  662.6 24.8 %collective-permute-done.58 = bf16[512,1280]{1,0:T(8,128)(2,1)} collective-permute-done((bf16[512,1280]{1,0:T(8,128)(2,1)}, bf16[512,1280]{1,0:T(8,128)(2,1)}, u32[]{:S(2)}, u32[]{:S(2)}) %collective-permute-start.58) | collective-permute-done | bytes 1310752 | tf_op jit(solution)/shard_map/ppermute | solution.py:18
  687.4 4.0 fusion.7
  728.4 22.4 %collective-permute-done.69 = bf16[128,1280]{1,0:T(8,128)(2,1)} collective-permute-done((bf16[128,1280]{1,0:T(8,128)(2,1)}, bf16[128,1280]{1,0:T(8,128)(2,1)}, u32[]{:S(2)}, u32[]{:S(2)}) %collective-permute-start.69) | collective-permute-done | bytes 327712 | tf_op jit(solution)/shard_map/ppermute | solution.py:41
  750.8 10.9 %collective-permute-done.68 = bf16[128,1280]{1,0:T(8,128)(2,1)} collective-permute-done((bf16[128,1280]{1,0:T(8,128)(2,1)}, bf16[128,1280]{1,0:T(8,128)(2,1)}, u32[]{:S(2)}, u32[]{:S(2)}) %collective-permute-start.68) | collective-permute-done | bytes 327712 | tf_op jit(solution)/shard_map/ppermute | solution.py:41
  763.6 4.9 reduce-scatter.8.cloned.1.call-done
  768.6 5.7 collective-permute-start.71
  777.1 9.8 %collective-permute-done.71 = bf16[80,2688]{1,0:T(8,128)(2,1)S(1)} collective-permute-done((bf16[80,2688]{1,0:T(8,128)(2,1)}, bf16[80,2688]{1,0:T(8,128)(2,1)S(1)}, u32[]{:S(2)}, u32[]{:S(2)}) %collective-permute-start.71) | collective-permute-done | bytes 430112 | tf_op jit(solution)/shard_map/ppermute | solution.py:563
  (481 shorter events, 277.6 us)
Async XLA Ops:
  7.2 245.1 %all-gather.4.cloned.1.call-start = ((), (), s32[]{:S(2)}) async-start(), calls=%async_computation.4 | async-start | bytes 7311360 | tf_op jit(solution)/shard_map/all_gather | solution.py:457
  12.7 16.1 %collective-permute-start.11 = (bf16[80,2688]{1,0:T(8,128)(2,1)S(1)}, bf16[80,2688]{1,0:T(8,128)(2,1)}, u32[]{:S(2)}, u32[]{:S(2)}) collective-permute-start(bf16[80,2688]{1,0:T(8,128)(2,1)S(1)} %fusion.58), channel_id=1, source_target_pairs={{0,0},{16,1},{1,2},{17,3},{2,4},{18,5},{3,6},{19,7},{4,8},{20,9},{... | collective-permute-start | bytes 1290248 | tf_op jit(solution)/shard_map/ppermute | solution.py:456
  28.8 306.9 %all-gather.8.cloned.1.call-start = ((), (), s32[]{:S(2)}) async-start(), calls=%async_computation.6 | async-start | bytes 3932160 | tf_op jit(solution)/shard_map/all_gather | solution.py:470
  42.6 50.9 %collective-permute-start = (bf16[64,2048]{1,0:T(8,128)(2,1)}, bf16[64,2048]{1,0:T(8,128)(2,1)S(1)}, u32[]{:S(2)}, u32[]{:S(2)}) collective-permute-start(bf16[64,2048]{1,0:T(8,128)(2,1)} %get-tuple-element.240), channel_id=1, source_target_pairs={{0,4},{4,0},{1,5},{5,1},{2,6},{6,2},{3,7},{7,3},{8,12},{12,8},{9,1... | collective-permute-start | bytes 786440 | tf_op jit(solution)/shard_map/ppermute | solution.py:18
  43.7 64.8 %collective-permute-start.36 = (bf16[64,2048]{1,0:T(8,128)(2,1)}, bf16[64,2048]{1,0:T(8,128)(2,1)}, u32[]{:S(2)}, u32[]{:S(2)}) collective-permute-start(bf16[64,2048]{1,0:T(8,128)(2,1)} %get-tuple-element.236), channel_id=1, source_target_pairs={{0,4},{4,0},{1,5},{5,1},{2,6},{6,2},{3,7},{7,3},{8,12},{12,8},{9,1... | collective-permute-start | bytes 786440 | tf_op jit(solution)/shard_map/ppermute | solution.py:18
  46.3 59.9 %collective-permute-start.6 = (bf16[128,1280]{1,0:T(8,128)(2,1)S(1)}, bf16[128,1280]{1,0:T(8,128)(2,1)}, u32[]{:S(2)}, u32[]{:S(2)}) collective-permute-start(bf16[128,1280]{1,0:T(8,128)(2,1)S(1)} %maximum_select_fusion.11), channel_id=1, source_target_pairs={{0,24},{8,16},{16,8},{24,0},{1,25},{9,17},{17,9},{25,1},{2,26},{10... | collective-permute-start | bytes 983048 | tf_op jit(solution)/shard_map/ppermute | solution.py:41
  47.0 58.1 %collective-permute-start.5 = (bf16[128,1280]{1,0:T(8,128)(2,1)S(1)}, bf16[128,1280]{1,0:T(8,128)(2,1)}, u32[]{:S(2)}, u32[]{:S(2)}) collective-permute-start(bf16[128,1280]{1,0:T(8,128)(2,1)S(1)} %maximum_select_fusion.11), channel_id=1, source_target_pairs={{0,16},{8,24},{16,0},{24,8},{1,17},{9,25},{17,1},{25,9},{2,18},{10... | collective-permute-start | bytes 983048 | tf_op jit(solution)/shard_map/ppermute | solution.py:41
  47.0 53.3 %collective-permute-start.4 = (bf16[128,1280]{1,0:T(8,128)(2,1)S(1)}, bf16[128,1280]{1,0:T(8,128)(2,1)}, u32[]{:S(2)}, u32[]{:S(2)}) collective-permute-start(bf16[128,1280]{1,0:T(8,128)(2,1)S(1)} %maximum_select_fusion.11), channel_id=1, source_target_pairs={{0,8},{8,0},{16,24},{24,16},{1,9},{9,1},{17,25},{25,17},{2,10},{10... | collective-permute-start | bytes 983048 | tf_op jit(solution)/shard_map/ppermute | solution.py:41
  50.5 41.6 %all-to-all-start = ((bf16[32,1,128]{2,1,0:T(2,128)(2,1)}), bf16[32,1,128]{2,1,0:T(2,128)(2,1)S(1)}, u32[]{:S(2)}, u32[]{:S(2)}) async-start(bf16[32,1,128]{2,1,0:T(2,128)(2,1)} %tile.9), calls=%async_computation | async-start | bytes 32768 | tf_op jit(solution)/shard_map/all_to_all | solution.py:447
  57.5 307.3 %all-gather.6.cloned.1.call-start = ((), (), s32[]{:S(2)}) async-start(), calls=%async_computation.5 | async-start | bytes 7864320 | tf_op jit(solution)/shard_map/all_gather | solution.py:467
  93.5 46.8 %collective-permute-start.17 = (bf16[128,1280]{1,0:T(8,128)(2,1)S(1)}, bf16[128,1280]{1,0:T(8,128)(2,1)}, u32[]{:S(2)}, u32[]{:S(2)}) collective-permute-start(bf16[128,1280]{1,0:T(8,128)(2,1)S(1)} %maximum_select_fusion.10), channel_id=1, source_target_pairs={{0,24},{8,16},{16,8},{24,0},{1,25},{9,17},{17,9},{25,1},{2,26},{10... | collective-permute-start | bytes 983048 | tf_op jit(solution)/shard_map/ppermute | solution.py:41
  100.3 38.3 %collective-permute-start.16 = (bf16[128,1280]{1,0:T(8,128)(2,1)S(1)}, bf16[128,1280]{1,0:T(8,128)(2,1)}, u32[]{:S(2)}, u32[]{:S(2)}) collective-permute-start(bf16[128,1280]{1,0:T(8,128)(2,1)S(1)} %maximum_select_fusion.10), channel_id=1, source_target_pairs={{0,16},{8,24},{16,0},{24,8},{1,17},{9,25},{17,1},{25,9},{2,18},{10... | collective-permute-start | bytes 983048 | tf_op jit(solution)/shard_map/ppermute | solution.py:41
  106.2 45.2 %collective-permute-start.28 = (bf16[256,1536]{0,1:T(8,128)(2,1)}, bf16[256,1536]{0,1:T(8,128)(2,1)}, u32[]{:S(2)}, u32[]{:S(2)}) collective-permute-start(bf16[256,1536]{0,1:T(8,128)(2,1)} %bitcast.21), channel_id=1, source_target_pairs={{0,4},{4,0},{1,5},{5,1},{2,6},{6,2},{3,7},{7,3},{8,12},{12,8},{9,1... | collective-permute-start | bytes 2359304 | tf_op jit(solution)/shard_map/ppermute | solution.py:18
  108.5 51.8 %collective-permute-start.8 = (bf16[512,1280]{1,0:T(8,128)(2,1)S(1)}, bf16[512,1280]{1,0:T(8,128)(2,1)}, u32[]{:S(2)}, u32[]{:S(2)}) collective-permute-start(bf16[512,1280]{1,0:T(8,128)(2,1)S(1)} %constant_dynamic-update-slice_fusion.28), channel_id=1, source_target_pairs={{0,2},{2,0},{1,3},{3,1},{4,6},{6,4},{5,7},{7,5},{8,10},{10,8},{9,1... | collective-permute-start | bytes 3932168 | tf_op jit(solution)/shard_map/ppermute | solution.py:18
  119.3 60.3 %collective-permute-start.7 = (bf16[512,1280]{1,0:T(8,128)(2,1)S(1)}, bf16[512,1280]{1,0:T(8,128)(2,1)}, u32[]{:S(2)}, u32[]{:S(2)}) collective-permute-start(bf16[512,1280]{1,0:T(8,128)(2,1)S(1)} %constant_dynamic-update-slice_fusion.28), channel_id=1, source_target_pairs={{0,4},{4,0},{1,5},{5,1},{2,6},{6,2},{3,7},{7,3},{8,12},{12,8},{9,1... | collective-permute-start | bytes 3932168 | tf_op jit(solution)/shard_map/ppermute | solution.py:18
  142.0 68.4 %collective-permute-start.19 = (bf16[512,1280]{1,0:T(8,128)(2,1)}, bf16[512,1280]{1,0:T(8,128)(2,1)}, u32[]{:S(2)}, u32[]{:S(2)}) collective-permute-start(bf16[512,1280]{1,0:T(8,128)(2,1)} %constant_dynamic-update-slice_fusion.20), channel_id=1, source_target_pairs={{0,2},{2,0},{1,3},{3,1},{4,6},{6,4},{5,7},{7,5},{8,10},{10,8},{9,1... | collective-permute-start | bytes 3932168 | tf_op jit(solution)/shard_map/ppermute | solution.py:18
  143.2 64.6 %collective-permute-start.18 = (bf16[512,1280]{1,0:T(8,128)(2,1)}, bf16[512,1280]{1,0:T(8,128)(2,1)}, u32[]{:S(2)}, u32[]{:S(2)}) collective-permute-start(bf16[512,1280]{1,0:T(8,128)(2,1)} %constant_dynamic-update-slice_fusion.20), channel_id=1, source_target_pairs={{0,4},{4,0},{1,5},{5,1},{2,6},{6,2},{3,7},{7,3},{8,12},{12,8},{9,1... | collective-permute-start | bytes 3932168 | tf_op jit(solution)/shard_map/ppermute | solution.py:18
  151.4 141.9 %collective-permute-start.38 = (bf16[128,2048]{1,0:T(8,128)(2,1)}, bf16[128,2048]{1,0:T(8,128)(2,1)}, u32[]{:S(2)}, u32[]{:S(2)}) collective-permute-start(bf16[128,2048]{1,0:T(8,128)(2,1)} %get-tuple-element.185), channel_id=1, source_target_pairs={{0,4},{4,0},{1,5},{5,1},{2,6},{6,2},{3,7},{7,3},{8,12},{12,8},{9,1... | collective-permute-start | bytes 1572872 | tf_op jit(solution)/shard_map/ppermute | solution.py:18
  160.3 85.2 %collective-permute-start.9 = (bf16[512,1280]{1,0:T(8,128)(2,1)}, bf16[512,1280]{1,0:T(8,128)(2,1)}, u32[]{:S(2)}, u32[]{:S(2)}) collective-permute-start(bf16[512,1280]{1,0:T(8,128)(2,1)} %collective-permute-done.8), channel_id=1, source_target_pairs={{0,4},{4,0},{1,5},{5,1},{2,6},{6,2},{3,7},{7,3},{8,12},{12,8},{9,1... | collective-permute-start | bytes 3932168 | tf_op jit(solution)/shard_map/ppermute | solution.py:18
  163.4 460.3 %reduce-scatter.6.cloned.1.call-start = ((), (), s32[]{:S(2)}) async-start(), calls=%async_computation.8 | async-start | bytes 3932160 | tf_op jit(solution)/shard_map/reduce_scatter | solution.py:510
  179.7 115.3 %collective-permute-start.37 = (bf16[128,2048]{1,0:T(8,128)(2,1)}, bf16[128,2048]{1,0:T(8,128)(2,1)}, u32[]{:S(2)}, u32[]{:S(2)}) collective-permute-start(bf16[128,2048]{1,0:T(8,128)(2,1)} %get-tuple-element.185), channel_id=1, source_target_pairs={{0,2},{2,0},{1,3},{3,1},{4,6},{6,4},{5,7},{7,5},{8,10},{10,8},{9,1... | collective-permute-start | bytes 1572872 | tf_op jit(solution)/shard_map/ppermute | solution.py:18
  207.7 39.2 %collective-permute-start.3 = (bf16[128,2048]{0,1:T(8,128)(2,1)S(1)}, bf16[128,2048]{0,1:T(8,128)(2,1)S(1)}, u32[]{:S(2)}, u32[]{:S(2)}) collective-permute-start(bf16[128,2048]{0,1:T(8,128)(2,1)S(1)} %bitcast.148), channel_id=1, source_target_pairs={{0,1},{1,0},{2,3},{3,2},{4,5},{5,4},{6,7},{7,6},{8,9},{9,8},{10,11... | collective-permute-start | bytes 1572872 | tf_op jit(solution)/shard_map/ppermute | solution.py:18
  210.4 65.7 %collective-permute-start.20 = (bf16[512,1280]{1,0:T(8,128)(2,1)}, bf16[512,1280]{1,0:T(8,128)(2,1)}, u32[]{:S(2)}, u32[]{:S(2)}) collective-permute-start(bf16[512,1280]{1,0:T(8,128)(2,1)} %collective-permute-done.18), channel_id=1, source_target_pairs={{0,2},{2,0},{1,3},{3,1},{4,6},{6,4},{5,7},{7,5},{8,10},{10,8},{9,1... | collective-permute-start | bytes 3932168 | tf_op jit(solution)/shard_map/ppermute | solution.py:18
  305.9 28.5 %collective-permute-start.42 = (bf16[384,2048]{1,0:T(8,128)(2,1)S(1)}, bf16[384,2048]{1,0:T(8,128)(2,1)S(1)}, u32[]{:S(2)}, u32[]{:S(2)}) collective-permute-start(bf16[384,2048]{1,0:T(8,128)(2,1)S(1)} %pad_maximum_fusion.5), channel_id=1, source_target_pairs={{0,1},{1,0},{2,3},{3,2},{4,5},{5,4},{6,7},{7,6},{8,9},{9,8},{10,11... | collective-permute-start | bytes 4718600 | tf_op jit(solution)/shard_map/ppermute | solution.py:18
  311.6 21.9 %collective-permute-start.41 = (bf16[128,2048]{1,0:T(8,128)(2,1)}, bf16[128,2048]{1,0:T(8,128)(2,1)S(1)}, u32[]{:S(2)}, u32[]{:S(2)}) collective-permute-start(bf16[128,2048]{1,0:T(8,128)(2,1)} %get-tuple-element.185), channel_id=1, source_target_pairs={{0,1},{1,0},{2,3},{3,2},{4,5},{5,4},{6,7},{7,6},{8,9},{9,8},{10,11... | collective-permute-start | bytes 1572872 | tf_op jit(solution)/shard_map/ppermute | solution.py:18
  392.5 256.9 %reduce-scatter.4.cloned.1.call-start = ((), (), s32[]{:S(2)}) async-start(), calls=%async_computation.7 | async-start | bytes 7864320 | tf_op jit(solution)/shard_map/reduce_scatter | solution.py:507
  403.8 364.8 %reduce-scatter.8.cloned.1.call-start = ((), (), s32[]{:S(2)}) async-start(), calls=%async_computation.9 | async-start | bytes 7311360 | tf_op jit(solution)/shard_map/reduce_scatter | solution.py:562
  431.9 17.4 %collective-permute-start.47 = (bf16[128,2048]{1,0:T(8,128)(2,1)S(1)}, bf16[128,2048]{1,0:T(8,128)(2,1)S(1)}, u32[]{:S(2)}, u32[]{:S(2)}) collective-permute-start(bf16[128,2048]{1,0:T(8,128)(2,1)S(1)} %pad_maximum_fusion.14), channel_id=1, source_target_pairs={{0,4},{4,0},{1,5},{5,1},{2,6},{6,2},{3,7},{7,3},{8,12},{12,8},{9,1... | collective-permute-start | bytes 1572872 | tf_op jit(solution)/shard_map/ppermute | solution.py:18
  433.9 15.3 %collective-permute-start.45 = (bf16[128,2048]{1,0:T(8,128)(2,1)S(1)}, bf16[128,2048]{1,0:T(8,128)(2,1)S(1)}, u32[]{:S(2)}, u32[]{:S(2)}) collective-permute-start(bf16[128,2048]{1,0:T(8,128)(2,1)S(1)} %pad_maximum_fusion.13), channel_id=1, source_target_pairs={{0,2},{2,0},{1,3},{3,1},{4,6},{6,4},{5,7},{7,5},{8,10},{10,8},{9,1... | collective-permute-start | bytes 1572872 | tf_op jit(solution)/shard_map/ppermute | solution.py:18
  438.2 21.1 %collective-permute-start.34 = (bf16[128,2048]{1,0:T(8,128)(2,1)S(1)}, bf16[128,2048]{1,0:T(8,128)(2,1)S(1)}, u32[]{:S(2)}, u32[]{:S(2)}) collective-permute-start(bf16[128,2048]{1,0:T(8,128)(2,1)S(1)} %pad_maximum_fusion.12), channel_id=1, source_target_pairs={{0,4},{4,0},{1,5},{5,1},{2,6},{6,2},{3,7},{7,3},{8,12},{12,8},{9,1... | collective-permute-start | bytes 1572872 | tf_op jit(solution)/shard_map/ppermute | solution.py:18
  439.6 19.7 %collective-permute-start.32 = (bf16[128,2048]{1,0:T(8,128)(2,1)S(1)}, bf16[128,2048]{1,0:T(8,128)(2,1)S(1)}, u32[]{:S(2)}, u32[]{:S(2)}) collective-permute-start(bf16[128,2048]{1,0:T(8,128)(2,1)S(1)} %pad_maximum_fusion.11), channel_id=1, source_target_pairs={{0,2},{2,0},{1,3},{3,1},{4,6},{6,4},{5,7},{7,5},{8,10},{10,8},{9,1... | collective-permute-start | bytes 1572872 | tf_op jit(solution)/shard_map/ppermute | solution.py:18
  512.7 31.9 %collective-permute-start.52 = (bf16[512,1280]{1,0:T(8,128)(2,1)}, bf16[512,1280]{1,0:T(8,128)(2,1)S(1)}, u32[]{:S(2)}, u32[]{:S(2)}) collective-permute-start(bf16[512,1280]{1,0:T(8,128)(2,1)} %convolution_convert_fusion.6), channel_id=1, source_target_pairs={{0,2},{2,0},{1,3},{3,1},{4,6},{6,4},{5,7},{7,5},{8,10},{10,8},{9,1... | collective-permute-start | bytes 3932168 | tf_op jit(solution)/shard_map/ppermute | solution.py:18
  515.1 31.6 %collective-permute-start.35 = (bf16[64,2048]{1,0:T(8,128)(2,1)S(1)}, bf16[64,2048]{1,0:T(8,128)(2,1)S(1)}, u32[]{:S(2)}, u32[]{:S(2)}) collective-permute-start(bf16[64,2048]{1,0:T(8,128)(2,1)S(1)} %get-tuple-element.239), channel_id=1, source_target_pairs={{0,4},{4,0},{1,5},{5,1},{2,6},{6,2},{3,7},{7,3},{8,12},{12,8},{9,1... | collective-permute-start | bytes 786440 | tf_op jit(solution)/shard_map/ppermute | solution.py:18
  517.1 54.3 %collective-permute-start.54 = (bf16[512,1280]{1,0:T(8,128)(2,1)S(1)}, bf16[512,1280]{1,0:T(8,128)(2,1)S(1)}, u32[]{:S(2)}, u32[]{:S(2)}) collective-permute-start(bf16[512,1280]{1,0:T(8,128)(2,1)S(1)} %convolution_convert_fusion.5), channel_id=1, source_target_pairs={{0,2},{2,0},{1,3},{3,1},{4,6},{6,4},{5,7},{7,5},{8,10},{10,8},{9,1... | collective-permute-start | bytes 3932168 | tf_op jit(solution)/shard_map/ppermute | solution.py:18
  545.1 28.5 %collective-permute-start.55 = (bf16[512,1280]{1,0:T(8,128)(2,1)S(1)}, bf16[512,1280]{1,0:T(8,128)(2,1)S(1)}, u32[]{:S(2)}, u32[]{:S(2)}) collective-permute-start(bf16[512,1280]{1,0:T(8,128)(2,1)S(1)} %fusion.15), channel_id=1, source_target_pairs={{0,4},{4,0},{1,5},{5,1},{2,6},{6,2},{3,7},{7,3},{8,12},{12,8},{9,1... | collective-permute-start | bytes 3932168 | tf_op jit(solution)/shard_map/ppermute | solution.py:18
  575.1 33.5 %collective-permute-start.65 = (bf16[128,1280]{1,0:T(8,128)(2,1)S(1)}, bf16[128,1280]{1,0:T(8,128)(2,1)S(1)}, u32[]{:S(2)}, u32[]{:S(2)}) collective-permute-start(bf16[128,1280]{1,0:T(8,128)(2,1)S(1)} %get-tuple-element.207), channel_id=1, source_target_pairs={{0,24},{8,16},{16,8},{24,0},{1,25},{9,17},{17,9},{25,1},{2,26},{10... | collective-permute-start | bytes 983048 | tf_op jit(solution)/shard_map/ppermute | solution.py:41
  578.0 39.6 %collective-permute-start.64 = (bf16[128,1280]{1,0:T(8,128)(2,1)S(1)}, bf16[128,1280]{1,0:T(8,128)(2,1)S(1)}, u32[]{:S(2)}, u32[]{:S(2)}) collective-permute-start(bf16[128,1280]{1,0:T(8,128)(2,1)S(1)} %get-tuple-element.208), channel_id=1, source_target_pairs={{0,16},{8,24},{16,0},{24,8},{1,17},{9,25},{17,1},{25,9},{2,18},{10... | collective-permute-start | bytes 983048 | tf_op jit(solution)/shard_map/ppermute | solution.py:41
  585.6 45.8 %collective-permute-start.61 = (f32[128,2048]{1,0:T(8,128)}, f32[128,2048]{1,0:T(8,128)}, u32[]{:S(2)}, u32[]{:S(2)}) collective-permute-start(f32[128,2048]{1,0:T(8,128)} %slice.375), channel_id=1, source_target_pairs={{0,1},{1,0},{2,3},{3,2},{4,5},{5,4},{6,7},{7,6},{8,9},{9,8},{10,11... | collective-permute-start | bytes 3145736 | tf_op jit(solution)/shard_map/ppermute | solution.py:18
  587.2 53.5 %collective-permute-start.57 = (bf16[512,1280]{1,0:T(8,128)(2,1)}, bf16[512,1280]{1,0:T(8,128)(2,1)}, u32[]{:S(2)}, u32[]{:S(2)}) collective-permute-start(bf16[512,1280]{1,0:T(8,128)(2,1)} %convolution_convert_fusion.3), channel_id=1, source_target_pairs={{0,4},{4,0},{1,5},{5,1},{2,6},{6,2},{3,7},{7,3},{8,12},{12,8},{9,1... | collective-permute-start | bytes 3932168 | tf_op jit(solution)/shard_map/ppermute | solution.py:18
  620.0 42.5 %collective-permute-start.56 = (bf16[512,1280]{1,0:T(8,128)(2,1)}, bf16[512,1280]{1,0:T(8,128)(2,1)}, u32[]{:S(2)}, u32[]{:S(2)}) collective-permute-start(bf16[512,1280]{1,0:T(8,128)(2,1)} %convolution_convert_fusion.4), channel_id=1, source_target_pairs={{0,4},{4,0},{1,5},{5,1},{2,6},{6,2},{3,7},{7,3},{8,12},{12,8},{9,1... | collective-permute-start | bytes 3932168 | tf_op jit(solution)/shard_map/ppermute | solution.py:18
  629.4 66.3 %collective-permute-start.60 = (bf16[256,768]{0,1:T(8,128)(2,1)}, bf16[256,768]{0,1:T(8,128)(2,1)}, u32[]{:S(2)}, u32[]{:S(2)}) collective-permute-start(bf16[256,768]{0,1:T(8,128)(2,1)} %bitcast.112), channel_id=1, source_target_pairs={{0,4},{4,0},{1,5},{5,1},{2,6},{6,2},{3,7},{7,3},{8,12},{12,8},{9,1... | collective-permute-start | bytes 1179656 | tf_op jit(solution)/shard_map/ppermute | solution.py:18
  643.7 43.7 %collective-permute-start.58 = (bf16[512,1280]{1,0:T(8,128)(2,1)}, bf16[512,1280]{1,0:T(8,128)(2,1)}, u32[]{:S(2)}, u32[]{:S(2)}) collective-permute-start(bf16[512,1280]{1,0:T(8,128)(2,1)} %fusion.16), channel_id=1, source_target_pairs={{0,2},{2,0},{1,3},{3,1},{4,6},{6,4},{5,7},{7,5},{8,10},{10,8},{9,1... | collective-permute-start | bytes 3932168 | tf_op jit(solution)/shard_map/ppermute | solution.py:18
  652.5 43.4 %collective-permute-start.59 = (bf16[256,1536]{1,0:T(8,128)(2,1)}, bf16[256,1536]{1,0:T(8,128)(2,1)}, u32[]{:S(2)}, u32[]{:S(2)}) collective-permute-start(bf16[256,1536]{1,0:T(8,128)(2,1)} %fusion.46), channel_id=1, source_target_pairs={{0,4},{4,0},{1,5},{5,1},{2,6},{6,2},{3,7},{7,3},{8,12},{12,8},{9,1... | collective-permute-start | bytes 2359304 | tf_op jit(solution)/shard_map/ppermute | solution.py:18
  696.8 77.5 %collective-permute-start.62 = (bf16[64,2048]{1,0:T(8,128)(2,1)}, bf16[64,2048]{1,0:T(8,128)(2,1)}, u32[]{:S(2)}, u32[]{:S(2)}) collective-permute-start(bf16[64,2048]{1,0:T(8,128)(2,1)} %get-tuple-element.235), channel_id=1, source_target_pairs={{0,4},{4,0},{1,5},{5,1},{2,6},{6,2},{3,7},{7,3},{8,12},{12,8},{9,1... | collective-permute-start | bytes 786440 | tf_op jit(solution)/shard_map/ppermute | solution.py:18
  699.3 29.1 %collective-permute-start.67 = (bf16[128,1280]{1,0:T(8,128)(2,1)}, bf16[128,1280]{1,0:T(8,128)(2,1)S(1)}, u32[]{:S(2)}, u32[]{:S(2)}) collective-permute-start(bf16[128,1280]{1,0:T(8,128)(2,1)} %get-tuple-element.203), channel_id=1, source_target_pairs={{0,8},{8,0},{16,24},{24,16},{1,9},{9,1},{17,25},{25,17},{2,10},{10... | collective-permute-start | bytes 983048 | tf_op jit(solution)/shard_map/ppermute | solution.py:41
  724.9 25.9 %collective-permute-start.69 = (bf16[128,1280]{1,0:T(8,128)(2,1)}, bf16[128,1280]{1,0:T(8,128)(2,1)}, u32[]{:S(2)}, u32[]{:S(2)}) collective-permute-start(bf16[128,1280]{1,0:T(8,128)(2,1)} %get-tuple-element.204), channel_id=1, source_target_pairs={{0,24},{8,16},{16,8},{24,0},{1,25},{9,17},{17,9},{25,1},{2,26},{10... | collective-permute-start | bytes 983048 | tf_op jit(solution)/shard_map/ppermute | solution.py:41
  726.9 34.8 %collective-permute-start.68 = (bf16[128,1280]{1,0:T(8,128)(2,1)}, bf16[128,1280]{1,0:T(8,128)(2,1)}, u32[]{:S(2)}, u32[]{:S(2)}) collective-permute-start(bf16[128,1280]{1,0:T(8,128)(2,1)} %get-tuple-element.205), channel_id=1, source_target_pairs={{0,16},{8,24},{16,0},{24,8},{1,17},{9,25},{17,1},{25,9},{2,18},{10... | collective-permute-start | bytes 983048 | tf_op jit(solution)/shard_map/ppermute | solution.py:41
  768.6 18.3 %collective-permute-start.71 = (bf16[80,2688]{1,0:T(8,128)(2,1)}, bf16[80,2688]{1,0:T(8,128)(2,1)S(1)}, u32[]{:S(2)}, u32[]{:S(2)}) collective-permute-start(bf16[80,2688]{1,0:T(8,128)(2,1)} %reduce-scatter.8.cloned.1.call-done), channel_id=1, source_target_pairs={{0,0},{1,16},{2,1},{3,17},{4,2},{5,18},{6,3},{7,19},{8,4},{9,20},{... | collective-permute-start | bytes 1290248 | tf_op jit(solution)/shard_map/ppermute | solution.py:563
  (115 other events, 1660.1 us)
Sparse Core Ops, SparseCore 0:
  29.0 156.9 all-gather.3
  187.5 60.2 all-gather.7
  250.0 114.6 all-gather.5
  392.6 61.0 reduce-scatter.5
  455.8 114.7 reduce-scatter.3
  575.9 192.6 reduce-scatter.7

commit v3 on v2

--- a/solution.py
+++ b/solution.py
@@ -453,9 +453,9 @@
     )
     vectors = jnp.pad(vectors.T, ((0, 0), (0, 120)))
     out_gates = jnp.concatenate([w_recur_out, w_rgate, w_igate, vectors], axis=1)
-    out_gates = lax.ppermute(out_gates, EVERY, to_halves(devices))
-    out_gates = lax.all_gather(out_gates, CHIPS, axis=0, tiled=True)
-    out_full = out_gates[:, :width]
+    out_gates = lax.all_gather(out_gates, EVERY, axis=0, tiled=True)
+    out_gates = pick(out_gates.reshape(2, channels, -1), c, 0)
+    out_full, gates = out_gates[:, :width], out_gates[:, width:]
     branch_full = fine_gather(z_gather(branch_shard), "y", "x")
     recur_in_full = fine_gather(z_gather(recur_in_shard), "x", "y")
 
@@ -467,10 +467,8 @@
     gate_up_full = lax.all_gather(gate_up_shard, "z", axis=0, tiled=True)
     down = w_down.reshape(2, units, -1)
     down_shard = ordered(first_y, pick(down, y, 0), swap(pick(down, 1 - y, 0), "y"), 1)
-    down_full = lax.all_gather(down_shard, "z", axis=0)
-    down_full = jnp.swapaxes(down_full, 0, 1).reshape(units, width)
-
-    vec = out_gates[:, width + 512 : width + 520].T.astype(F32)
+
+    vec = gates[:, 512:520].T.astype(F32)
     rate = vec[7]
     eight = -8.0 * jax.nn.softplus(rate)
     vec = jnp.concatenate([vec[:7], eight[None]])
@@ -483,8 +481,10 @@
     recur_pre = mm(normed, recur_in_full).reshape(2, length, channels)
     branch_act, gelu_pull = jax.vjp(partial(jax.nn.gelu, approximate=True), branch_pre)
     halo = z_shift(recur_pre[:, length - 8 :], 1)
-    conv, sig_r, sig_i, decay, state, prod = run_forward(recur_pre, halo, vec, out_gates)
+    conv, sig_r, sig_i, decay, state, prod = run_forward(recur_pre, halo, vec, gates)
     carry = z_carry(prod[:, -1], state[:, -1], 1)
+    carry, down_shard = lax.optimization_barrier((carry, down_shard))
+    down_across = lax.all_gather(down_shard.T, "z", axis=0, tiled=True)
     states = (state + prod * carry[:, None]).reshape(2 * length, channels)
     mixed_low = low(states * branch_act)
     recur_out = mm(mixed_low, out_full)
@@ -495,12 +495,12 @@
     pre = mm(tokens_all, gate_up_full)
     hidden_f, mlp_pull = jax.vjp(mlp_act, pre[:, :units], pre[:, units:])
     hidden = low(hidden_f)
-    mlp_out = group_scatter(mm(hidden, down_full))
+    mlp_out = group_scatter(mm_rows(hidden, down_across))
     block_output = own_tokens(low(middle + mlp_out))
 
     own_grad = own_sequence(cotangent)
     grad_all = group_gather(own_grad)
-    grad_hidden = mm_rows(grad_all, down_full)
+    grad_hidden = mm(grad_all, down_across)
     grad_pre = jnp.concatenate([low(g) for g in mlp_pull(grad_hidden)], axis=1)
     grad_normed2 = group_scatter(mm_rows(grad_pre, gate_up_full))
     block = width // z_count
@@ -523,11 +523,6 @@
     grad_mixed = mm_rows(grad_out_low, out_full)
     grad_states = (grad_mixed * branch_act).reshape(2, length, channels)
     grad_branch_low = low(gelu_pull(grad_mixed * states)[0])
-    local, ahead, sent = run_reverse(decay, grad_states)
-    entering = z_carry(prod[:, -1], sent, -1)
-    grad_conv, grad_rgate, grad_igate, small = run_backward(
-        local, ahead, entering, state, prod, carry, conv, sig_r, sig_i, recur_pre, halo, vec, out_gates
-    )
 
     def quarter(grad):
         def part(at):
@@ -537,8 +532,14 @@
         return part
 
     block, corner, far, onward = fine_near(quarter(grad_branch_low), "y", "x")
-    grad_conv, corner = lax.optimization_barrier((grad_conv, corner))
+    local, ahead, sent = run_reverse(decay, grad_states)
+    entering = z_carry(prod[:, -1], sent, -1)
+    entering, corner = lax.optimization_barrier((entering, corner))
     near = onward(corner)
+    grad_conv, grad_rgate, grad_igate, small = run_backward(
+        local, ahead, entering, state, prod, carry, conv, sig_r, sig_i, recur_pre, halo, vec, gates
+    )
+
     rim = z_shift(grad_conv[:, :8], -1)
     grad_ext = jnp.concatenate([grad_conv, rim], axis=1)
     grad_recur_low = low(sum(vec[k] * grad_ext[:, k : k + length] for k in range(CONV)))

time: 809 us -> 796 us (0.984)
  waiting for transfers between devices: 375 us -> 359 us
  matrix products: 90.6 us -> 99.6 us
    all_gather x2, waiting for transfers between devices: 0.02 us -> 18.5 us  [the longest x1 18.5 us: on_device(): down_across = lax.all_gather(down_shard.T, 'z', axis=0, tiled=True)]
    all_gather x1, waiting for transfers between devices: 15.8 us -> 0.01 us  [on_device(): gate_up_full = lax.all_gather(gate_up_shard, 'z', axis=0, tiled=True)]
    ppermute x1 -> x0, waiting for transfers between devices: 11.6 us -> none  [on_device(): out_gates = lax.ppermute(out_gates, EVERY, to_halves(devices))]
    dot_general x5, matrix products: 22.6 us -> 33.5 us  [mm(): return jnp.dot(left, right, preferred_element_type=F32)]
    ppermute x53, starting transfers between devices: 52 us -> 42.9 us  [swap(): return lax.ppermute(value, axis, PAIR)]
    unnamed x177 -> x160, local copies, waits for them, and re-layouts: 32.1 us -> 37.3 us
  transfers between devices with their start and end apart: 85 -> 84, of which waited for: 38 -> 38; matrix products, arithmetic and copies ran while one was open for 29% -> 31% of each run, Pallas kernels for 3% -> 3%
where the time goes in v3:
time: 796 us; the launch traced here: 786 us
  waiting for transfers between devices  359 us (45%)
  local copies, waits for them, and re-layouts  124 us (16%)
  matrix products  99.6 us (13%)
  starting transfers between devices  99.5 us (12%)
  other arithmetic  64 us (8%)
  Pallas kernels  24 us (3%)
  between operations  15.7 us (2%)
    ppermute x53, waiting for transfers between devices, swap(): return lax.ppermute(value, axis, PAIR)  210 us
    ppermute x15, waiting for transfers between devices, z_send(): return lax.ppermute(value, 'z', [(s, s ^ j) for s in range(count)])  88.9 us
    ppermute x53, starting transfers between devices, swap(): return lax.ppermute(value, axis, PAIR)  42.9 us
    dot_general x11, matrix products, outer_sum(): lax.dot_general(left, right, (((0,), (0,)), ((), ())), preferred_element_...  38.1 us
    unnamed x160, local copies, waits for them, and re-layouts  37.3 us
    dot_general x5, matrix products, mm(): return jnp.dot(left, right, preferred_element_type=F32)  33.5 us
    dot_general x5, matrix products, mm_rows(): lax.dot_general(left, weight, (((1,), (1,)), ((), ())), preferred_element...  28 us
    dynamic_update_slice x16, local copies, waits for them, and re-layouts, place(): full = lax.dynamic_update_slice_in_dim(full, piece, at * rows, 0)  26.8 us
  transfers between devices with their start and end apart: 84, of which 38 were waited for; matrix products, arithmetic and copies ran while one was open for 31% of the time, Pallas kernels for 3%

profile of v3, /device:TPU:10, one launch (start us, length us, event | category | flops | bytes accessed | tf_op | source)
XLA Modules:
  0.0 785.9 jit_solution(6427148380592325333)
XLA Ops:
  24.9 6.3 all-to-all-start
  38.0 23.1 %all-to-all-done = bf16[32,1,128]{2,1,0:T(2,128)(2,1)S(1)} async-done(((bf16[32,1,128]{2,1,0:T(2,128)(2,1)}), bf16[32,1,128]{2,1,0:T(2,128)(2,1)S(1)}, u32[]{:S(2)}, u32[]{:S(2)}) %all-to-all-start) | async-done | bytes 8224 | tf_op jit(solution)/shard_map/all_to_all | solution.py:447
  65.2 4.9 fusion.57
  80.7 19.3 %collective-permute-done.15 = bf16[128,1280]{1,0:T(8,128)(2,1)S(1)} collective-permute-done((bf16[128,1280]{1,0:T(8,128)(2,1)}, bf16[128,1280]{1,0:T(8,128)(2,1)S(1)}, u32[]{:S(2)}, u32[]{:S(2)}) %collective-permute-start.15) | collective-permute-done | bytes 327712 | tf_op jit(solution)/shard_map/ppermute | solution.py:41
  101.0 5.0 collective-permute-done.16
  121.1 34.2 %collective-permute-done.8 = bf16[512,1280]{1,0:T(8,128)(2,1)} collective-permute-done((bf16[512,1280]{1,0:T(8,128)(2,1)S(1)}, bf16[512,1280]{1,0:T(8,128)(2,1)}, u32[]{:S(2)}, u32[]{:S(2)}) %collective-permute-start.8) | collective-permute-done | bytes 1310752 | tf_op jit(solution)/shard_map/ppermute | solution.py:18
  167.3 22.6 %collective-permute-done.18 = bf16[512,1280]{1,0:T(8,128)(2,1)} collective-permute-done((bf16[512,1280]{1,0:T(8,128)(2,1)}, bf16[512,1280]{1,0:T(8,128)(2,1)}, u32[]{:S(2)}, u32[]{:S(2)}) %collective-permute-start.18) | collective-permute-done | bytes 1310752 | tf_op jit(solution)/shard_map/ppermute | solution.py:18
  195.6 33.3 %collective-permute-done.9 = bf16[512,1280]{1,0:T(8,128)(2,1)} collective-permute-done((bf16[512,1280]{1,0:T(8,128)(2,1)}, bf16[512,1280]{1,0:T(8,128)(2,1)}, u32[]{:S(2)}, u32[]{:S(2)}) %collective-permute-start.9) | collective-permute-done | bytes 1310752 | tf_op jit(solution)/shard_map/ppermute | solution.py:18
  236.7 3.5 dynamic-slice_bitcast_fusion
  249.8 9.6 %recur_forward.1 = (f32[2,128,1280]{2,1,0:T(8,128)}, f32[2,128,1280]{2,1,0:T(8,128)}, f32[2,128,1280]{2,1,0:T(8,128)}, f32[2,128,1280]{2,1,0:T(8,128)}, f32[2,12...) custom-call(f32[2,128,1280]{2,1,0:T(8,128)} %bitcast.174, f32[2,8,1280]{2,1,0:T(8,128)} %collective-permute-done.10.halo_ref, ...), custom_call_target="tpu_custom_call" | custom-call | flops 335544320 | bytes 9175040 | tf_op jit(solution)/shard_map/recur_forward/pallas_call | solution.py:311
  273.0 6.0 fusion.30
  286.2 6.5 collective-permute-done.39
  305.3 8.7 %collective-permute-done.23 = bf16[128,2048]{1,0:T(8,128)(2,1)S(1)} collective-permute-done((bf16[128,2048]{1,0:T(8,128)(2,1)}, bf16[128,2048]{1,0:T(8,128)(2,1)S(1)}, u32[]{:S(2)}, u32[]{:S(2)}) %collective-permute-start.23) | collective-permute-done | bytes 524320 | tf_op jit(solution)/shard_map/ppermute | solution.py:18
  333.9 12.3 %fusion.98 = f32[1024,1536]{1,0:T(8,128)} fusion(bf16[1024,2048]{1,0:T(8,128)(2,1)} %constant_dynamic-update-slice_fusion, bf16[2048,1536]{0,1:T(8,128)(2,1)} %all-gather.6.cloned.1.call-done), kind=kOutput, calls=%fused_computation.277 | convolution fusion | flops 6442450944 | bytes 16777216 | tf_op jit(solution)/shard_map/dot_general | solution.py:389
  346.2 18.5 %all-gather.8.cloned.1.call-done = bf16[2048,768]{0,1:T(8,128)(2,1)} async-done(((bf16[512,768]{0,1:T(8,128)(2,1)}), bf16[2048,768]{0,1:T(8,128)(2,1)}) %all-gather.8.cloned.1.call-update) | async-done | bytes 3145744 | tf_op jit(solution)/shard_map/all_gather | solution.py:487
  364.7 12.1 %fusion.14 = (bf16[1024,768]{1,0:T(8,128)(2,1)}, bf16[1024,768]{1,0:T(8,128)(2,1)}, bf16[1024,768]{1,0:T(8,128)(2,1)S(1)}) fusion(f32[1024,1536]{1,0:T(8,128)} %fusion.98, bf16[1024,2048]{1,0:T(8,128)(2,1)} %constant_dynamic-update-slice_fusion.7, bf16[2048,768]{0,1:T(8,128)(2,1)} %all-gather.8.cloned.1.call-done), kind=kOutput, calls=%fused_computation.29 | convolution fusion | flops 3241672704 | bytes 18350080 | tf_op jit(solution)/shard_map/dot_general | solution.py:389
  378.0 7.3 convolution_convert_fusion.2
  385.4 9.9 %fusion.17 = f32[1024,2048]{1,0:T(8,128)S(1)} fusion(bf16[2048,1536]{0,1:T(8,128)(2,1)} %all-gather.6.cloned.1.call-done, bf16[1024,768]{1,0:T(8,128)(2,1)} %get-tuple-element.199, bf16[1024,768]{1,0:T(8,128)(2,1)} %get-tuple-element.198), kind=kOutput, calls=%fused_computation.42 | convolution fusion | flops 6448742400 | bytes 17825792 | tf_op jit(solution)/shard_map/dot_general | solution.py:393
  401.3 11.3 %convolution_convert_fusion.1 = bf16[2048,1536]{1,0:T(8,128)(2,1)} fusion(bf16[1024,2048]{1,0:T(8,128)(2,1)} %constant_dynamic-update-slice_fusion, bf16[1024,768]{1,0:T(8,128)(2,1)S(1)} %copy-done.64, bf16[1024,768]{1,0:T(8,128)(2,1)S(1)} %copy-done.63), kind=kOutput, calls=%fused_computation.3 | convolution fusion | flops 6451888128 | bytes 13631488 | tf_op jit(solution)/shard_map/dot_general | solution.py:397
  412.8 5.8 fusion.99
  419.0 3.7 fusion.92
  428.2 3.9 collective-permute-done.45
  441.5 7.9 %collective-permute-done.46 = bf16[128,2048]{1,0:T(8,128)(2,1)S(1)} collective-permute-done((bf16[128,2048]{1,0:T(8,128)(2,1)S(1)}, bf16[128,2048]{1,0:T(8,128)(2,1)S(1)}, u32[]{:S(2)}, u32[]{:S(2)}) %collective-permute-start.46) | collective-permute-done | bytes 524320 | tf_op jit(solution)/shard_map/ppermute | solution.py:18
  449.9 10.0 %collective-permute-done.33 = bf16[128,2048]{1,0:T(8,128)(2,1)S(1)} collective-permute-done((bf16[128,2048]{1,0:T(8,128)(2,1)S(1)}, bf16[128,2048]{1,0:T(8,128)(2,1)S(1)}, u32[]{:S(2)}, u32[]{:S(2)}) %collective-permute-start.33) | collective-permute-done | bytes 524320 | tf_op jit(solution)/shard_map/ppermute | solution.py:18
  465.5 6.7 fusion.25
  475.5 5.1 recur_reverse.1
  483.3 5.2 collective-permute-start.48
  488.4 5.0 convolution_convert_fusion
  494.8 10.2 %collective-permute-done.51 = bf16[512,1280]{1,0:T(8,128)(2,1)} collective-permute-done((bf16[512,1280]{1,0:T(8,128)(2,1)}, bf16[512,1280]{1,0:T(8,128)(2,1)}, u32[]{:S(2)}, u32[]{:S(2)}) %collective-permute-start.51) | collective-permute-done | bytes 1310752 | tf_op jit(solution)/shard_map/ppermute | solution.py:18
  504.9 9.3 %recur_backward.1 = (f32[2,128,1280]{2,1,0:T(8,128)}, f32[1280,256]{1,0:T(8,128)}, f32[1280,256]{1,0:T(8,128)}, f32[8,1280]{1,0:T(8,128)}) custom-call(f32[2,128,1280]{2,1,0:T(8,128)} %get-tuple-element.64.l_ref, f32[2,128,1280]{2,1,0:T(8,128)} %get-tuple-element.65.q_ref, f32[2,1280]{1,0:T(2,128)} %fusion.70.e_ref, ...), custom_call_target="tpu_custom_call" | custom-call | flops 671088640 | bytes 13107200 | tf_op jit(solution)/shard_map/recur_backward/pallas_call | solution.py:348
  518.8 5.9 fusion.1
  535.0 4.7 collective-permute-start.52
  539.8 3.9 collective-permute-done.52
  544.3 13.1 %collective-permute-done.53 = bf16[512,1280]{1,0:T(8,128)(2,1)S(1)} collective-permute-done((bf16[512,1280]{1,0:T(8,128)(2,1)S(1)}, bf16[512,1280]{1,0:T(8,128)(2,1)S(1)}, u32[]{:S(2)}, u32[]{:S(2)}) %collective-permute-start.53) | collective-permute-done | bytes 1310752 | tf_op jit(solution)/shard_map/ppermute | solution.py:18
  557.4 3.8 collective-permute-done.54
  568.5 4.1 convolution_add_fusion.4
  576.9 18.8 %collective-permute-done.64 = bf16[128,1280]{1,0:T(8,128)(2,1)S(1)} collective-permute-done((bf16[128,1280]{1,0:T(8,128)(2,1)S(1)}, bf16[128,1280]{1,0:T(8,128)(2,1)S(1)}, u32[]{:S(2)}, u32[]{:S(2)}) %collective-permute-start.64) | collective-permute-done | bytes 327712 | tf_op jit(solution)/shard_map/ppermute | solution.py:41
  595.7 9.2 %collective-permute-done.63 = bf16[128,1280]{1,0:T(8,128)(2,1)S(1)} collective-permute-done((bf16[128,1280]{1,0:T(8,128)(2,1)S(1)}, bf16[128,1280]{1,0:T(8,128)(2,1)S(1)}, u32[]{:S(2)}, u32[]{:S(2)}) %collective-permute-start.63) | collective-permute-done | bytes 327712 | tf_op jit(solution)/shard_map/ppermute | solution.py:41
  638.5 11.6 %collective-permute-done.55 = bf16[512,1280]{1,0:T(8,128)(2,1)} collective-permute-done((bf16[512,1280]{1,0:T(8,128)(2,1)}, bf16[512,1280]{1,0:T(8,128)(2,1)}, u32[]{:S(2)}, u32[]{:S(2)}) %collective-permute-start.55) | collective-permute-done | bytes 1310752 | tf_op jit(solution)/shard_map/ppermute | solution.py:18
  650.1 19.7 %collective-permute-done.57 = bf16[512,1280]{1,0:T(8,128)(2,1)} collective-permute-done((bf16[512,1280]{1,0:T(8,128)(2,1)}, bf16[512,1280]{1,0:T(8,128)(2,1)}, u32[]{:S(2)}, u32[]{:S(2)}) %collective-permute-start.57) | collective-permute-done | bytes 1310752 | tf_op jit(solution)/shard_map/ppermute | solution.py:18
  669.7 3.8 fusion.7
  678.0 6.2 collective-permute-done.58
  686.7 3.8 collective-permute-start.66
  694.6 3.4 maximum_select_fusion
  716.9 23.4 %collective-permute-done.68 = bf16[128,1280]{1,0:T(8,128)(2,1)} collective-permute-done((bf16[128,1280]{1,0:T(8,128)(2,1)}, bf16[128,1280]{1,0:T(8,128)(2,1)}, u32[]{:S(2)}, u32[]{:S(2)}) %collective-permute-start.68) | collective-permute-done | bytes 327712 | tf_op jit(solution)/shard_map/ppermute | solution.py:41
  740.3 13.2 %collective-permute-done.67 = bf16[128,1280]{1,0:T(8,128)(2,1)} collective-permute-done((bf16[128,1280]{1,0:T(8,128)(2,1)}, bf16[128,1280]{1,0:T(8,128)(2,1)}, u32[]{:S(2)}, u32[]{:S(2)}) %collective-permute-start.67) | collective-permute-done | bytes 327712 | tf_op jit(solution)/shard_map/ppermute | solution.py:41
  757.3 5.3 collective-permute-start.70
  765.4 10.4 %collective-permute-done.70 = bf16[80,2688]{1,0:T(8,128)(2,1)S(1)} collective-permute-done((bf16[80,2688]{1,0:T(8,128)(2,1)}, bf16[80,2688]{1,0:T(8,128)(2,1)S(1)}, u32[]{:S(2)}, u32[]{:S(2)}) %collective-permute-start.70) | collective-permute-done | bytes 430112 | tf_op jit(solution)/shard_map/ppermute | solution.py:564
  (462 shorter events, 278.7 us)
Async XLA Ops:
  7.2 229.5 %all-gather.4.cloned.1.call-start = ((), (), s32[]{:S(2)}) async-start(), calls=%async_computation.4 | async-start | bytes 14192640 | tf_op jit(solution)/shard_map/all_gather | solution.py:456
  15.5 47.1 %collective-permute-start = (bf16[64,2048]{1,0:T(8,128)(2,1)}, bf16[64,2048]{1,0:T(8,128)(2,1)S(1)}, u32[]{:S(2)}, u32[]{:S(2)}) collective-permute-start(bf16[64,2048]{1,0:T(8,128)(2,1)} %get-tuple-element.244), channel_id=1, source_target_pairs={{0,4},{4,0},{1,5},{5,1},{2,6},{6,2},{3,7},{7,3},{8,12},{12,8},{9,1... | collective-permute-start | bytes 786440 | tf_op jit(solution)/shard_map/ppermute | solution.py:18
  18.8 51.2 %collective-permute-start.35 = (bf16[64,2048]{1,0:T(8,128)(2,1)}, bf16[64,2048]{1,0:T(8,128)(2,1)}, u32[]{:S(2)}, u32[]{:S(2)}) collective-permute-start(bf16[64,2048]{1,0:T(8,128)(2,1)} %get-tuple-element.240), channel_id=1, source_target_pairs={{0,4},{4,0},{1,5},{5,1},{2,6},{6,2},{3,7},{7,3},{8,12},{12,8},{9,1... | collective-permute-start | bytes 786440 | tf_op jit(solution)/shard_map/ppermute | solution.py:18
  20.2 58.1 %collective-permute-start.6 = (bf16[128,1280]{1,0:T(8,128)(2,1)}, bf16[128,1280]{1,0:T(8,128)(2,1)}, u32[]{:S(2)}, u32[]{:S(2)}) collective-permute-start(bf16[128,1280]{1,0:T(8,128)(2,1)} %maximum_select_fusion.11), channel_id=1, source_target_pairs={{0,24},{8,16},{16,8},{24,0},{1,25},{9,17},{17,9},{25,1},{2,26},{10... | collective-permute-start | bytes 983048 | tf_op jit(solution)/shard_map/ppermute | solution.py:41
  21.7 54.7 %collective-permute-start.5 = (bf16[128,1280]{1,0:T(8,128)(2,1)}, bf16[128,1280]{1,0:T(8,128)(2,1)}, u32[]{:S(2)}, u32[]{:S(2)}) collective-permute-start(bf16[128,1280]{1,0:T(8,128)(2,1)} %maximum_select_fusion.11), channel_id=1, source_target_pairs={{0,16},{8,24},{16,0},{24,8},{1,17},{9,25},{17,1},{25,9},{2,18},{10... | collective-permute-start | bytes 983048 | tf_op jit(solution)/shard_map/ppermute | solution.py:41
  23.0 52.3 %collective-permute-start.4 = (bf16[128,1280]{1,0:T(8,128)(2,1)}, bf16[128,1280]{1,0:T(8,128)(2,1)}, u32[]{:S(2)}, u32[]{:S(2)}) collective-permute-start(bf16[128,1280]{1,0:T(8,128)(2,1)} %maximum_select_fusion.11), channel_id=1, source_target_pairs={{0,8},{8,0},{16,24},{24,16},{1,9},{9,1},{17,25},{25,17},{2,10},{10... | collective-permute-start | bytes 983048 | tf_op jit(solution)/shard_map/ppermute | solution.py:41
  24.9 36.2 %all-to-all-start = ((bf16[32,1,128]{2,1,0:T(2,128)(2,1)}), bf16[32,1,128]{2,1,0:T(2,128)(2,1)S(1)}, u32[]{:S(2)}, u32[]{:S(2)}) async-start(bf16[32,1,128]{2,1,0:T(2,128)(2,1)} %tile.9), calls=%async_computation | async-start | bytes 32768 | tf_op jit(solution)/shard_map/all_to_all | solution.py:447
  31.3 302.6 %all-gather.6.cloned.1.call-start = ((), (), s32[]{:S(2)}) async-start(), calls=%async_computation.5 | async-start | bytes 7864320 | tf_op jit(solution)/shard_map/all_gather | solution.py:467
  62.6 46.7 %collective-permute-start.17 = (bf16[128,1280]{1,0:T(8,128)(2,1)}, bf16[128,1280]{1,0:T(8,128)(2,1)}, u32[]{:S(2)}, u32[]{:S(2)}) collective-permute-start(bf16[128,1280]{1,0:T(8,128)(2,1)} %maximum_select_fusion.10), channel_id=1, source_target_pairs={{0,24},{8,16},{16,8},{24,0},{1,25},{9,17},{17,9},{25,1},{2,26},{10... | collective-permute-start | bytes 983048 | tf_op jit(solution)/shard_map/ppermute | solution.py:41
  70.0 36.0 %collective-permute-start.16 = (bf16[128,1280]{1,0:T(8,128)(2,1)}, bf16[128,1280]{1,0:T(8,128)(2,1)}, u32[]{:S(2)}, u32[]{:S(2)}) collective-permute-start(bf16[128,1280]{1,0:T(8,128)(2,1)} %maximum_select_fusion.10), channel_id=1, source_target_pairs={{0,16},{8,24},{16,0},{24,8},{1,17},{9,25},{17,1},{25,9},{2,18},{10... | collective-permute-start | bytes 983048 | tf_op jit(solution)/shard_map/ppermute | solution.py:41
  75.3 24.6 %collective-permute-start.15 = (bf16[128,1280]{1,0:T(8,128)(2,1)}, bf16[128,1280]{1,0:T(8,128)(2,1)S(1)}, u32[]{:S(2)}, u32[]{:S(2)}) collective-permute-start(bf16[128,1280]{1,0:T(8,128)(2,1)} %maximum_select_fusion.10), channel_id=1, source_target_pairs={{0,8},{8,0},{16,24},{24,16},{1,9},{9,1},{17,25},{25,17},{2,10},{10... | collective-permute-start | bytes 983048 | tf_op jit(solution)/shard_map/ppermute | solution.py:41
  76.5 35.7 %collective-permute-start.14 = (bf16[768,256]{1,0:T(8,128)(2,1)}, bf16[768,256]{1,0:T(8,128)(2,1)S(1)}, u32[]{:S(2)}, u32[]{:S(2)}) collective-permute-start(bf16[768,256]{1,0:T(8,128)(2,1)} %get-tuple-element.227), channel_id=1, source_target_pairs={{0,4},{4,0},{1,5},{5,1},{2,6},{6,2},{3,7},{7,3},{8,12},{12,8},{9,1... | collective-permute-start | bytes 1179656 | tf_op jit(solution)/shard_map/ppermute | solution.py:18
  78.3 41.4 %collective-permute-start.28 = (bf16[256,1536]{0,1:T(8,128)(2,1)}, bf16[256,1536]{0,1:T(8,128)(2,1)S(1)}, u32[]{:S(2)}, u32[]{:S(2)}) collective-permute-start(bf16[256,1536]{0,1:T(8,128)(2,1)} %bitcast.194), channel_id=1, source_target_pairs={{0,4},{4,0},{1,5},{5,1},{2,6},{6,2},{3,7},{7,3},{8,12},{12,8},{9,1... | collective-permute-start | bytes 2359304 | tf_op jit(solution)/shard_map/ppermute | solution.py:18
  99.9 55.3 %collective-permute-start.8 = (bf16[512,1280]{1,0:T(8,128)(2,1)S(1)}, bf16[512,1280]{1,0:T(8,128)(2,1)}, u32[]{:S(2)}, u32[]{:S(2)}) collective-permute-start(bf16[512,1280]{1,0:T(8,128)(2,1)S(1)} %constant_dynamic-update-slice_fusion.28), channel_id=1, source_target_pairs={{0,2},{2,0},{1,3},{3,1},{4,6},{6,4},{5,7},{7,5},{8,10},{10,8},{9,1... | collective-permute-start | bytes 3932168 | tf_op jit(solution)/shard_map/ppermute | solution.py:18
  106.0 55.8 %collective-permute-start.7 = (bf16[512,1280]{1,0:T(8,128)(2,1)S(1)}, bf16[512,1280]{1,0:T(8,128)(2,1)}, u32[]{:S(2)}, u32[]{:S(2)}) collective-permute-start(bf16[512,1280]{1,0:T(8,128)(2,1)S(1)} %constant_dynamic-update-slice_fusion.28), channel_id=1, source_target_pairs={{0,4},{4,0},{1,5},{5,1},{2,6},{6,2},{3,7},{7,3},{8,12},{12,8},{9,1... | collective-permute-start | bytes 3932168 | tf_op jit(solution)/shard_map/ppermute | solution.py:18
  111.1 78.9 %collective-permute-start.18 = (bf16[512,1280]{1,0:T(8,128)(2,1)}, bf16[512,1280]{1,0:T(8,128)(2,1)}, u32[]{:S(2)}, u32[]{:S(2)}) collective-permute-start(bf16[512,1280]{1,0:T(8,128)(2,1)} %constant_dynamic-update-slice_fusion.20), channel_id=1, source_target_pairs={{0,4},{4,0},{1,5},{5,1},{2,6},{6,2},{3,7},{7,3},{8,12},{12,8},{9,1... | collective-permute-start | bytes 3932168 | tf_op jit(solution)/shard_map/ppermute | solution.py:18
  112.2 80.4 %collective-permute-start.19 = (bf16[512,1280]{1,0:T(8,128)(2,1)}, bf16[512,1280]{1,0:T(8,128)(2,1)}, u32[]{:S(2)}, u32[]{:S(2)}) collective-permute-start(bf16[512,1280]{1,0:T(8,128)(2,1)} %constant_dynamic-update-slice_fusion.20), channel_id=1, source_target_pairs={{0,2},{2,0},{1,3},{3,1},{4,6},{6,4},{5,7},{7,5},{8,10},{10,8},{9,1... | collective-permute-start | bytes 3932168 | tf_op jit(solution)/shard_map/ppermute | solution.py:18
  119.7 163.3 %collective-permute-start.37 = (bf16[128,2048]{1,0:T(8,128)(2,1)}, bf16[128,2048]{1,0:T(8,128)(2,1)}, u32[]{:S(2)}, u32[]{:S(2)}) collective-permute-start(bf16[128,2048]{1,0:T(8,128)(2,1)} %get-tuple-element.189), channel_id=1, source_target_pairs={{0,4},{4,0},{1,5},{5,1},{2,6},{6,2},{3,7},{7,3},{8,12},{12,8},{9,1... | collective-permute-start | bytes 1572872 | tf_op jit(solution)/shard_map/ppermute | solution.py:18
  155.3 73.6 %collective-permute-start.9 = (bf16[512,1280]{1,0:T(8,128)(2,1)}, bf16[512,1280]{1,0:T(8,128)(2,1)}, u32[]{:S(2)}, u32[]{:S(2)}) collective-permute-start(bf16[512,1280]{1,0:T(8,128)(2,1)} %collective-permute-done.8), channel_id=1, source_target_pairs={{0,4},{4,0},{1,5},{5,1},{2,6},{6,2},{3,7},{7,3},{8,12},{12,8},{9,1... | collective-permute-start | bytes 3932168 | tf_op jit(solution)/shard_map/ppermute | solution.py:18
  158.4 206.3 %all-gather.8.cloned.1.call-start = ((), (), s32[]{:S(2)}) async-start(), calls=%async_computation.6 | async-start | bytes 3932160 | tf_op jit(solution)/shard_map/all_gather | solution.py:487
  161.8 122.7 %collective-permute-start.36 = (bf16[128,2048]{1,0:T(8,128)(2,1)}, bf16[128,2048]{1,0:T(8,128)(2,1)}, u32[]{:S(2)}, u32[]{:S(2)}) collective-permute-start(bf16[128,2048]{1,0:T(8,128)(2,1)} %get-tuple-element.189), channel_id=1, source_target_pairs={{0,2},{2,0},{1,3},{3,1},{4,6},{6,4},{5,7},{7,5},{8,10},{10,8},{9,1... | collective-permute-start | bytes 1572872 | tf_op jit(solution)/shard_map/ppermute | solution.py:18
  189.9 40.4 %collective-permute-start.3 = (bf16[128,2048]{0,1:T(8,128)(2,1)S(1)}, bf16[128,2048]{0,1:T(8,128)(2,1)S(1)}, u32[]{:S(2)}, u32[]{:S(2)}) collective-permute-start(bf16[128,2048]{0,1:T(8,128)(2,1)S(1)} %bitcast.148), channel_id=1, source_target_pairs={{0,1},{1,0},{2,3},{3,2},{4,5},{5,4},{6,7},{7,6},{8,9},{9,8},{10,11... | collective-permute-start | bytes 1572872 | tf_op jit(solution)/shard_map/ppermute | solution.py:18
  192.6 74.0 %collective-permute-start.20 = (bf16[512,1280]{1,0:T(8,128)(2,1)}, bf16[512,1280]{1,0:T(8,128)(2,1)}, u32[]{:S(2)}, u32[]{:S(2)}) collective-permute-start(bf16[512,1280]{1,0:T(8,128)(2,1)} %collective-permute-done.18), channel_id=1, source_target_pairs={{0,2},{2,0},{1,3},{3,1},{4,6},{6,4},{5,7},{7,5},{8,10},{10,8},{9,1... | collective-permute-start | bytes 3932168 | tf_op jit(solution)/shard_map/ppermute | solution.py:18
  296.6 28.7 %collective-permute-start.41 = (bf16[384,2048]{1,0:T(8,128)(2,1)}, bf16[384,2048]{1,0:T(8,128)(2,1)}, u32[]{:S(2)}, u32[]{:S(2)}) collective-permute-start(bf16[384,2048]{1,0:T(8,128)(2,1)} %pad_maximum_fusion.5), channel_id=1, source_target_pairs={{0,1},{1,0},{2,3},{3,2},{4,5},{5,4},{6,7},{7,6},{8,9},{9,8},{10,11... | collective-permute-start | bytes 4718600 | tf_op jit(solution)/shard_map/ppermute | solution.py:18
  301.5 22.0 %collective-permute-start.40 = (bf16[128,2048]{1,0:T(8,128)(2,1)}, bf16[128,2048]{1,0:T(8,128)(2,1)}, u32[]{:S(2)}, u32[]{:S(2)}) collective-permute-start(bf16[128,2048]{1,0:T(8,128)(2,1)} %get-tuple-element.189), channel_id=1, source_target_pairs={{0,1},{1,0},{2,3},{3,2},{4,5},{5,4},{6,7},{7,6},{8,9},{9,8},{10,11... | collective-permute-start | bytes 1572872 | tf_op jit(solution)/shard_map/ppermute | solution.py:18
  303.4 306.0 %reduce-scatter.6.cloned.1.call-start = ((), (), s32[]{:S(2)}) async-start(), calls=%async_computation.8 | async-start | bytes 3932160 | tf_op jit(solution)/shard_map/reduce_scatter | solution.py:510
  385.3 247.7 %reduce-scatter.4.cloned.1.call-start = ((), (), s32[]{:S(2)}) async-start(), calls=%async_computation.7 | async-start | bytes 7864320 | tf_op jit(solution)/shard_map/reduce_scatter | solution.py:507
  400.4 18.6 %collective-permute-start.42 = (bf16[512,2048]{1,0:T(8,128)(2,1)}, bf16[512,2048]{1,0:T(8,128)(2,1)}, u32[]{:S(2)}, u32[]{:S(2)}) collective-permute-start(bf16[512,2048]{1,0:T(8,128)(2,1)} %slice.522), channel_id=1, source_target_pairs={{0,1},{1,0},{2,3},{3,2},{4,5},{5,4},{6,7},{7,6},{8,9},{9,8},{10,11... | collective-permute-start | bytes 6291464 | tf_op jit(solution)/shard_map/ppermute | solution.py:18
  412.7 344.6 %reduce-scatter.8.cloned.1.call-start = ((), (), s32[]{:S(2)}) async-start(), calls=%async_computation.9 | async-start | bytes 7311360 | tf_op jit(solution)/shard_map/reduce_scatter | solution.py:563
  432.7 16.7 %collective-permute-start.46 = (bf16[128,2048]{1,0:T(8,128)(2,1)S(1)}, bf16[128,2048]{1,0:T(8,128)(2,1)S(1)}, u32[]{:S(2)}, u32[]{:S(2)}) collective-permute-start(bf16[128,2048]{1,0:T(8,128)(2,1)S(1)} %pad_maximum_fusion.14), channel_id=1, source_target_pairs={{0,4},{4,0},{1,5},{5,1},{2,6},{6,2},{3,7},{7,3},{8,12},{12,8},{9,1... | collective-permute-start | bytes 1572872 | tf_op jit(solution)/shard_map/ppermute | solution.py:18
  438.4 21.5 %collective-permute-start.33 = (bf16[128,2048]{1,0:T(8,128)(2,1)S(1)}, bf16[128,2048]{1,0:T(8,128)(2,1)S(1)}, u32[]{:S(2)}, u32[]{:S(2)}) collective-permute-start(bf16[128,2048]{1,0:T(8,128)(2,1)S(1)} %pad_maximum_fusion.12), channel_id=1, source_target_pairs={{0,4},{4,0},{1,5},{5,1},{2,6},{6,2},{3,7},{7,3},{8,12},{12,8},{9,1... | collective-permute-start | bytes 1572872 | tf_op jit(solution)/shard_map/ppermute | solution.py:18
  440.0 19.9 %collective-permute-start.31 = (bf16[128,2048]{1,0:T(8,128)(2,1)S(1)}, bf16[128,2048]{1,0:T(8,128)(2,1)S(1)}, u32[]{:S(2)}, u32[]{:S(2)}) collective-permute-start(bf16[128,2048]{1,0:T(8,128)(2,1)S(1)} %pad_maximum_fusion.11), channel_id=1, source_target_pairs={{0,2},{2,0},{1,3},{3,1},{4,6},{6,4},{5,7},{7,5},{8,10},{10,8},{9,1... | collective-permute-start | bytes 1572872 | tf_op jit(solution)/shard_map/ppermute | solution.py:18
  473.8 31.1 %collective-permute-start.51 = (bf16[512,1280]{1,0:T(8,128)(2,1)}, bf16[512,1280]{1,0:T(8,128)(2,1)}, u32[]{:S(2)}, u32[]{:S(2)}) collective-permute-start(bf16[512,1280]{1,0:T(8,128)(2,1)} %convolution_convert_fusion.6), channel_id=1, source_target_pairs={{0,2},{2,0},{1,3},{3,1},{4,6},{6,4},{5,7},{7,5},{8,10},{10,8},{9,1... | collective-permute-start | bytes 3932168 | tf_op jit(solution)/shard_map/ppermute | solution.py:18
  527.6 29.8 %collective-permute-start.53 = (bf16[512,1280]{1,0:T(8,128)(2,1)S(1)}, bf16[512,1280]{1,0:T(8,128)(2,1)S(1)}, u32[]{:S(2)}, u32[]{:S(2)}) collective-permute-start(bf16[512,1280]{1,0:T(8,128)(2,1)S(1)} %convolution_convert_fusion.5), channel_id=1, source_target_pairs={{0,2},{2,0},{1,3},{3,1},{4,6},{6,4},{5,7},{7,5},{8,10},{10,8},{9,1... | collective-permute-start | bytes 3932168 | tf_op jit(solution)/shard_map/ppermute | solution.py:18
  530.8 30.4 %collective-permute-start.54 = (bf16[512,1280]{1,0:T(8,128)(2,1)S(1)}, bf16[512,1280]{1,0:T(8,128)(2,1)S(1)}, u32[]{:S(2)}, u32[]{:S(2)}) collective-permute-start(bf16[512,1280]{1,0:T(8,128)(2,1)S(1)} %fusion.15), channel_id=1, source_target_pairs={{0,4},{4,0},{1,5},{5,1},{2,6},{6,2},{3,7},{7,3},{8,12},{12,8},{9,1... | collective-permute-start | bytes 3932168 | tf_op jit(solution)/shard_map/ppermute | solution.py:18
  564.5 31.2 %collective-permute-start.64 = (bf16[128,1280]{1,0:T(8,128)(2,1)S(1)}, bf16[128,1280]{1,0:T(8,128)(2,1)S(1)}, u32[]{:S(2)}, u32[]{:S(2)}) collective-permute-start(bf16[128,1280]{1,0:T(8,128)(2,1)S(1)} %get-tuple-element.211), channel_id=1, source_target_pairs={{0,24},{8,16},{16,8},{24,0},{1,25},{9,17},{17,9},{25,1},{2,26},{10... | collective-permute-start | bytes 983048 | tf_op jit(solution)/shard_map/ppermute | solution.py:41
  564.5 40.4 %collective-permute-start.63 = (bf16[128,1280]{1,0:T(8,128)(2,1)S(1)}, bf16[128,1280]{1,0:T(8,128)(2,1)S(1)}, u32[]{:S(2)}, u32[]{:S(2)}) collective-permute-start(bf16[128,1280]{1,0:T(8,128)(2,1)S(1)} %get-tuple-element.212), channel_id=1, source_target_pairs={{0,16},{8,24},{16,0},{24,8},{1,17},{9,25},{17,1},{25,9},{2,18},{10... | collective-permute-start | bytes 983048 | tf_op jit(solution)/shard_map/ppermute | solution.py:41
  573.9 43.3 %collective-permute-start.60 = (f32[128,2048]{1,0:T(8,128)}, f32[128,2048]{1,0:T(8,128)}, u32[]{:S(2)}, u32[]{:S(2)}) collective-permute-start(f32[128,2048]{1,0:T(8,128)} %slice.381), channel_id=1, source_target_pairs={{0,1},{1,0},{2,3},{3,2},{4,5},{5,4},{6,7},{7,6},{8,9},{9,8},{10,11... | collective-permute-start | bytes 3145736 | tf_op jit(solution)/shard_map/ppermute | solution.py:18
  575.4 50.9 %collective-permute-start.56 = (bf16[512,1280]{1,0:T(8,128)(2,1)}, bf16[512,1280]{1,0:T(8,128)(2,1)}, u32[]{:S(2)}, u32[]{:S(2)}) collective-permute-start(bf16[512,1280]{1,0:T(8,128)(2,1)} %convolution_convert_fusion.3), channel_id=1, source_target_pairs={{0,4},{4,0},{1,5},{5,1},{2,6},{6,2},{3,7},{7,3},{8,12},{12,8},{9,1... | collective-permute-start | bytes 3932168 | tf_op jit(solution)/shard_map/ppermute | solution.py:18
  607.4 42.6 %collective-permute-start.55 = (bf16[512,1280]{1,0:T(8,128)(2,1)}, bf16[512,1280]{1,0:T(8,128)(2,1)}, u32[]{:S(2)}, u32[]{:S(2)}) collective-permute-start(bf16[512,1280]{1,0:T(8,128)(2,1)} %convolution_convert_fusion.4), channel_id=1, source_target_pairs={{0,4},{4,0},{1,5},{5,1},{2,6},{6,2},{3,7},{7,3},{8,12},{12,8},{9,1... | collective-permute-start | bytes 3932168 | tf_op jit(solution)/shard_map/ppermute | solution.py:18
  615.1 62.9 %collective-permute-start.59 = (bf16[256,768]{0,1:T(8,128)(2,1)}, bf16[256,768]{0,1:T(8,128)(2,1)}, u32[]{:S(2)}, u32[]{:S(2)}) collective-permute-start(bf16[256,768]{0,1:T(8,128)(2,1)} %bitcast.114), channel_id=1, source_target_pairs={{0,4},{4,0},{1,5},{5,1},{2,6},{6,2},{3,7},{7,3},{8,12},{12,8},{9,1... | collective-permute-start | bytes 1179656 | tf_op jit(solution)/shard_map/ppermute | solution.py:18
  629.3 40.4 %collective-permute-start.57 = (bf16[512,1280]{1,0:T(8,128)(2,1)}, bf16[512,1280]{1,0:T(8,128)(2,1)}, u32[]{:S(2)}, u32[]{:S(2)}) collective-permute-start(bf16[512,1280]{1,0:T(8,128)(2,1)} %fusion.16), channel_id=1, source_target_pairs={{0,2},{2,0},{1,3},{3,1},{4,6},{6,4},{5,7},{7,5},{8,10},{10,8},{9,1... | collective-permute-start | bytes 3932168 | tf_op jit(solution)/shard_map/ppermute | solution.py:18
  636.0 48.2 %collective-permute-start.58 = (bf16[256,1536]{1,0:T(8,128)(2,1)}, bf16[256,1536]{1,0:T(8,128)(2,1)}, u32[]{:S(2)}, u32[]{:S(2)}) collective-permute-start(bf16[256,1536]{1,0:T(8,128)(2,1)} %fusion.46), channel_id=1, source_target_pairs={{0,4},{4,0},{1,5},{5,1},{2,6},{6,2},{3,7},{7,3},{8,12},{12,8},{9,1... | collective-permute-start | bytes 2359304 | tf_op jit(solution)/shard_map/ppermute | solution.py:18
  685.1 77.5 %collective-permute-start.61 = (bf16[64,2048]{1,0:T(8,128)(2,1)}, bf16[64,2048]{1,0:T(8,128)(2,1)}, u32[]{:S(2)}, u32[]{:S(2)}) collective-permute-start(bf16[64,2048]{1,0:T(8,128)(2,1)} %get-tuple-element.239), channel_id=1, source_target_pairs={{0,4},{4,0},{1,5},{5,1},{2,6},{6,2},{3,7},{7,3},{8,12},{12,8},{9,1... | collective-permute-start | bytes 786440 | tf_op jit(solution)/shard_map/ppermute | solution.py:18
  686.7 30.3 %collective-permute-start.66 = (bf16[128,1280]{1,0:T(8,128)(2,1)}, bf16[128,1280]{1,0:T(8,128)(2,1)S(1)}, u32[]{:S(2)}, u32[]{:S(2)}) collective-permute-start(bf16[128,1280]{1,0:T(8,128)(2,1)} %get-tuple-element.207), channel_id=1, source_target_pairs={{0,8},{8,0},{16,24},{24,16},{1,9},{9,1},{17,25},{25,17},{2,10},{10... | collective-permute-start | bytes 983048 | tf_op jit(solution)/shard_map/ppermute | solution.py:41
  713.5 26.8 %collective-permute-start.68 = (bf16[128,1280]{1,0:T(8,128)(2,1)}, bf16[128,1280]{1,0:T(8,128)(2,1)}, u32[]{:S(2)}, u32[]{:S(2)}) collective-permute-start(bf16[128,1280]{1,0:T(8,128)(2,1)} %get-tuple-element.208), channel_id=1, source_target_pairs={{0,24},{8,16},{16,8},{24,0},{1,25},{9,17},{17,9},{25,1},{2,26},{10... | collective-permute-start | bytes 983048 | tf_op jit(solution)/shard_map/ppermute | solution.py:41
  714.3 39.2 %collective-permute-start.67 = (bf16[128,1280]{1,0:T(8,128)(2,1)}, bf16[128,1280]{1,0:T(8,128)(2,1)}, u32[]{:S(2)}, u32[]{:S(2)}) collective-permute-start(bf16[128,1280]{1,0:T(8,128)(2,1)} %get-tuple-element.209), channel_id=1, source_target_pairs={{0,16},{8,24},{16,0},{24,8},{1,17},{9,25},{17,1},{25,9},{2,18},{10... | collective-permute-start | bytes 983048 | tf_op jit(solution)/shard_map/ppermute | solution.py:41
  757.3 18.5 %collective-permute-start.70 = (bf16[80,2688]{1,0:T(8,128)(2,1)}, bf16[80,2688]{1,0:T(8,128)(2,1)S(1)}, u32[]{:S(2)}, u32[]{:S(2)}) collective-permute-start(bf16[80,2688]{1,0:T(8,128)(2,1)} %reduce-scatter.8.cloned.1.call-done), channel_id=1, source_target_pairs={{0,0},{1,16},{2,1},{3,17},{4,2},{5,18},{6,3},{7,19},{8,4},{9,20},{... | collective-permute-start | bytes 1290248 | tf_op jit(solution)/shard_map/ppermute | solution.py:564
  (105 other events, 1407.6 us)
Sparse Core Ops, SparseCore 0:
  14.9 159.9 all-gather.3
  177.0 115.4 all-gather.5
  303.5 61.1 all-gather.7
  385.5 60.5 reduce-scatter.5
  448.2 114.7 reduce-scatter.3
  568.3 188.9 reduce-scatter.7

commit v4 on v3

--- a/solution.py
+++ b/solution.py
@@ -304,7 +304,6 @@
     seqs, length, full = rec.shape
     heads = HEADS // 2
     width = full // heads
-    column = (gates.shape[1] - 640) // width
     block = pl.BlockSpec((seqs, length, width), lambda h: (0, 0, h))
     whole = pl.BlockSpec((seqs, length, full), lambda h: (0, 0, 0))
     array = jax.ShapeDtypeStruct(rec.shape, F32)
@@ -315,8 +314,8 @@
             block,
             pl.BlockSpec((seqs, 8, width), lambda h: (0, 0, h)),
             pl.BlockSpec((8, width), lambda h: (0, h)),
-            pl.BlockSpec((width, width), lambda h: (h, column)),
-            pl.BlockSpec((width, width), lambda h: (h, column + 1)),
+            pl.BlockSpec((width, width), lambda h: (h, 0)),
+            pl.BlockSpec((width, width), lambda h: (h, 1)),
         ],
         out_specs=[block, block, block, whole, whole, whole],
         out_shape=[array] * 6,
@@ -341,7 +340,6 @@
     seqs, length, full = rec.shape
     heads = HEADS // 2
     width = full // heads
-    column = (gates.shape[1] - 640) // width
     block = pl.BlockSpec((seqs, length, width), lambda h: (0, 0, h))
     row = pl.BlockSpec((seqs, width), lambda h: (0, h))
     weight = pl.BlockSpec((width, width), lambda h: (h, 0))
@@ -361,8 +359,8 @@
             block,
             pl.BlockSpec((seqs, 8, width), lambda h: (0, 0, h)),
             pl.BlockSpec((8, width), lambda h: (0, h)),
-            pl.BlockSpec((width, width), lambda h: (h, column)),
-            pl.BlockSpec((width, width), lambda h: (h, column + 1)),
+            pl.BlockSpec((width, width), lambda h: (h, 0)),
+            pl.BlockSpec((width, width), lambda h: (h, 1)),
         ],
         out_specs=[block, weight, weight, pl.BlockSpec((8, width), lambda h: (0, h))],
         out_shape=[
@@ -443,16 +441,17 @@
         (branch_shard, recur_in_shard, w_recur_out, w_rgate, w_gate, w_up, w_down, norm_gain)
     )
 
-    gains = jnp.stack([norm_gain, mlp_gain]).reshape(1, -1)
+    vectors = jnp.concatenate(
+        [conv_weight, conv_bias[None], rgate_bias[None], igate_bias[None], rate_param[None]]
+    )
+    gains = jnp.concatenate([norm_gain, mlp_gain, vectors.reshape(-1)]).reshape(1, -1)
     gains = lax.all_to_all(jnp.tile(gains, (devices, 1)), EVERY, 0, 0, tiled=True)
+    gains, vectors = gains[:, : 2 * norm_gain.shape[0]], gains[:, 2 * norm_gain.shape[0] :]
     gains = jnp.swapaxes(gains.reshape(devices, 2, -1), 0, 1).reshape(2, width).astype(F32)
     ngain, mgain = gains[0], gains[1]
-
-    vectors = jnp.concatenate(
-        [conv_weight, conv_bias[None], rgate_bias[None], igate_bias[None], rate_param[None]]
-    )
-    vectors = jnp.pad(vectors.T, ((0, 0), (0, 120)))
-    out_gates = jnp.concatenate([w_recur_out, w_rgate, w_igate, vectors], axis=1)
+    vectors = jnp.swapaxes(vectors.reshape(devices, 8, -1), 0, 1).reshape(8, 2, channels)
+
+    out_gates = jnp.concatenate([w_recur_out, w_rgate, w_igate], axis=1)
     out_gates = lax.all_gather(out_gates, EVERY, axis=0, tiled=True)
     out_gates = pick(out_gates.reshape(2, channels, -1), c, 0)
     out_full, gates = out_gates[:, :width], out_gates[:, width:]
@@ -468,7 +467,7 @@
     down = w_down.reshape(2, units, -1)
     down_shard = ordered(first_y, pick(down, y, 0), swap(pick(down, 1 - y, 0), "y"), 1)
 
-    vec = gates[:, 512:520].T.astype(F32)
+    vec = pick(vectors, c, 1).astype(F32)
     rate = vec[7]
     eight = -8.0 * jax.nn.softplus(rate)
     vec = jnp.concatenate([vec[:7], eight[None]])

time: 796 us -> 780 us (0.980)
  local copies, waits for them, and re-layouts: 124 us -> 113 us
    ppermute x53, waiting for transfers between devices: 210 us -> 201 us  [swap(): return lax.ppermute(value, axis, PAIR)]
    unnamed x160 -> x152, local copies, waits for them, and re-layouts: 37.3 us -> 32.3 us
  transfers between devices with their start and end apart: 84 -> 84, of which waited for: 38 -> 39; matrix products, arithmetic and copies ran while one was open for 31% -> 30% of each run, Pallas kernels for 3% -> 3%
where the time goes in v4:
time: 780 us; the launch traced here: 771 us
  waiting for transfers between devices  355 us (46%)
  local copies, waits for them, and re-layouts  113 us (14%)
  starting transfers between devices  106 us (14%)
  matrix products  94.2 us (12%)
  other arithmetic  61.8 us (8%)
  Pallas kernels  24.1 us (3%)
  between operations  15.7 us (2%)
    ppermute x53, waiting for transfers between devices, swap(): return lax.ppermute(value, axis, PAIR)  201 us
    ppermute x15, waiting for transfers between devices, z_send(): return lax.ppermute(value, 'z', [(s, s ^ j) for s in range(count)])  86 us
    ppermute x53, starting transfers between devices, swap(): return lax.ppermute(value, axis, PAIR)  48.5 us
    dot_general x11, matrix products, outer_sum(): lax.dot_general(left, right, (((0,), (0,)), ((), ())), preferred_element_...  35.7 us
    dot_general x5, matrix products, mm(): return jnp.dot(left, right, preferred_element_type=F32)  33 us
    unnamed x152, local copies, waits for them, and re-layouts  32.3 us
    ppermute x15, starting transfers between devices, z_send(): return lax.ppermute(value, 'z', [(s, s ^ j) for s in range(count)])  26.5 us
    dot_general x5, matrix products, mm_rows(): lax.dot_general(left, weight, (((1,), (1,)), ((), ())), preferred_element...  25.5 us
  transfers between devices with their start and end apart: 84, of which 39 were waited for; matrix products, arithmetic and copies ran while one was open for 30% of the time, Pallas kernels for 3%

profile of v4, /device:TPU:10, one launch (start us, length us, event | category | flops | bytes accessed | tf_op | source)
XLA Modules:
  0.0 770.7 jit_solution(14343136876812083551)
XLA Ops:
  27.6 6.3 all-to-all-start
  41.2 23.5 %all-to-all-done = bf16[32,2,384]{2,1,0:T(2,128)(2,1)S(1)} async-done(((bf16[32,2,384]{2,1,0:T(2,128)(2,1)}), bf16[32,2,384]{2,1,0:T(2,128)(2,1)S(1)}, u32[]{:S(2)}, u32[]{:S(2)}) %all-to-all-start) | async-done | bytes 49184 | tf_op jit(solution)/shard_map/all_to_all | solution.py:448
  70.3 4.9 fusion.55
  88.1 12.3 %collective-permute-done.15 = bf16[128,1280]{1,0:T(8,128)(2,1)} collective-permute-done((bf16[128,1280]{1,0:T(8,128)(2,1)S(1)}, bf16[128,1280]{1,0:T(8,128)(2,1)}, u32[]{:S(2)}, u32[]{:S(2)}) %collective-permute-start.15) | collective-permute-done | bytes 327712 | tf_op jit(solution)/shard_map/ppermute | solution.py:41
  103.5 7.6 collective-permute-done.16
  131.7 32.5 %collective-permute-done.7 = bf16[512,1280]{1,0:T(8,128)(2,1)} collective-permute-done((bf16[512,1280]{1,0:T(8,128)(2,1)}, bf16[512,1280]{1,0:T(8,128)(2,1)}, u32[]{:S(2)}, u32[]{:S(2)}) %collective-permute-start.7) | collective-permute-done | bytes 1310752 | tf_op jit(solution)/shard_map/ppermute | solution.py:18
  168.5 23.8 %collective-permute-done.18 = bf16[512,1280]{1,0:T(8,128)(2,1)} collective-permute-done((bf16[512,1280]{1,0:T(8,128)(2,1)}, bf16[512,1280]{1,0:T(8,128)(2,1)}, u32[]{:S(2)}, u32[]{:S(2)}) %collective-permute-start.18) | collective-permute-done | bytes 1310752 | tf_op jit(solution)/shard_map/ppermute | solution.py:18
  196.4 23.8 %collective-permute-done.9 = bf16[512,1280]{1,0:T(8,128)(2,1)S(1)} collective-permute-done((bf16[512,1280]{1,0:T(8,128)(2,1)}, bf16[512,1280]{1,0:T(8,128)(2,1)S(1)}, u32[]{:S(2)}, u32[]{:S(2)}) %collective-permute-start.9) | collective-permute-done | bytes 1310752 | tf_op jit(solution)/shard_map/ppermute | solution.py:18
  223.8 3.4 collective-permute-start.10
  227.3 3.3 dynamic-slice_bitcast_fusion
  235.0 9.5 %recur_forward.1 = (f32[2,128,1280]{2,1,0:T(8,128)}, f32[2,128,1280]{2,1,0:T(8,128)}, f32[2,128,1280]{2,1,0:T(8,128)}, f32[2,128,1280]{2,1,0:T(8,128)}, f32[2,12...) custom-call(f32[2,128,1280]{2,1,0:T(8,128)} %bitcast.183, f32[2,8,1280]{2,1,0:T(8,128)} %copy-done.33, ...), custom_call_target="tpu_custom_call" | custom-call | flops 335544320 | bytes 9175040 | tf_op jit(solution)/shard_map/recur_forward/pallas_call | solution.py:310
  258.2 5.9 fusion.30
  269.8 5.9 collective-permute-done.39
  285.7 9.9 %collective-permute-done.23 = bf16[128,2048]{1,0:T(8,128)(2,1)S(1)} collective-permute-done((bf16[128,2048]{1,0:T(8,128)(2,1)}, bf16[128,2048]{1,0:T(8,128)(2,1)S(1)}, u32[]{:S(2)}, u32[]{:S(2)}) %collective-permute-start.23) | collective-permute-done | bytes 524320 | tf_op jit(solution)/shard_map/ppermute | solution.py:18
  318.7 11.8 %fusion.97 = f32[1024,1536]{1,0:T(8,128)} fusion(bf16[1024,2048]{1,0:T(8,128)(2,1)} %constant_dynamic-update-slice_fusion, bf16[2048,1536]{0,1:T(8,128)(2,1)} %all-gather.6.cloned.1.call-done), kind=kOutput, calls=%fused_computation.280 | convolution fusion | flops 6442450944 | bytes 16777216 | tf_op jit(solution)/shard_map/dot_general | solution.py:387
  330.5 20.7 %all-gather.8.cloned.1.call-done = bf16[2048,768]{0,1:T(8,128)(2,1)} async-done(((bf16[512,768]{0,1:T(8,128)(2,1)}), bf16[2048,768]{0,1:T(8,128)(2,1)}) %all-gather.8.cloned.1.call-update) | async-done | bytes 3145744 | tf_op jit(solution)/shard_map/all_gather | solution.py:486
  351.2 12.2 %fusion.14 = (bf16[1024,768]{1,0:T(8,128)(2,1)}, bf16[1024,768]{1,0:T(8,128)(2,1)}, bf16[1024,768]{1,0:T(8,128)(2,1)S(1)}) fusion(f32[1024,1536]{1,0:T(8,128)} %fusion.97, bf16[1024,2048]{1,0:T(8,128)(2,1)} %constant_dynamic-update-slice_fusion.7, bf16[2048,768]{0,1:T(8,128)(2,1)} %all-gather.8.cloned.1.call-done), kind=kOutput, calls=%fused_computation.29 | convolution fusion | flops 3241672704 | bytes 18350080 | tf_op jit(solution)/shard_map/dot_general | solution.py:387
  364.5 4.9 convolution_convert_fusion.2
  369.7 9.7 %fusion.17 = f32[1024,2048]{1,0:T(8,128)S(1)} fusion(bf16[2048,1536]{0,1:T(8,128)(2,1)} %all-gather.6.cloned.1.call-done, bf16[1024,768]{1,0:T(8,128)(2,1)} %get-tuple-element.182, bf16[1024,768]{1,0:T(8,128)(2,1)} %get-tuple-element.181), kind=kOutput, calls=%fused_computation.42 | convolution fusion | flops 6448742400 | bytes 17825792 | tf_op jit(solution)/shard_map/dot_general | solution.py:391
  379.4 3.3 copy-done.11
  385.4 11.3 %convolution_convert_fusion.1 = bf16[2048,1536]{1,0:T(8,128)(2,1)} fusion(bf16[1024,2048]{1,0:T(8,128)(2,1)} %constant_dynamic-update-slice_fusion, bf16[1024,768]{1,0:T(8,128)(2,1)S(1)} %copy-done.57, bf16[1024,768]{1,0:T(8,128)(2,1)S(1)} %copy-done.56), kind=kOutput, calls=%fused_computation.3 | convolution fusion | flops 6451888128 | bytes 13631488 | tf_op jit(solution)/shard_map/dot_general | solution.py:395
  396.8 5.8 fusion.98
  403.0 3.7 fusion.91
  412.2 3.9 collective-permute-done.45
  425.5 7.9 %collective-permute-done.46 = bf16[128,2048]{1,0:T(8,128)(2,1)S(1)} collective-permute-done((bf16[128,2048]{1,0:T(8,128)(2,1)S(1)}, bf16[128,2048]{1,0:T(8,128)(2,1)S(1)}, u32[]{:S(2)}, u32[]{:S(2)}) %collective-permute-start.46) | collective-permute-done | bytes 524320 | tf_op jit(solution)/shard_map/ppermute | solution.py:18
  433.9 10.0 %collective-permute-done.33 = bf16[128,2048]{1,0:T(8,128)(2,1)S(1)} collective-permute-done((bf16[128,2048]{1,0:T(8,128)(2,1)S(1)}, bf16[128,2048]{1,0:T(8,128)(2,1)S(1)}, u32[]{:S(2)}, u32[]{:S(2)}) %collective-permute-start.33) | collective-permute-done | bytes 524320 | tf_op jit(solution)/shard_map/ppermute | solution.py:18
  448.6 6.9 fusion.25
  458.6 5.1 recur_reverse.1
  466.3 5.1 collective-permute-start.48
  471.4 5.0 convolution_convert_fusion
  477.1 11.2 %collective-permute-done.51 = bf16[512,1280]{1,0:T(8,128)(2,1)} collective-permute-done((bf16[512,1280]{1,0:T(8,128)(2,1)}, bf16[512,1280]{1,0:T(8,128)(2,1)}, u32[]{:S(2)}, u32[]{:S(2)}) %collective-permute-start.51) | collective-permute-done | bytes 1310752 | tf_op jit(solution)/shard_map/ppermute | solution.py:18
  488.2 9.4 %recur_backward.1 = (f32[2,128,1280]{2,1,0:T(8,128)}, f32[1280,256]{1,0:T(8,128)}, f32[1280,256]{1,0:T(8,128)}, f32[8,1280]{1,0:T(8,128)}) custom-call(f32[2,128,1280]{2,1,0:T(8,128)} %get-tuple-element.64.l_ref, f32[2,128,1280]{2,1,0:T(8,128)} %get-tuple-element.65.q_ref, f32[2,1280]{1,0:T(2,128)} %fusion.67.e_ref, ...), custom_call_target="tpu_custom_call" | custom-call | flops 671088640 | bytes 13107200 | tf_op jit(solution)/shard_map/recur_backward/pallas_call | solution.py:346
  502.3 5.9 fusion.1
  517.6 4.8 collective-permute-start.52
  522.5 5.1 collective-permute-done.52
  528.1 12.1 %collective-permute-done.53 = bf16[512,1280]{1,0:T(8,128)(2,1)S(1)} collective-permute-done((bf16[512,1280]{1,0:T(8,128)(2,1)S(1)}, bf16[512,1280]{1,0:T(8,128)(2,1)S(1)}, u32[]{:S(2)}, u32[]{:S(2)}) %collective-permute-start.53) | collective-permute-done | bytes 1310752 | tf_op jit(solution)/shard_map/ppermute | solution.py:18
  540.2 3.8 collective-permute-done.54
  559.2 18.8 %collective-permute-done.64 = bf16[128,1280]{1,0:T(8,128)(2,1)S(1)} collective-permute-done((bf16[128,1280]{1,0:T(8,128)(2,1)S(1)}, bf16[128,1280]{1,0:T(8,128)(2,1)S(1)}, u32[]{:S(2)}, u32[]{:S(2)}) %collective-permute-start.64) | collective-permute-done | bytes 327712 | tf_op jit(solution)/shard_map/ppermute | solution.py:41
  578.0 9.5 %collective-permute-done.63 = bf16[128,1280]{1,0:T(8,128)(2,1)S(1)} collective-permute-done((bf16[128,1280]{1,0:T(8,128)(2,1)S(1)}, bf16[128,1280]{1,0:T(8,128)(2,1)S(1)}, u32[]{:S(2)}, u32[]{:S(2)}) %collective-permute-start.63) | collective-permute-done | bytes 327712 | tf_op jit(solution)/shard_map/ppermute | solution.py:41
  620.8 10.4 %collective-permute-done.55 = bf16[512,1280]{1,0:T(8,128)(2,1)} collective-permute-done((bf16[512,1280]{1,0:T(8,128)(2,1)}, bf16[512,1280]{1,0:T(8,128)(2,1)}, u32[]{:S(2)}, u32[]{:S(2)}) %collective-permute-start.55) | collective-permute-done | bytes 1310752 | tf_op jit(solution)/shard_map/ppermute | solution.py:18
  631.2 21.4 %collective-permute-done.57 = bf16[512,1280]{1,0:T(8,128)(2,1)} collective-permute-done((bf16[512,1280]{1,0:T(8,128)(2,1)}, bf16[512,1280]{1,0:T(8,128)(2,1)}, u32[]{:S(2)}, u32[]{:S(2)}) %collective-permute-start.57) | collective-permute-done | bytes 1310752 | tf_op jit(solution)/shard_map/ppermute | solution.py:18
  652.6 3.9 fusion.7
  659.6 5.9 collective-permute-done.58
  670.6 4.8 collective-permute-start.66
  699.5 24.4 %collective-permute-done.68 = bf16[128,1280]{1,0:T(8,128)(2,1)S(1)} collective-permute-done((bf16[128,1280]{1,0:T(8,128)(2,1)S(1)}, bf16[128,1280]{1,0:T(8,128)(2,1)S(1)}, u32[]{:S(2)}, u32[]{:S(2)}) %collective-permute-start.68) | collective-permute-done | bytes 327712 | tf_op jit(solution)/shard_map/ppermute | solution.py:41
  723.9 11.3 %collective-permute-done.67 = bf16[128,1280]{1,0:T(8,128)(2,1)S(1)} collective-permute-done((bf16[128,1280]{1,0:T(8,128)(2,1)S(1)}, bf16[128,1280]{1,0:T(8,128)(2,1)S(1)}, u32[]{:S(2)}, u32[]{:S(2)}) %collective-permute-start.67) | collective-permute-done | bytes 327712 | tf_op jit(solution)/shard_map/ppermute | solution.py:41
  737.1 4.8 reduce-scatter.8.cloned.1.call-done
  747.9 12.8 %collective-permute-done.70 = bf16[80,2688]{1,0:T(8,128)(2,1)S(1)} collective-permute-done((bf16[80,2688]{1,0:T(8,128)(2,1)}, bf16[80,2688]{1,0:T(8,128)(2,1)S(1)}, u32[]{:S(2)}, u32[]{:S(2)}) %collective-permute-start.70) | collective-permute-done | bytes 430112 | tf_op jit(solution)/shard_map/ppermute | solution.py:563
  (461 shorter events, 274.9 us)
Async XLA Ops:
  7.2 220.1 %all-gather.4.cloned.1.call-start = ((), (), s32[]{:S(2)}) async-start(), calls=%async_computation.4 | async-start | bytes 13516800 | tf_op jit(solution)/shard_map/all_gather | solution.py:455
  16.5 50.1 %collective-permute-start = (bf16[64,2048]{1,0:T(8,128)(2,1)}, bf16[64,2048]{1,0:T(8,128)(2,1)S(1)}, u32[]{:S(2)}, u32[]{:S(2)}) collective-permute-start(bf16[64,2048]{1,0:T(8,128)(2,1)} %get-tuple-element.221), channel_id=1, source_target_pairs={{0,4},{4,0},{1,5},{5,1},{2,6},{6,2},{3,7},{7,3},{8,12},{12,8},{9,1... | collective-permute-start | bytes 786440 | tf_op jit(solution)/shard_map/ppermute | solution.py:18
  19.8 64.5 %collective-permute-start.35 = (bf16[64,2048]{1,0:T(8,128)(2,1)}, bf16[64,2048]{1,0:T(8,128)(2,1)}, u32[]{:S(2)}, u32[]{:S(2)}) collective-permute-start(bf16[64,2048]{1,0:T(8,128)(2,1)} %get-tuple-element.217), channel_id=1, source_target_pairs={{0,4},{4,0},{1,5},{5,1},{2,6},{6,2},{3,7},{7,3},{8,12},{12,8},{9,1... | collective-permute-start | bytes 786440 | tf_op jit(solution)/shard_map/ppermute | solution.py:18
  21.3 59.9 %collective-permute-start.6 = (bf16[128,1280]{1,0:T(8,128)(2,1)}, bf16[128,1280]{1,0:T(8,128)(2,1)}, u32[]{:S(2)}, u32[]{:S(2)}) collective-permute-start(bf16[128,1280]{1,0:T(8,128)(2,1)} %maximum_select_fusion.11), channel_id=1, source_target_pairs={{0,24},{8,16},{16,8},{24,0},{1,25},{9,17},{17,9},{25,1},{2,26},{10... | collective-permute-start | bytes 983048 | tf_op jit(solution)/shard_map/ppermute | solution.py:41
  22.9 55.1 %collective-permute-start.5 = (bf16[128,1280]{1,0:T(8,128)(2,1)}, bf16[128,1280]{1,0:T(8,128)(2,1)}, u32[]{:S(2)}, u32[]{:S(2)}) collective-permute-start(bf16[128,1280]{1,0:T(8,128)(2,1)} %maximum_select_fusion.11), channel_id=1, source_target_pairs={{0,16},{8,24},{16,0},{24,8},{1,17},{9,25},{17,1},{25,9},{2,18},{10... | collective-permute-start | bytes 983048 | tf_op jit(solution)/shard_map/ppermute | solution.py:41
  24.1 51.0 %collective-permute-start.4 = (bf16[128,1280]{1,0:T(8,128)(2,1)}, bf16[128,1280]{1,0:T(8,128)(2,1)}, u32[]{:S(2)}, u32[]{:S(2)}) collective-permute-start(bf16[128,1280]{1,0:T(8,128)(2,1)} %maximum_select_fusion.11), channel_id=1, source_target_pairs={{0,8},{8,0},{16,24},{24,16},{1,9},{9,1},{17,25},{25,17},{2,10},{10... | collective-permute-start | bytes 983048 | tf_op jit(solution)/shard_map/ppermute | solution.py:41
  27.6 37.1 %all-to-all-start = ((bf16[32,2,384]{2,1,0:T(2,128)(2,1)}), bf16[32,2,384]{2,1,0:T(2,128)(2,1)S(1)}, u32[]{:S(2)}, u32[]{:S(2)}) async-start(bf16[32,2,384]{2,1,0:T(2,128)(2,1)} %reshape.316), calls=%async_computation | async-start | bytes 98304 | tf_op jit(solution)/shard_map/all_to_all | solution.py:448
  33.9 284.8 %all-gather.6.cloned.1.call-start = ((), (), s32[]{:S(2)}) async-start(), calls=%async_computation.5 | async-start | bytes 7864320 | tf_op jit(solution)/shard_map/all_gather | solution.py:466
  66.6 47.8 %collective-permute-start.17 = (bf16[128,1280]{1,0:T(8,128)(2,1)S(1)}, bf16[128,1280]{1,0:T(8,128)(2,1)}, u32[]{:S(2)}, u32[]{:S(2)}) collective-permute-start(bf16[128,1280]{1,0:T(8,128)(2,1)S(1)} %copy-done.24), channel_id=1, source_target_pairs={{0,24},{8,16},{16,8},{24,0},{1,25},{9,17},{17,9},{25,1},{2,26},{10... | collective-permute-start | bytes 983048 | tf_op jit(solution)/shard_map/ppermute | solution.py:41
  75.1 35.9 %collective-permute-start.16 = (bf16[128,1280]{1,0:T(8,128)(2,1)S(1)}, bf16[128,1280]{1,0:T(8,128)(2,1)}, u32[]{:S(2)}, u32[]{:S(2)}) collective-permute-start(bf16[128,1280]{1,0:T(8,128)(2,1)S(1)} %copy-done.24), channel_id=1, source_target_pairs={{0,16},{8,24},{16,0},{24,8},{1,17},{9,25},{17,1},{25,9},{2,18},{10... | collective-permute-start | bytes 983048 | tf_op jit(solution)/shard_map/ppermute | solution.py:41
  78.0 22.5 %collective-permute-start.15 = (bf16[128,1280]{1,0:T(8,128)(2,1)S(1)}, bf16[128,1280]{1,0:T(8,128)(2,1)}, u32[]{:S(2)}, u32[]{:S(2)}) collective-permute-start(bf16[128,1280]{1,0:T(8,128)(2,1)S(1)} %copy-done.24), channel_id=1, source_target_pairs={{0,8},{8,0},{16,24},{24,16},{1,9},{9,1},{17,25},{25,17},{2,10},{10... | collective-permute-start | bytes 983048 | tf_op jit(solution)/shard_map/ppermute | solution.py:41
  81.2 36.3 %collective-permute-start.28 = (bf16[256,1536]{0,1:T(8,128)(2,1)}, bf16[256,1536]{0,1:T(8,128)(2,1)}, u32[]{:S(2)}, u32[]{:S(2)}) collective-permute-start(bf16[256,1536]{0,1:T(8,128)(2,1)} %bitcast.25), channel_id=1, source_target_pairs={{0,4},{4,0},{1,5},{5,1},{2,6},{6,2},{3,7},{7,3},{8,12},{12,8},{9,1... | collective-permute-start | bytes 2359304 | tf_op jit(solution)/shard_map/ppermute | solution.py:18
  84.3 42.4 %collective-permute-start.8 = (bf16[512,1280]{1,0:T(8,128)(2,1)}, bf16[512,1280]{1,0:T(8,128)(2,1)}, u32[]{:S(2)}, u32[]{:S(2)}) collective-permute-start(bf16[512,1280]{1,0:T(8,128)(2,1)} %constant_dynamic-update-slice_fusion.28), channel_id=1, source_target_pairs={{0,2},{2,0},{1,3},{3,1},{4,6},{6,4},{5,7},{7,5},{8,10},{10,8},{9,1... | collective-permute-start | bytes 3932168 | tf_op jit(solution)/shard_map/ppermute | solution.py:18
  100.5 28.1 %collective-permute-start.14 = (bf16[768,256]{1,0:T(8,128)(2,1)}, bf16[768,256]{1,0:T(8,128)(2,1)S(1)}, u32[]{:S(2)}, u32[]{:S(2)}) collective-permute-start(bf16[768,256]{1,0:T(8,128)(2,1)} %get-tuple-element.210), channel_id=1, source_target_pairs={{0,4},{4,0},{1,5},{5,1},{2,6},{6,2},{3,7},{7,3},{8,12},{12,8},{9,1... | collective-permute-start | bytes 1179656 | tf_op jit(solution)/shard_map/ppermute | solution.py:18
  111.1 53.1 %collective-permute-start.7 = (bf16[512,1280]{1,0:T(8,128)(2,1)}, bf16[512,1280]{1,0:T(8,128)(2,1)}, u32[]{:S(2)}, u32[]{:S(2)}) collective-permute-start(bf16[512,1280]{1,0:T(8,128)(2,1)} %constant_dynamic-update-slice_fusion.28), channel_id=1, source_target_pairs={{0,4},{4,0},{1,5},{5,1},{2,6},{6,2},{3,7},{7,3},{8,12},{12,8},{9,1... | collective-permute-start | bytes 3932168 | tf_op jit(solution)/shard_map/ppermute | solution.py:18
  116.2 77.6 %collective-permute-start.19 = (bf16[512,1280]{1,0:T(8,128)(2,1)}, bf16[512,1280]{1,0:T(8,128)(2,1)}, u32[]{:S(2)}, u32[]{:S(2)}) collective-permute-start(bf16[512,1280]{1,0:T(8,128)(2,1)} %constant_dynamic-update-slice_fusion.20), channel_id=1, source_target_pairs={{0,2},{2,0},{1,3},{3,1},{4,6},{6,4},{5,7},{7,5},{8,10},{10,8},{9,1... | collective-permute-start | bytes 3932168 | tf_op jit(solution)/shard_map/ppermute | solution.py:18
  117.5 74.8 %collective-permute-start.18 = (bf16[512,1280]{1,0:T(8,128)(2,1)}, bf16[512,1280]{1,0:T(8,128)(2,1)}, u32[]{:S(2)}, u32[]{:S(2)}) collective-permute-start(bf16[512,1280]{1,0:T(8,128)(2,1)} %constant_dynamic-update-slice_fusion.20), channel_id=1, source_target_pairs={{0,4},{4,0},{1,5},{5,1},{2,6},{6,2},{3,7},{7,3},{8,12},{12,8},{9,1... | collective-permute-start | bytes 3932168 | tf_op jit(solution)/shard_map/ppermute | solution.py:18
  122.5 228.7 %all-gather.8.cloned.1.call-start = ((), (), s32[]{:S(2)}) async-start(), calls=%async_computation.6 | async-start | bytes 3932160 | tf_op jit(solution)/shard_map/all_gather | solution.py:486
  126.7 93.5 %collective-permute-start.9 = (bf16[512,1280]{1,0:T(8,128)(2,1)}, bf16[512,1280]{1,0:T(8,128)(2,1)S(1)}, u32[]{:S(2)}, u32[]{:S(2)}) collective-permute-start(bf16[512,1280]{1,0:T(8,128)(2,1)} %collective-permute-done.8), channel_id=1, source_target_pairs={{0,4},{4,0},{1,5},{5,1},{2,6},{6,2},{3,7},{7,3},{8,12},{12,8},{9,1... | collective-permute-start | bytes 3932168 | tf_op jit(solution)/shard_map/ppermute | solution.py:18
  128.6 138.3 %collective-permute-start.37 = (bf16[128,2048]{1,0:T(8,128)(2,1)}, bf16[128,2048]{1,0:T(8,128)(2,1)S(1)}, u32[]{:S(2)}, u32[]{:S(2)}) collective-permute-start(bf16[128,2048]{1,0:T(8,128)(2,1)} %get-tuple-element.172), channel_id=1, source_target_pairs={{0,4},{4,0},{1,5},{5,1},{2,6},{6,2},{3,7},{7,3},{8,12},{12,8},{9,1... | collective-permute-start | bytes 1572872 | tf_op jit(solution)/shard_map/ppermute | solution.py:18
  164.2 103.3 %collective-permute-start.36 = (bf16[128,2048]{1,0:T(8,128)(2,1)}, bf16[128,2048]{1,0:T(8,128)(2,1)S(1)}, u32[]{:S(2)}, u32[]{:S(2)}) collective-permute-start(bf16[128,2048]{1,0:T(8,128)(2,1)} %get-tuple-element.172), channel_id=1, source_target_pairs={{0,2},{2,0},{1,3},{3,1},{4,6},{6,4},{5,7},{7,5},{8,10},{10,8},{9,1... | collective-permute-start | bytes 1572872 | tf_op jit(solution)/shard_map/ppermute | solution.py:18
  192.3 28.1 %collective-permute-start.3 = (bf16[128,2048]{0,1:T(8,128)(2,1)S(1)}, bf16[128,2048]{0,1:T(8,128)(2,1)S(1)}, u32[]{:S(2)}, u32[]{:S(2)}) collective-permute-start(bf16[128,2048]{0,1:T(8,128)(2,1)S(1)} %bitcast.156), channel_id=1, source_target_pairs={{0,1},{1,0},{2,3},{3,2},{4,5},{5,4},{6,7},{7,6},{8,9},{9,8},{10,11... | collective-permute-start | bytes 1572872 | tf_op jit(solution)/shard_map/ppermute | solution.py:18
  193.8 58.0 %collective-permute-start.20 = (bf16[512,1280]{1,0:T(8,128)(2,1)}, bf16[512,1280]{1,0:T(8,128)(2,1)}, u32[]{:S(2)}, u32[]{:S(2)}) collective-permute-start(bf16[512,1280]{1,0:T(8,128)(2,1)} %collective-permute-done.18), channel_id=1, source_target_pairs={{0,2},{2,0},{1,3},{3,1},{4,6},{6,4},{5,7},{7,5},{8,10},{10,8},{9,1... | collective-permute-start | bytes 3932168 | tf_op jit(solution)/shard_map/ppermute | solution.py:18
  278.2 30.9 %collective-permute-start.41 = (bf16[384,2048]{1,0:T(8,128)(2,1)}, bf16[384,2048]{1,0:T(8,128)(2,1)}, u32[]{:S(2)}, u32[]{:S(2)}) collective-permute-start(bf16[384,2048]{1,0:T(8,128)(2,1)} %pad_maximum_fusion.5), channel_id=1, source_target_pairs={{0,1},{1,0},{2,3},{3,2},{4,5},{5,4},{6,7},{7,6},{8,9},{9,8},{10,11... | collective-permute-start | bytes 4718600 | tf_op jit(solution)/shard_map/ppermute | solution.py:18
  283.6 23.6 %collective-permute-start.40 = (bf16[128,2048]{1,0:T(8,128)(2,1)}, bf16[128,2048]{1,0:T(8,128)(2,1)}, u32[]{:S(2)}, u32[]{:S(2)}) collective-permute-start(bf16[128,2048]{1,0:T(8,128)(2,1)} %get-tuple-element.172), channel_id=1, source_target_pairs={{0,1},{1,0},{2,3},{3,2},{4,5},{5,4},{6,7},{7,6},{8,9},{9,8},{10,11... | collective-permute-start | bytes 1572872 | tf_op jit(solution)/shard_map/ppermute | solution.py:18
  284.5 307.6 %reduce-scatter.6.cloned.1.call-start = ((), (), s32[]{:S(2)}) async-start(), calls=%async_computation.8 | async-start | bytes 3932160 | tf_op jit(solution)/shard_map/reduce_scatter | solution.py:509
  369.4 246.3 %reduce-scatter.4.cloned.1.call-start = ((), (), s32[]{:S(2)}) async-start(), calls=%async_computation.7 | async-start | bytes 7864320 | tf_op jit(solution)/shard_map/reduce_scatter | solution.py:506
  384.4 18.6 %collective-permute-start.42 = (bf16[512,2048]{1,0:T(8,128)(2,1)}, bf16[512,2048]{1,0:T(8,128)(2,1)}, u32[]{:S(2)}, u32[]{:S(2)}) collective-permute-start(bf16[512,2048]{1,0:T(8,128)(2,1)} %slice.544), channel_id=1, source_target_pairs={{0,1},{1,0},{2,3},{3,2},{4,5},{5,4},{6,7},{7,6},{8,9},{9,8},{10,11... | collective-permute-start | bytes 6291464 | tf_op jit(solution)/shard_map/ppermute | solution.py:18
  396.7 345.2 %reduce-scatter.8.cloned.1.call-start = ((), (), s32[]{:S(2)}) async-start(), calls=%async_computation.9 | async-start | bytes 7311360 | tf_op jit(solution)/shard_map/reduce_scatter | solution.py:562
  416.7 16.7 %collective-permute-start.46 = (bf16[128,2048]{1,0:T(8,128)(2,1)S(1)}, bf16[128,2048]{1,0:T(8,128)(2,1)S(1)}, u32[]{:S(2)}, u32[]{:S(2)}) collective-permute-start(bf16[128,2048]{1,0:T(8,128)(2,1)S(1)} %pad_maximum_fusion.14), channel_id=1, source_target_pairs={{0,4},{4,0},{1,5},{5,1},{2,6},{6,2},{3,7},{7,3},{8,12},{12,8},{9,1... | collective-permute-start | bytes 1572872 | tf_op jit(solution)/shard_map/ppermute | solution.py:18
  422.3 21.6 %collective-permute-start.33 = (bf16[128,2048]{1,0:T(8,128)(2,1)S(1)}, bf16[128,2048]{1,0:T(8,128)(2,1)S(1)}, u32[]{:S(2)}, u32[]{:S(2)}) collective-permute-start(bf16[128,2048]{1,0:T(8,128)(2,1)S(1)} %pad_maximum_fusion.12), channel_id=1, source_target_pairs={{0,4},{4,0},{1,5},{5,1},{2,6},{6,2},{3,7},{7,3},{8,12},{12,8},{9,1... | collective-permute-start | bytes 1572872 | tf_op jit(solution)/shard_map/ppermute | solution.py:18
  423.9 20.0 %collective-permute-start.31 = (bf16[128,2048]{1,0:T(8,128)(2,1)S(1)}, bf16[128,2048]{1,0:T(8,128)(2,1)S(1)}, u32[]{:S(2)}, u32[]{:S(2)}) collective-permute-start(bf16[128,2048]{1,0:T(8,128)(2,1)S(1)} %pad_maximum_fusion.11), channel_id=1, source_target_pairs={{0,2},{2,0},{1,3},{3,1},{4,6},{6,4},{5,7},{7,5},{8,10},{10,8},{9,1... | collective-permute-start | bytes 1572872 | tf_op jit(solution)/shard_map/ppermute | solution.py:18
  457.1 31.2 %collective-permute-start.51 = (bf16[512,1280]{1,0:T(8,128)(2,1)}, bf16[512,1280]{1,0:T(8,128)(2,1)}, u32[]{:S(2)}, u32[]{:S(2)}) collective-permute-start(bf16[512,1280]{1,0:T(8,128)(2,1)} %convolution_convert_fusion.6), channel_id=1, source_target_pairs={{0,2},{2,0},{1,3},{3,1},{4,6},{6,4},{5,7},{7,5},{8,10},{10,8},{9,1... | collective-permute-start | bytes 3932168 | tf_op jit(solution)/shard_map/ppermute | solution.py:18
  510.4 29.8 %collective-permute-start.53 = (bf16[512,1280]{1,0:T(8,128)(2,1)S(1)}, bf16[512,1280]{1,0:T(8,128)(2,1)S(1)}, u32[]{:S(2)}, u32[]{:S(2)}) collective-permute-start(bf16[512,1280]{1,0:T(8,128)(2,1)S(1)} %convolution_convert_fusion.5), channel_id=1, source_target_pairs={{0,2},{2,0},{1,3},{3,1},{4,6},{6,4},{5,7},{7,5},{8,10},{10,8},{9,1... | collective-permute-start | bytes 3932168 | tf_op jit(solution)/shard_map/ppermute | solution.py:18
  513.8 30.2 %collective-permute-start.54 = (bf16[512,1280]{1,0:T(8,128)(2,1)S(1)}, bf16[512,1280]{1,0:T(8,128)(2,1)S(1)}, u32[]{:S(2)}, u32[]{:S(2)}) collective-permute-start(bf16[512,1280]{1,0:T(8,128)(2,1)S(1)} %fusion.15), channel_id=1, source_target_pairs={{0,4},{4,0},{1,5},{5,1},{2,6},{6,2},{3,7},{7,3},{8,12},{12,8},{9,1... | collective-permute-start | bytes 3932168 | tf_op jit(solution)/shard_map/ppermute | solution.py:18
  547.3 30.7 %collective-permute-start.64 = (bf16[128,1280]{1,0:T(8,128)(2,1)S(1)}, bf16[128,1280]{1,0:T(8,128)(2,1)S(1)}, u32[]{:S(2)}, u32[]{:S(2)}) collective-permute-start(bf16[128,1280]{1,0:T(8,128)(2,1)S(1)} %get-tuple-element.194), channel_id=1, source_target_pairs={{0,24},{8,16},{16,8},{24,0},{1,25},{9,17},{17,9},{25,1},{2,26},{10... | collective-permute-start | bytes 983048 | tf_op jit(solution)/shard_map/ppermute | solution.py:41
  547.3 40.2 %collective-permute-start.63 = (bf16[128,1280]{1,0:T(8,128)(2,1)S(1)}, bf16[128,1280]{1,0:T(8,128)(2,1)S(1)}, u32[]{:S(2)}, u32[]{:S(2)}) collective-permute-start(bf16[128,1280]{1,0:T(8,128)(2,1)S(1)} %get-tuple-element.195), channel_id=1, source_target_pairs={{0,16},{8,24},{16,0},{24,8},{1,17},{9,25},{17,1},{25,9},{2,18},{10... | collective-permute-start | bytes 983048 | tf_op jit(solution)/shard_map/ppermute | solution.py:41
  554.1 45.7 %collective-permute-start.60 = (f32[128,2048]{1,0:T(8,128)}, f32[128,2048]{1,0:T(8,128)}, u32[]{:S(2)}, u32[]{:S(2)}) collective-permute-start(f32[128,2048]{1,0:T(8,128)} %slice.397), channel_id=1, source_target_pairs={{0,1},{1,0},{2,3},{3,2},{4,5},{5,4},{6,7},{7,6},{8,9},{9,8},{10,11... | collective-permute-start | bytes 3145736 | tf_op jit(solution)/shard_map/ppermute | solution.py:18
  555.7 53.3 %collective-permute-start.56 = (bf16[512,1280]{1,0:T(8,128)(2,1)}, bf16[512,1280]{1,0:T(8,128)(2,1)}, u32[]{:S(2)}, u32[]{:S(2)}) collective-permute-start(bf16[512,1280]{1,0:T(8,128)(2,1)} %convolution_convert_fusion.3), channel_id=1, source_target_pairs={{0,4},{4,0},{1,5},{5,1},{2,6},{6,2},{3,7},{7,3},{8,12},{12,8},{9,1... | collective-permute-start | bytes 3932168 | tf_op jit(solution)/shard_map/ppermute | solution.py:18
  589.9 41.3 %collective-permute-start.55 = (bf16[512,1280]{1,0:T(8,128)(2,1)}, bf16[512,1280]{1,0:T(8,128)(2,1)}, u32[]{:S(2)}, u32[]{:S(2)}) collective-permute-start(bf16[512,1280]{1,0:T(8,128)(2,1)} %convolution_convert_fusion.4), channel_id=1, source_target_pairs={{0,4},{4,0},{1,5},{5,1},{2,6},{6,2},{3,7},{7,3},{8,12},{12,8},{9,1... | collective-permute-start | bytes 3932168 | tf_op jit(solution)/shard_map/ppermute | solution.py:18
  597.8 61.8 %collective-permute-start.59 = (bf16[256,768]{0,1:T(8,128)(2,1)}, bf16[256,768]{0,1:T(8,128)(2,1)}, u32[]{:S(2)}, u32[]{:S(2)}) collective-permute-start(bf16[256,768]{0,1:T(8,128)(2,1)} %bitcast.121), channel_id=1, source_target_pairs={{0,4},{4,0},{1,5},{5,1},{2,6},{6,2},{3,7},{7,3},{8,12},{12,8},{9,1... | collective-permute-start | bytes 1179656 | tf_op jit(solution)/shard_map/ppermute | solution.py:18
  611.9 40.6 %collective-permute-start.57 = (bf16[512,1280]{1,0:T(8,128)(2,1)}, bf16[512,1280]{1,0:T(8,128)(2,1)}, u32[]{:S(2)}, u32[]{:S(2)}) collective-permute-start(bf16[512,1280]{1,0:T(8,128)(2,1)} %fusion.16), channel_id=1, source_target_pairs={{0,2},{2,0},{1,3},{3,1},{4,6},{6,4},{5,7},{7,5},{8,10},{10,8},{9,1... | collective-permute-start | bytes 3932168 | tf_op jit(solution)/shard_map/ppermute | solution.py:18
  618.8 46.8 %collective-permute-start.58 = (bf16[256,1536]{1,0:T(8,128)(2,1)}, bf16[256,1536]{1,0:T(8,128)(2,1)}, u32[]{:S(2)}, u32[]{:S(2)}) collective-permute-start(bf16[256,1536]{1,0:T(8,128)(2,1)} %fusion.45), channel_id=1, source_target_pairs={{0,4},{4,0},{1,5},{5,1},{2,6},{6,2},{3,7},{7,3},{8,12},{12,8},{9,1... | collective-permute-start | bytes 2359304 | tf_op jit(solution)/shard_map/ppermute | solution.py:18
  666.4 78.7 %collective-permute-start.61 = (bf16[64,2048]{1,0:T(8,128)(2,1)}, bf16[64,2048]{1,0:T(8,128)(2,1)}, u32[]{:S(2)}, u32[]{:S(2)}) collective-permute-start(bf16[64,2048]{1,0:T(8,128)(2,1)} %get-tuple-element.216), channel_id=1, source_target_pairs={{0,4},{4,0},{1,5},{5,1},{2,6},{6,2},{3,7},{7,3},{8,12},{12,8},{9,1... | collective-permute-start | bytes 786440 | tf_op jit(solution)/shard_map/ppermute | solution.py:18
  670.6 28.9 %collective-permute-start.66 = (bf16[128,1280]{1,0:T(8,128)(2,1)}, bf16[128,1280]{1,0:T(8,128)(2,1)S(1)}, u32[]{:S(2)}, u32[]{:S(2)}) collective-permute-start(bf16[128,1280]{1,0:T(8,128)(2,1)} %get-tuple-element.190), channel_id=1, source_target_pairs={{0,8},{8,0},{16,24},{24,16},{1,9},{9,1},{17,25},{25,17},{2,10},{10... | collective-permute-start | bytes 983048 | tf_op jit(solution)/shard_map/ppermute | solution.py:41
  696.1 27.9 %collective-permute-start.68 = (bf16[128,1280]{1,0:T(8,128)(2,1)S(1)}, bf16[128,1280]{1,0:T(8,128)(2,1)S(1)}, u32[]{:S(2)}, u32[]{:S(2)}) collective-permute-start(bf16[128,1280]{1,0:T(8,128)(2,1)S(1)} %copy-done.36), channel_id=1, source_target_pairs={{0,24},{8,16},{16,8},{24,0},{1,25},{9,17},{17,9},{25,1},{2,26},{10... | collective-permute-start | bytes 983048 | tf_op jit(solution)/shard_map/ppermute | solution.py:41
  696.2 39.0 %collective-permute-start.67 = (bf16[128,1280]{1,0:T(8,128)(2,1)S(1)}, bf16[128,1280]{1,0:T(8,128)(2,1)S(1)}, u32[]{:S(2)}, u32[]{:S(2)}) collective-permute-start(bf16[128,1280]{1,0:T(8,128)(2,1)S(1)} %copy-done.35), channel_id=1, source_target_pairs={{0,16},{8,24},{16,0},{24,8},{1,17},{9,25},{17,1},{25,9},{2,18},{10... | collective-permute-start | bytes 983048 | tf_op jit(solution)/shard_map/ppermute | solution.py:41
  741.9 18.7 %collective-permute-start.70 = (bf16[80,2688]{1,0:T(8,128)(2,1)}, bf16[80,2688]{1,0:T(8,128)(2,1)S(1)}, u32[]{:S(2)}, u32[]{:S(2)}) collective-permute-start(bf16[80,2688]{1,0:T(8,128)(2,1)} %reduce-scatter.8.cloned.1.call-done), channel_id=1, source_target_pairs={{0,0},{1,16},{2,1},{3,17},{4,2},{5,18},{6,3},{7,19},{8,4},{9,20},{... | collective-permute-start | bytes 1290248 | tf_op jit(solution)/shard_map/ppermute | solution.py:563
  (100 other events, 1369.8 us)
Sparse Core Ops, SparseCore 0:
  14.7 154.2 all-gather.3
  171.2 115.9 all-gather.5
  288.7 62.4 all-gather.7
  369.6 60.6 reduce-scatter.5
  432.4 114.7 reduce-scatter.3
  552.4 189.5 reduce-scatter.7
